TPU v7x, 32 devices: a whole 2x2x4 slice. The times are simulated.
32 devices in a mesh: wide: 16 (over z, y, core), narrow: 2 (over x).
Axes of the slice: x: 2, y: 2, z: 4, core: 2. Of those that a mesh axis runs over, the one named last changes fastest.
Arguments:
- hidden_in: bfloat16 [64, 512, 768], P(('wide', 'narrow')), may hold values from -6 to 6
- segment_ids: int32 [64, 512], P(('wide', 'narrow')), may hold values from 0 to 7, never falling along the last dimension, each value on 1 to 256 neighbouring positions
- cotangent: bfloat16 [64, 512, 768], P(('wide', 'narrow')), may hold values from -6 to 6
- attention_weights: float32 [4, 768, 768], P(None, 'wide'), may hold values from -1 to 1
- attention_momentum: float32 [4, 768, 768], P(None, 'wide'), may hold values from -32768 to 32768
- attention_average: float32 [4, 768, 768], P(None, 'wide'), may hold values from -0.21875 to 0.21875
- dense_weights: float32 [2, 768, 3072], P(None, 'wide'), may hold values from -0.21875 to 0.21875
- dense_momentum: float32 [2, 768, 3072], P(None, 'wide'), may hold values from -32768 to 32768
- dense_average: float32 [2, 768, 3072], P(None, 'wide'), may hold values from -0.21875 to 0.21875
- vector_params: float32 [12, 768], P(None, 'wide'), may hold values from -2 to 2
- vector_momentum: float32 [12, 768], P(None, 'wide'), may hold values from -32768 to 32768
- vector_average: float32 [12, 768], P(None, 'wide'), may hold values from -2 to 2
Outputs:
- block_output: bfloat16 [64, 512, 768], P(('wide', 'narrow'))
- grad_input: bfloat16 [64, 512, 768], P(('wide', 'narrow'))
- attention_momentum_new: float32 [4, 768, 768], P(None, 'wide')
- attention_weights_new: float32 [4, 768, 768], P(None, 'wide')
- attention_average_new: float32 [4, 768, 768], P(None, 'wide')
- dense_momentum_new: float32 [2, 768, 3072], P(None, 'wide')
- dense_weights_new: float32 [2, 768, 3072], P(None, 'wide')
- dense_average_new: float32 [2, 768, 3072], P(None, 'wide')
- vector_momentum_new: float32 [12, 768], P(None, 'wide')
- vector_params_new: float32 [12, 768], P(None, 'wide')
- vector_average_new: float32 [12, 768], P(None, 'wide')
Inputs may be any that keep to these rules, and one draw needn't show every extreme that they name: `segment_ids`: ids never fall along a row; tokens with equal ids in a row form one document or the padding.
All inputs are finite; a program needn't handle non-finite values.
Results may differ from a plain program's by a relative error of at most 0.015.
The roundings to bfloat16 on the way count: a program that leaves them out, or rounds other values in their place, can miss the bound.
Values may be sent and summed in bfloat16 or wider, within the bound.
A program may use at most 192 MiB of HBM per device.

v0:
```python
from functools import partial
import math

import jax
import jax.numpy as jnp
from jax import lax
from jax.sharding import PartitionSpec as P

HEAD_DIM = 64


epsilon = 1e-12
momentum_decay = 0.5
average_decay = 0.5
matrix_rate = 0.03
vector_rate = 0.3
score_scale = 0.125
masked_score = -1e30


def product(form, left_side, right_side):
    return jnp.einsum(form, left_side, right_side, preferred_element_type=jnp.float32)


def normalize(hidden):
    center = hidden - jnp.mean(hidden, -1, keepdims=True)
    inverse = lax.rsqrt(jnp.mean(center * center, -1, keepdims=True) + epsilon)
    return (center * inverse, inverse)


def norm_back(grad_normed, normed, inverse):
    first_mean = jnp.mean(grad_normed, -1, keepdims=True)
    second_mean = jnp.mean(grad_normed * normed, -1, keepdims=True)
    return inverse * (grad_normed - first_mean - normed * second_mean)


def row_scores(queries, key_rows, segment):
    scores = product("qhd,khd->hqk", queries, key_rows) * score_scale
    same_doc = segment[:, None] == segment[None, :]
    return jnp.where(same_doc[None], scores, masked_score)


def attend_forward(operands):
    queries, key_rows, value_rows, segment = operands
    scores = row_scores(queries, key_rows, segment)
    highest = jnp.max(scores, -1, keepdims=True)
    log_total = highest + jnp.log(jnp.sum(jnp.exp(scores - highest), -1, keepdims=True))
    soft_weights = jnp.exp(scores - log_total).astype(jnp.bfloat16)
    context = product("hqk,khd->qhd", soft_weights, value_rows)
    return (context.astype(jnp.bfloat16), log_total)


def attend_backward(operands):
    queries, key_rows, value_rows, segment, log_total, grad_context = operands
    scores = row_scores(queries, key_rows, segment)
    soft_weights = jnp.exp(scores - log_total)
    grad_values = product("hqk,qhd->khd", soft_weights.astype(jnp.bfloat16), grad_context)
    grad_weights = product("qhd,khd->hqk", grad_context, value_rows)
    inner_sum = jnp.sum(soft_weights * grad_weights, -1, keepdims=True)
    grad_scores = (soft_weights * (grad_weights - inner_sum)).astype(jnp.bfloat16)
    grad_queries = product("hqk,khd->qhd", grad_scores, key_rows) * score_scale
    grad_keys = product("hqk,qhd->khd", grad_scores, queries) * score_scale
    return (
        grad_queries.astype(jnp.bfloat16),
        grad_keys.astype(jnp.bfloat16),
        grad_values.astype(jnp.bfloat16),
    )


def split_heads(tensor, row_count, length):
    return tensor.reshape(row_count, length, -1, HEAD_DIM)


def advance(gradient, moment, weight, average, step_rate):
    moment_new = momentum_decay * moment + gradient
    weight_new = weight - step_rate * (gradient + momentum_decay * moment_new)
    average_new = average_decay * average + (1.0 - average_decay) * weight_new
    return (moment_new, weight_new, average_new)


def body(
    hidden_in,
    segment_ids,
    cotangent,
    attention_weights,
    attention_momentum,
    attention_average,
    dense_weights,
    dense_momentum,
    dense_average,
    vector_params,
    vector_momentum,
    vector_average,
):
    row_count, length, width = hidden_in.shape
    packed = (
        attention_weights.astype(jnp.bfloat16),
        dense_weights.astype(jnp.bfloat16),
        vector_params.astype(jnp.bfloat16),
    )
    attention_full, dense_full, vector_full = (
        lax.all_gather(packed[0], "wide", axis=1, tiled=True),
        lax.all_gather(packed[1], "wide", axis=1, tiled=True),
        lax.all_gather(packed[2], "wide", axis=1, tiled=True),
    )
    vector_vals = vector_full.astype(jnp.float32)
    flat_in = hidden_in.reshape(-1, width)
    queries = (product("ni,io->no", flat_in, attention_full[0]) + vector_vals[4]).astype(
        jnp.bfloat16
    )
    key_rows = product("ni,io->no", flat_in, attention_full[1]).astype(jnp.bfloat16)
    value_rows = (product("ni,io->no", flat_in, attention_full[2]) + vector_vals[5]).astype(
        jnp.bfloat16
    )
    heads_query = split_heads(queries, row_count, length)
    heads_key = split_heads(key_rows, row_count, length)
    heads_value = split_heads(value_rows, row_count, length)
    context, log_total = lax.map(attend_forward, (heads_query, heads_key, heads_value, segment_ids))
    context = context.reshape(-1, width)
    branch = product("ni,io->no", context, attention_full[3]) + vector_vals[6]
    normed_one, inverse_one = normalize(flat_in.astype(jnp.float32) + branch)
    middle = normed_one * vector_vals[0] + vector_vals[1]
    middle_low = middle.astype(jnp.bfloat16)
    inner_pre = product("ni,if->nf", middle_low, dense_full[0]) + vector_vals[8:].reshape(-1)
    active = jax.nn.gelu(inner_pre, approximate=False).astype(jnp.bfloat16)
    second = product("nf,if->ni", active, dense_full[1]) + vector_vals[7]
    normed_two, inverse_two = normalize(middle + second)
    block_output = (
        (normed_two * vector_vals[2] + vector_vals[3]).astype(jnp.bfloat16).reshape(hidden_in.shape)
    )
    attention_back, dense_back, vector_again = (
        lax.all_gather(packed[0], "wide", axis=1, tiled=True),
        lax.all_gather(packed[1], "wide", axis=1, tiled=True),
        lax.all_gather(packed[2], "wide", axis=1, tiled=True),
    )
    vector_back = vector_again.astype(jnp.float32)
    grad_top = cotangent.reshape(-1, width).astype(jnp.float32)
    grad_gain_two = jnp.sum(grad_top * normed_two, 0)
    grad_shift_two = jnp.sum(grad_top, 0)
    grad_sum_two = norm_back(grad_top * vector_back[2], normed_two, inverse_two)
    grad_second = grad_sum_two.astype(jnp.bfloat16)
    grad_down_bias = jnp.sum(grad_second, 0, dtype=jnp.float32)
    grad_down = product("ni,nf->if", grad_second, active)
    grad_active = product("ni,if->nf", grad_second, dense_back[1])
    gelu_pull = jax.vjp(partial(jax.nn.gelu, approximate=False), inner_pre)[1]
    grad_inner = gelu_pull(grad_active)[0].astype(jnp.bfloat16)
    grad_up_bias = jnp.sum(grad_inner, 0, dtype=jnp.float32)
    grad_up = product("ni,nf->if", middle_low, grad_inner)
    grad_middle = grad_sum_two + product("nf,if->ni", grad_inner, dense_back[0])
    grad_gain_one = jnp.sum(grad_middle * normed_one, 0)
    grad_shift_one = jnp.sum(grad_middle, 0)
    grad_sum_one = norm_back(grad_middle * vector_back[0], normed_one, inverse_one)
    grad_branch = grad_sum_one.astype(jnp.bfloat16)
    grad_out_bias = jnp.sum(grad_branch, 0, dtype=jnp.float32)
    grad_out_proj = product("ni,no->io", context, grad_branch)
    grad_context = product("no,io->ni", grad_branch, attention_back[3]).astype(jnp.bfloat16)
    grad_queries, grad_keys, grad_values = lax.map(
        attend_backward,
        (
            heads_query,
            heads_key,
            heads_value,
            segment_ids,
            log_total,
            split_heads(grad_context, row_count, length),
        ),
    )
    grad_queries = grad_queries.reshape(-1, width)
    grad_keys = grad_keys.reshape(-1, width)
    grad_values = grad_values.reshape(-1, width)
    grad_tokens = grad_sum_one + product("no,io->ni", grad_queries, attention_back[0])
    grad_tokens = grad_tokens + product("no,io->ni", grad_keys, attention_back[1])
    grad_tokens = grad_tokens + product("no,io->ni", grad_values, attention_back[2])
    grad_input = grad_tokens.astype(jnp.bfloat16).reshape(hidden_in.shape)
    attention_grad = jnp.stack(
        [
            product("ni,no->io", flat_in, grad_queries),
            product("ni,no->io", flat_in, grad_keys),
            product("ni,no->io", flat_in, grad_values),
            grad_out_proj,
        ]
    )
    dense_grad = jnp.stack([grad_up, grad_down])
    vector_rows = jnp.stack(
        [
            grad_gain_one,
            grad_shift_one,
            grad_gain_two,
            grad_shift_two,
            jnp.sum(grad_queries, 0, dtype=jnp.float32),
            jnp.sum(grad_values, 0, dtype=jnp.float32),
            grad_out_bias,
            grad_down_bias,
        ]
    )
    vector_grad = jnp.concatenate([vector_rows, grad_up_bias.reshape(-1, width)], 0)
    shares = (
        lax.psum_scatter(attention_grad, "wide", scatter_dimension=1, tiled=True),
        lax.psum_scatter(dense_grad, "wide", scatter_dimension=1, tiled=True),
        lax.psum_scatter(vector_grad, "wide", scatter_dimension=1, tiled=True),
    )
    totals = (
        lax.psum(shares[0].astype(jnp.bfloat16), "narrow").astype(jnp.float32),
        lax.psum(shares[1].astype(jnp.bfloat16), "narrow").astype(jnp.float32),
        lax.psum(shares[2].astype(jnp.bfloat16), "narrow").astype(jnp.float32),
    )
    replicas = lax.axis_size("narrow")
    tokens_all = row_count * length * lax.axis_size("wide") * replicas
    grad_scale = math.sqrt(tokens_all) / replicas
    attention_new = advance(
        totals[0] / replicas,
        attention_momentum,
        attention_weights,
        attention_average,
        matrix_rate / grad_scale,
    )
    dense_new = advance(
        totals[1] / replicas, dense_momentum, dense_weights, dense_average, matrix_rate / grad_scale
    )
    vector_new = advance(
        totals[2] / replicas,
        vector_momentum,
        vector_params,
        vector_average,
        vector_rate / grad_scale,
    )
    return (
        block_output,
        grad_input,
        attention_new[0],
        attention_new[1],
        attention_new[2],
        dense_new[0],
        dense_new[1],
        dense_new[2],
        vector_new[0],
        vector_new[1],
        vector_new[2],
    )


def solution(mesh):
    in_specs = (
        P(("wide", "narrow"), None, None),
        P(("wide", "narrow"), None),
        P(("wide", "narrow"), None, None),
        P(None, "wide", None),
        P(None, "wide", None),
        P(None, "wide", None),
        P(None, "wide", None),
        P(None, "wide", None),
        P(None, "wide", None),
        P(None, "wide"),
        P(None, "wide"),
        P(None, "wide"),
    )
    out_specs = (
        P(("wide", "narrow"), None, None),
        P(("wide", "narrow"), None, None),
        P(None, "wide", None),
        P(None, "wide", None),
        P(None, "wide", None),
        P(None, "wide", None),
        P(None, "wide", None),
        P(None, "wide", None),
        P(None, "wide"),
        P(None, "wide"),
        P(None, "wide"),
    )
    return jax.shard_map(body, mesh=mesh, in_specs=in_specs, out_specs=out_specs, check_vma=False)
```

profile of v0, /device:TPU:0, one launch (start us, length us, event | category | flops | bytes accessed | tf_op | source)
XLA Modules:
  0.0 695.3 jit_solution(13471967307445901062)
XLA Ops:
  11.5 23.5 %all-gather = bf16[16,48,12]{1,2,0:T(8,128)(2,1)S(1)} all-gather(bf16[1,48,12]{1,2,0:T(8,128)(2,1)S(1)} %convert_bitcast_fusion), channel_id=1, replica_groups=mesh['wide'=16,'narrow'=2] {'wide'}, dimensions={0}, use_global_device_ids=true | all-gather | bytes 19584 | tf_op jit(solution)/shard_map/all_gather | solution.py:104
  37.7 29.4 %all-gather.4.cloned.1.call-done = bf16[4,768,768]{2,1,0:T(8,128)(2,1)} async-done(((bf16[4,48,768]{2,1,0:T(8,128)(2,1)}), bf16[4,768,768]{2,1,0:T(8,128)(2,1)}) %all-gather.4.cloned.1.call-update) | async-done | bytes 4718608 | tf_op jit(solution)/shard_map/all_gather | solution.py:102
  80.2 3.8 convolution_convert_fusion.1
  91.1 20.2 %while.26 = (s32[]{:T(128)}, bf16[2,512,12,64]{1,3,2,0:T(8,128)(2,1)}, f32[2,12,512,1]{2,1,3,0:T(8,128)S(1)}, bf16[2,512,12,64]{1,3,2,0:T(8,128)(2,1)}, s32[2,51...) while((s32[]{:T(128)}, ...), condition=%wide.region_3.4_spmd, body=%wide.region_0.3_spmd.sunk | while | flops 840558592 | bytes 42180700 | solution.py:118
  96.0 5.1 fusion.130
  106.0 5.1 fusion.130
  111.3 4.2 copy.107
  120.0 30.0 %all-gather.6.cloned.1.call-done = bf16[2,768,3072]{2,1,0:T(8,128)(2,1)} async-done(((bf16[2,48,3072]{2,1,0:T(8,128)(2,1)}), bf16[2,768,3072]{2,1,0:T(8,128)(2,1)}) %all-gather.6.cloned.1.call-update) | async-done | bytes 9437200 | tf_op jit(solution)/shard_map/all_gather | solution.py:103
  150.0 36.5 %multiply_convert_fusion.3 = (bf16[1024,3072]{1,0:T(8,128)(2,1)S(1)}, f32[1024,3072]{1,0:T(8,128)}, f32[1024,3072]{1,0:T(8,128)}) fusion(f32[3072]{0:T(1024)S(1)} %add.184, bf16[2,768,3072]{2,1,0:T(8,128)(2,1)} %all-gather.6.cloned.1.call-done, f32[1024,768]{1,0:T(8,128)S(1)} %get-tuple-element.284, f32[768]{0:T(1024)S(1)} %get-tuple-element.220, ...), kind=kOutput, calls=%fused_computation.70 | convolution fusion | flops 5043388416 | bytes 39348224 | tf_op jit(solution)/shard_map/ni,if->nf/dot_general | solution.py:22
  186.5 5.4 fusion.92
  198.0 7.7 %convolution_bitcast_fusion = f32[1,768,3072]{2,1,0:T(8,128)} fusion(bf16[1024,3072]{1,0:T(8,128)(2,1)S(1)} %get-tuple-element.276, f32[1024,768]{1,0:T(8,128)S(1)} %get-tuple-element.267), kind=kOutput, calls=%fused_computation.85 | convolution fusion | flops 4832624640 | bytes 18874368 | tf_op jit(solution)/shard_map/ni,nf->if/dot_general | solution.py:22
  205.7 17.3 %convert_reduce_fusion = (f32[3072]{0:T(1024)}, bf16[1024,3072]{1,0:T(8,128)(2,1)}) fusion(f32[1024,3072]{1,0:T(8,128)} %get-tuple-element.277, bf16[2,768,3072]{2,1,0:T(8,128)(2,1)} %all-gather.6.cloned.1.call-done, f32[1024,768]{1,0:T(8,128)S(1)} %get-tuple-element.267, f32[1024,3072]{1,0:T(8,128)} %get-tuple-element.285, f32[3072]{0:T(1024)S(1)} %add.184), kind=kOutput, calls=%fused_computation.68 | convolution fusion | flops 4886098944 | bytes 39346176 | tf_op jit(solution)/shard_map/ni,if->nf/dot_general | solution.py:22
  223.1 8.2 %convolution_bitcast_fusion.1 = f32[1,768,3072]{2,1,0:T(8,128)S(1)} fusion(bf16[1024,3072]{1,0:T(8,128)(2,1)} %get-tuple-element.290, f32[1024,768]{1,0:T(8,128)S(1)} %get-tuple-element.284, f32[768]{0:T(1024)S(1)} %get-tuple-element.220, f32[768]{0:T(1024)S(1)} %get-tuple-element.221, f32[1024]{0:T(1024)S(1)} %add_rsqrt_fusion.1, ...), kind=kOutput, calls=%fused_computation.86 | convolution fusion | flops 4835770368 | bytes 18888704 | tf_op jit(solution)/shard_map/ni,nf->if/dot_general | solution.py:22
  231.3 6.7 pad_maximum_fusion
  240.5 12.0 %multiply_reduce_fusion.1 = (f32[768]{0:T(1024)}, f32[1024]{0:T(1024)S(1)}, f32[1024]{0:T(1024)S(1)}, f32[768]{0:T(1024)}, f32[1024,768]{1,0:T(8,128)S(1)}) fusion(f32[1024,768]{1,0:T(8,128)S(1)} %get-tuple-element.284, f32[1024]{0:T(1024)S(1)} %add_rsqrt_fusion.1, f32[1024]{0:T(1024)S(1)} %broadcast_multiply_fusion.4, f32[768]{0:T(1024)S(1)} %get-tuple-element.221, ...), kind=kOutput, calls=%fused_computation.107 | convolution fusion | flops 4839698432 | bytes 20472832 | tf_op jit(solution)/shard_map/nf,if->ni/dot_general | solution.py:22
  266.5 49.4 %while.27 = (s32[]{:T(128)}, bf16[2,512,12,64]{1,3,2,0:T(8,128)(2,1)}, bf16[2,512,12,64]{1,3,2,0:T(8,128)(2,1)}, bf16[2,512,12,64]{1,3,2,0:T(8,128)(2,1)}, bf16[...) while((s32[]{:T(128)}, ...), condition=%wide.region_14.15_spmd, body=%wide.region_12.14_spmd.sunk | while | flops 2062673920 | bytes 147524944 | solution.py:157
  268.8 6.9 multiply_reduce_fusion.7
  275.7 7.1 %multiply_convert_fusion.5 = bf16[12,512,512]{1,2,0:T(8,128)(2,1)S(1)} fusion(f32[12,512,512]{1,2,0:T(8,128)} %get-tuple-element.407, f32[12,512,512]{1,2,0:T(8,128)S(1)} %fusion.139, f32[12,512]{1,0:T(8,128)S(1)} %get-tuple-element.408, f32[12,512]{1,0:T(8,128)S(1)} %dynamic-slice_bitcast_fusion.2, pred[512,512]{0,1:T(8,128)(4,1)S(1)} %broadcast_compare_fusion.5), kind=kLoop, calls=%fused_computation.24.clone.1 | loop fusion | flops 18874368 | bytes 31768576 | tf_op jit(solution)/shard_map/while/body/eval_jaxpr/convert_element_type | solution.py:60
  287.2 3.9 fusion.142
  293.2 6.9 multiply_reduce_fusion.7
  300.1 7.2 %multiply_convert_fusion.5 = bf16[12,512,512]{1,2,0:T(8,128)(2,1)S(1)} fusion(f32[12,512,512]{1,2,0:T(8,128)} %get-tuple-element.407, f32[12,512,512]{1,2,0:T(8,128)S(1)} %fusion.139, f32[12,512]{1,0:T(8,128)S(1)} %get-tuple-element.408, f32[12,512]{1,0:T(8,128)S(1)} %dynamic-slice_bitcast_fusion.2, pred[512,512]{0,1:T(8,128)(4,1)S(1)} %broadcast_compare_fusion.5), kind=kLoop, calls=%fused_computation.24.clone.1 | loop fusion | flops 18874368 | bytes 31768576 | tf_op jit(solution)/shard_map/while/body/eval_jaxpr/convert_element_type | solution.py:60
  311.7 3.9 fusion.142
  335.6 4.3 pad_maximum_fusion.1
  339.9 12.1 %copy.117 = f32[4,768,768]{2,0,1:T(4,128)} copy(f32[4,768,768]{1,2,0:T(8,128)} %pad_maximum_fusion.1) | data formatting | bytes 18874368 | tf_op jit(solution)/shard_map/stack | solution.py:175
  352.0 224.7 %all-reduce.6 = bf16[4,768,768]{2,0,1:T(4,128)(2,1)} all-reduce(f32[4,768,768]{2,0,1:T(4,128)} %copy.117), channel_id=2, replica_groups=mesh['wide'=16,'narrow'=2] {'wide'}, use_global_device_ids=true, to_apply=%region_15.16.clone | all-reduce | flops 2359296 | bytes 14155776
  576.7 5.0 fusion.76
  581.7 4.4 fusion.77
  590.2 6.3 add_convert_fusion.1
  596.5 47.3 %reduce-scatter.7.cloned.1.call-done = f32[48,12]{1,0:T(8,128)} async-done(((f32[768,12]{1,0:T(8,128)}), f32[48,12]{1,0:T(8,128)}) %reduce-scatter.7.cloned.1.call-update) | async-done | bytes 2320
  644.6 4.9 psum.23
  650.2 32.2 %all-reduce.5.cloned.1.call-done = (bf16[4,48,768]{2,1,0:T(8,128)(2,1)}, bf16[2,48,3072]{2,1,0:T(8,128)(2,1)}) async-done(((bf16[4,48,768]{2,1,0:T(8,128)(2,1)}, bf16[2,48,3072]{2,1,0:T(8,128)(2,1)}), (bf16[4,48,768]{2,1,0:T(8,128)(2,1)}, bf16[2,48,3072]{2,1,0:T(8,128)(2,1)})) %all-reduce.5.cloned.1.call-update) | async-done | bytes 884752 | tf_op jit(solution)/shard_map/psum | solution.py:203
  682.4 4.5 add_multiply_fusion
  (235 shorter events, 101.9 us)
Async XLA Ops:
  7.2 4.3 copy-start.36
  7.2 28.6 %copy-start.7 = (bf16[2,512,768]{2,1,0:T(8,128)(2,1)S(1)}, bf16[2,512,768]{2,1,0:T(8,128)(2,1)}, u32[]{:S(2)}) copy-start(bf16[2,512,768]{2,1,0:T(8,128)(2,1)} %param.18) | copy-start | bytes 4718596
  7.2 59.9 %all-gather.4.cloned.1.call-start = ((), (), s32[]{:S(2)}) async-start(), calls=%async_computation.2 | async-start | bytes 5013504 | tf_op jit(solution)/shard_map/all_gather | solution.py:102
  9.2 140.8 %all-gather.6.cloned.1.call-start = ((), (), s32[]{:S(2)}) async-start(), calls=%async_computation.3 | async-start | bytes 10027008 | tf_op jit(solution)/shard_map/all_gather | solution.py:103
  11.4 576.5 %reduce-scatter.5.cloned.1.call-start = ((), (), s32[]{:S(2)}) async-start(), calls=%async_computation.4 | async-start | bytes 20054016 | tf_op jit(solution)/shard_map/reduce_scatter | solution.py:199
  35.8 31.3 %copy-start.34 = (f32[768]{0:T(1024)}, f32[768]{0:T(1024)S(1)}, u32[]{:S(2)}) copy-start(f32[768]{0:T(1024)S(1)} %get-tuple-element.217) | copy-start | bytes 9220
  111.3 4.7 copy-start
  111.3 4.7 copy-start.2
  111.3 4.7 copy-start.29
  111.3 4.7 copy-start.54
  150.0 36.5 %copy-start.48 = (f32[768]{0:T(1024)S(1)}, f32[768]{0:T(1024)}, u32[]{:S(2)}) copy-start(f32[768]{0:T(1024)} %get-tuple-element.219) | copy-start | bytes 9220
  150.0 36.5 %copy-start.51 = (bf16[2,768,3072]{2,1,0:T(8,128)(2,1)S(1)}, bf16[2,768,3072]{2,1,0:T(8,128)(2,1)}, u32[]{:S(2)}) copy-start(bf16[2,768,3072]{2,1,0:T(8,128)(2,1)} %all-gather.6.cloned.1.call-done) | copy-start | bytes 28311556
  198.0 7.7 %copy-start.20 = (f32[1024,768]{1,0:T(8,128)}, f32[1024,768]{1,0:T(8,128)S(1)}, u32[]{:S(2)}) copy-start(f32[1024,768]{1,0:T(8,128)S(1)} %get-tuple-element.267) | copy-start | bytes 9437188
  223.1 8.2 %copy-start.15 = (f32[1,768,3072]{2,1,0:T(8,128)S(1)}, f32[1,768,3072]{2,1,0:T(8,128)}, u32[]{:S(2)}) copy-start(f32[1,768,3072]{2,1,0:T(8,128)} %convolution_bitcast_fusion) | copy-start | bytes 28311556
  238.1 405.7 %reduce-scatter.7.cloned.1.call-start = ((), (), s32[]{:S(2)}) async-start(), calls=%async_computation.5 | async-start | bytes 417792
  262.5 3.9 copy-start.1
  262.5 3.9 copy-start.3
  262.5 3.9 copy-start.30
  262.5 3.9 copy-start.33
  275.7 7.1 %copy-start.16 = (bf16[2,512,12,64]{1,3,2,0:T(8,128)(2,1)S(1)}, bf16[2,512,12,64]{1,3,2,0:T(8,128)(2,1)}, u32[]{:S(2)}) copy-start(bf16[2,512,12,64]{1,3,2,0:T(8,128)(2,1)} %get-tuple-element.446) | copy-start | bytes 4718596 | tf_op jit(solution)/shard_map/while
  300.1 7.3 %copy-start.16 = (bf16[2,512,12,64]{1,3,2,0:T(8,128)(2,1)S(1)}, bf16[2,512,12,64]{1,3,2,0:T(8,128)(2,1)}, u32[]{:S(2)}) copy-start(bf16[2,512,12,64]{1,3,2,0:T(8,128)(2,1)} %get-tuple-element.446) | copy-start | bytes 4718596 | tf_op jit(solution)/shard_map/while
  315.9 3.6 copy-start.12
  319.1 3.6 copy-start.44
  576.7 105.7 %all-reduce.5.cloned.1.call-start = ((), (), s32[]{:S(2)}) async-start(), calls=%async_computation.6 | async-start | bytes 1769472 | tf_op jit(solution)/shard_map/psum | solution.py:203
  576.7 5.0 copy-start.25
  590.1 59.4 %copy-start.37 = (f32[12,48]{1,0:T(8,128)S(1)}, f32[12,48]{1,0:T(8,128)}, u32[]{:S(2)}) copy-start(f32[12,48]{1,0:T(8,128)} %param.25) | copy-start | bytes 6916
  590.1 59.4 %copy-start.46 = (f32[12,48]{1,0:T(8,128)S(1)}, f32[12,48]{1,0:T(8,128)}, u32[]{:S(2)}) copy-start(f32[12,48]{1,0:T(8,128)} %param.27) | copy-start | bytes 6916
  590.1 59.4 %copy-start.47 = (f32[12,48]{1,0:T(8,128)S(1)}, f32[12,48]{1,0:T(8,128)}, u32[]{:S(2)}) copy-start(f32[12,48]{1,0:T(8,128)} %param.26) | copy-start | bytes 6916
  682.4 4.5 copy-start.21
  682.4 4.5 copy-start.27
  682.4 4.5 copy-start.28
  682.4 4.5 copy-start.31
  (37 other events, 85.7 us)
Sparse Core Ops, SparseCore 0:
  10.9 56.1 all-gather.3
  70.0 79.9 all-gather.5
  238.2 234.5 reduce-scatter.4
  576.8 66.9 reduce-scatter.6
  646.7 35.6 all-reduce.4
where the time goes:
time: 695 us
  blocking collectives  253 us (36%)
  matrix products  170 us (24%)
  waiting for transfers between devices  139 us (20%)
  local copies, waits for them, and re-layouts  62.5 us (9%)
  other arithmetic  53.3 us (8%)
  between operations  15.7 us (2%)
    unnamed x1, blocking collectives  225 us
    dot_general x32, matrix products, product(): jnp.einsum(form, left_side, right_side, preferred_element_type=jnp.float32)  170 us
    unnamed x6, waiting for transfers between devices  47.4 us
    psum x1, waiting for transfers between devices, body(): lax.psum(shares[0].astype(jnp.bfloat16), 'narrow').astype(jnp.float32)  32.2 us
    all_gather x1, waiting for transfers between devices, body(): lax.all_gather(packed[1], 'wide', axis=1, tiled=True)  30 us
    all_gather x1, waiting for transfers between devices, body(): lax.all_gather(packed[0], 'wide', axis=1, tiled=True)  29.4 us
    all_gather x1, blocking collectives, body(): lax.all_gather(packed[2], 'wide', axis=1, tiled=True)  23.5 us
    convert_element_type x2, other arithmetic, attend_backward(): (soft_weights * (grad_weights - inner_sum)).astype(jnp.bfloat16)  14.3 us
  transfers between devices with their start and end apart: 5, of which 4 were waited for; matrix products, arithmetic and copies ran while one was open for 26% of the time, Pallas kernels for 0%

commit v1 on v0

v1 whole, which is shorter than its diff:
```python
import functools, math
import jax, jax.numpy as jnp
from jax import lax
from jax.sharding import PartitionSpec as P
from jax.experimental import pallas as pl
from jax.experimental.pallas import tpu as pltpu

HD = 64
LOG2E = 1.4426950408889634
SCALE2 = 0.125 * LOG2E
NEG = -1e30
EPS = 1e-12
momentum_decay = 0.5
average_decay = 0.5
matrix_rate = 0.03
vector_rate = 0.3
f32, bf16 = jnp.float32, jnp.bfloat16
BIG = 60 * 2**20

def dot(a, b):
    return lax.dot_general(a, b, (((1,), (0,)), ((), ())), preferred_element_type=f32)
def dot_nt(a, b):
    return lax.dot_general(a, b, (((1,), (1,)), ((), ())), preferred_element_type=f32)
def dot_tn(a, b):
    return lax.dot_general(a, b, (((0,), (0,)), ((), ())), preferred_element_type=f32)

def key_range(c, seq, blk):
    lo = max(0, c * blk - seq // 2 + 1) // blk * blk
    hi = min(seq, -(-((c + 1) * blk - 1 + seq // 2) // blk) * blk)
    return lo, hi

def fill_bias(seg_ref, bias_ref):
    segf = seg_ref[0].astype(f32)
    seq = segf.shape[1]
    rep = jnp.broadcast_to(segf, (128, seq)).T
    for j in range(seq // 128):
        bias_ref[:, j * 128:(j + 1) * 128] = jnp.where(rep == segf[:, j * 128:(j + 1) * 128], 0.0, NEG)

def fwd_kernel(blk, x_ref, seg_ref, w_ref, b_ref, qkv_ref, c_ref, lse_ref, bias_ref, lsea_ref):
    seq, width = x_ref.shape
    x = x_ref[...]
    for j in range(3):
        sl = slice(j * width, (j + 1) * width)
        qkv_ref[:, sl] = (dot(x, w_ref[:, sl]) + b_ref[:, sl]).astype(bf16)
    fill_bias(seg_ref, bias_ref)
    lane = lax.broadcasted_iota(jnp.int32, (blk, 128), 1)
    first = lane < HD
    ones = jnp.ones((seq, 128), bf16)
    def pair(p, _):
        col = pl.multiple_of(p * 128, 128)
        q2 = qkv_ref[:, pl.ds(col, 128)]
        k2 = qkv_ref[:, pl.ds(col + width, 128)]
        v2 = jnp.concatenate([qkv_ref[:, pl.ds(col + 2 * width, 128)], ones], 1)
        for c in range(seq // blk):
            lo, hi = key_range(c, seq, blk)
            rows = slice(c * blk, (c + 1) * blk)
            qc = q2[rows]
            outs = []
            la = lsea_ref[rows, :]
            for h in range(2):
                qm = jnp.where(first if h == 0 else ~first, qc, jnp.zeros_like(qc))
                s = dot_nt(qm, k2[lo:hi]) + bias_ref[rows, lo:hi]
                m = jnp.max(s, 1, keepdims=True)
                e = jnp.exp2((s - m) * SCALE2)
                o = dot(e.astype(bf16), v2[lo:hi])
                l = o[:, 128:]
                outs.append(o[:, :128] / l)
                la = jnp.where(lane == 2 * p + h, m * SCALE2 + jnp.log(l) * LOG2E, la)
            lsea_ref[rows, :] = la
            c_ref[rows, pl.ds(col, 128)] = jnp.where(first, outs[0], outs[1]).astype(bf16)
        return 0
    lax.fori_loop(0, width // 128, pair, 0)
    lse_ref[0] = lsea_ref[...].T[:lse_ref.shape[1]]

def attn_fwd(x, seg, w, b, blk=128):
    rows, seq = seg.shape
    width = x.shape[1]
    return pl.pallas_call(
        functools.partial(fwd_kernel, blk), grid=(rows,),
        out_shape=(jax.ShapeDtypeStruct((rows * seq, 3 * width), bf16), jax.ShapeDtypeStruct((rows * seq, width), bf16),
                   jax.ShapeDtypeStruct((rows, 16, seq), f32)),
        in_specs=[pl.BlockSpec((seq, width), lambda r: (r, 0)), pl.BlockSpec((1, 1, seq), lambda r: (r, 0, 0)),
                  pl.BlockSpec((width, 3 * width), lambda r: (0, 0)), pl.BlockSpec((1, 3 * width), lambda r: (0, 0))],
        out_specs=(pl.BlockSpec((seq, 3 * width), lambda r: (r, 0)), pl.BlockSpec((seq, width), lambda r: (r, 0)),
                   pl.BlockSpec((1, 16, seq), lambda r: (r, 0, 0))),
        scratch_shapes=[pltpu.VMEM((seq, seq), f32), pltpu.VMEM((seq, 128), f32)],
        compiler_params=pltpu.CompilerParams(vmem_limit_bytes=BIG),
        name="attn_fwd",
    )(x, seg.reshape(rows, 1, seq), w, b)

def bwd_kernel(blk, seg_ref, qkv_ref, dc_ref, lse_ref, delta_ref, dh1_ref, w_ref, x_ref, dqkv_ref, gin_ref, dw_ref, db_ref, bias_ref, ds_ref, acc_ref):
    r = pl.program_id(0)
    seq = dc_ref.shape[0]
    width = dc_ref.shape[1]
    fill_bias(seg_ref, bias_ref)
    ds_ref[...] = jnp.zeros_like(ds_ref)
    lane = lax.broadcasted_iota(jnp.int32, (blk, 128), 1)
    first = lane < HD
    lane_s = lax.broadcasted_iota(jnp.int32, (seq, 128), 1)
    def pair(p, _):
        col = pl.multiple_of(p * 128, 128)
        q2 = qkv_ref[:, pl.ds(col, 128)]
        k2 = qkv_ref[:, pl.ds(col + width, 128)]
        v2 = qkv_ref[:, pl.ds(col + 2 * width, 128)]
        dc2 = dc_ref[:, pl.ds(col, 128)]
        dqs = []
        for h in range(2):
            lse = lse_ref[0, pl.ds(2 * p + h, 1), :]
            dl = delta_ref[pl.ds(2 * p + h, 1), :]
            mine = first if h == 0 else ~first
            for c in range(seq // blk):
                lo, hi = key_range(c, seq, blk)
                rows = slice(c * blk, (c + 1) * blk)
                kc, vc = k2[rows], v2[rows]
                km = jnp.where(mine, kc, jnp.zeros_like(kc))
                vm = jnp.where(mine, vc, jnp.zeros_like(vc))
                st = dot_nt(km, q2[lo:hi])
                pt = jnp.exp2((st + bias_ref[rows, lo:hi]) * SCALE2 - lse[:, lo:hi])
                dp = dot_nt(vm, dc2[lo:hi])
                ds = (pt * (dp - dl[:, lo:hi])).astype(bf16)
                ds_ref[h, rows, lo:hi] = ds
                dv = dot(pt.astype(bf16), dc2[lo:hi])
                dk = dot(ds, q2[lo:hi]) * 0.125
                if h == 0:
                    dqkv_ref[rows, pl.ds(col + 2 * width, 128)] = dv.astype(bf16)
                    dqkv_ref[rows, pl.ds(col + width, 128)] = dk.astype(bf16)
                else:
                    ov = dqkv_ref[rows, pl.ds(col + 2 * width, 128)]
                    ok = dqkv_ref[rows, pl.ds(col + width, 128)]
                    dqkv_ref[rows, pl.ds(col + 2 * width, 128)] = jnp.where(first, ov, dv.astype(bf16))
                    dqkv_ref[rows, pl.ds(col + width, 128)] = jnp.where(first, ok, dk.astype(bf16))
            dqs.append(dot_tn(ds_ref[h], k2) * 0.125)
        dqkv_ref[:, pl.ds(col, 128)] = jnp.where(lane_s < HD, dqs[0], dqs[1]).astype(bf16)
        return 0
    lax.fori_loop(0, width // 128, pair, 0)
    dqkv = dqkv_ref[...]
    gin_ref[...] = (dh1_ref[...] + dot_nt(dqkv, w_ref[...])).astype(bf16)
    x = x_ref[...]
    for j in range(3):
        sl = slice(j * width, (j + 1) * width)
        d = dot_tn(x, dqkv[:, sl])
        s = jnp.sum(dqkv[:, sl].astype(f32), 0, keepdims=True)
        @pl.when(r == 0)
        def _():
            acc_ref[:, sl] = d
            db_ref[:, sl] = s
        @pl.when(r == pl.num_programs(0) - 1)
        def _():
            dw_ref[:, sl] = (acc_ref[:, sl] + d).astype(bf16)
            db_ref[:, sl] += s

def attn_bwd(seg, qkv, dc, lse, delta, dh1, w, x, blk=128):
    rows, seq = seg.shape
    width = dc.shape[1]
    assert rows == 2
    return pl.pallas_call(
        functools.partial(bwd_kernel, blk), grid=(rows,),
        out_shape=(jax.ShapeDtypeStruct((rows * seq, 3 * width), bf16), jax.ShapeDtypeStruct((rows * seq, width), bf16),
                   jax.ShapeDtypeStruct((width, 3 * width), bf16), jax.ShapeDtypeStruct((1, 3 * width), f32)),
        in_specs=[pl.BlockSpec((1, 1, seq), lambda r: (r, 0, 0)), pl.BlockSpec((seq, 3 * width), lambda r: (r, 0)),
                  pl.BlockSpec((seq, width), lambda r: (r, 0)), pl.BlockSpec((1, 16, seq), lambda r: (r, 0, 0)),
                  pl.BlockSpec((16, seq), lambda r: (0, r)), pl.BlockSpec((seq, width), lambda r: (r, 0)),
                  pl.BlockSpec((width, 3 * width), lambda r: (0, 0)), pl.BlockSpec((seq, width), lambda r: (r, 0))],
        out_specs=(pl.BlockSpec((seq, 3 * width), lambda r: (r, 0)), pl.BlockSpec((seq, width), lambda r: (r, 0)),
                   pl.BlockSpec((width, 3 * width), lambda r: (0, 0)), pl.BlockSpec((1, 3 * width), lambda r: (0, 0))),
        scratch_shapes=[pltpu.VMEM((seq, seq), f32), pltpu.VMEM((2, seq, seq), bf16), pltpu.VMEM((width, 3 * width), f32)],
        compiler_params=pltpu.CompilerParams(vmem_limit_bytes=BIG),
        name="attn_bwd",
    )(seg.reshape(rows, 1, seq), qkv, dc, lse, delta, dh1, w, x)

RSQRT_2PI = 1.0 / math.sqrt(2 * math.pi)
def gelu_parts(u):
    phi_cdf = 0.5 + 0.5 * lax.erf(u * math.sqrt(0.5))
    dens = jnp.exp2(u * u * (-0.5 * LOG2E)) * RSQRT_2PI
    return u * phi_cdf, phi_cdf + u * dens

def mid_kernel(chunk, x_ref, c_ref, e_ref, wo_ref, win_ref, wd_ref, v_ref, bin_ref,
               out_ref, y1_ref, g_ref, dz_ref, du_ref, da_ref, dc_ref, dh1_ref, delta_ref, dv_ref, dbin_ref, gp_ref):
    i = pl.program_id(0)
    blk, width = x_ref.shape
    ff = win_ref.shape[1]
    @pl.when(i == 0)
    def _():
        dv_ref[...] = jnp.zeros_like(dv_ref)
        dbin_ref[...] = jnp.zeros_like(dbin_ref)
    g1, s1, g2, s2, bo, bd = (v_ref[j:j + 1, :] for j in (0, 1, 2, 3, 6, 7))
    cb = c_ref[...]
    h1 = x_ref[...].astype(f32) + (dot(cb, wo_ref[...]) + bo)
    cen = h1 - jnp.mean(h1, 1, keepdims=True)
    r1 = lax.rsqrt(jnp.mean(cen * cen, 1, keepdims=True) + EPS)
    n1 = cen * r1
    y1 = n1 * g1 + s1
    y1l = y1.astype(bf16)
    y1_ref[...] = y1l
    z = jnp.zeros((blk, width), f32)
    for j in range(ff // chunk):
        sl = slice(j * chunk, (j + 1) * chunk)
        u = dot(y1l, win_ref[:, sl]) + bin_ref[:, sl]
        g, gp = gelu_parts(u)
        gl = g.astype(bf16)
        g_ref[:, sl] = gl
        gp_ref[:, sl] = gp
        z += dot_nt(gl, wd_ref[:, sl])
    h2 = y1 + (z + bd)
    cen = h2 - jnp.mean(h2, 1, keepdims=True)
    r2 = lax.rsqrt(jnp.mean(cen * cen, 1, keepdims=True) + EPS)
    n2 = cen * r2
    out_ref[...] = (n2 * g2 + s2).astype(bf16)
    e = e_ref[...].astype(f32)
    eg = e * g2
    dh2 = r2 * (eg - jnp.mean(eg, 1, keepdims=True) - n2 * jnp.mean(eg * n2, 1, keepdims=True))
    dz = dh2.astype(bf16)
    dz_ref[...] = dz
    dy1 = dh2
    for j in range(ff // chunk):
        sl = slice(j * chunk, (j + 1) * chunk)
        du = (dot(dz, wd_ref[:, sl]) * gp_ref[:, sl]).astype(bf16)
        du_ref[:, sl] = du
        dbin_ref[:, sl] += jnp.sum(du.astype(f32), 0, keepdims=True)
        dy1 += dot_nt(du, win_ref[:, sl])
    dn = dy1 * g1
    dh1 = r1 * (dn - jnp.mean(dn, 1, keepdims=True) - n1 * jnp.mean(dn * n1, 1, keepdims=True))
    dh1_ref[...] = dh1
    da = dh1.astype(bf16)
    da_ref[...] = da
    dc = dot_nt(da, wo_ref[...]).astype(bf16)
    dc_ref[...] = dc
    prod = dc.astype(f32) * cb.astype(f32)
    hi = prod.astype(bf16)
    lo = (prod - hi.astype(f32)).astype(bf16)
    sel = jnp.where(lax.broadcasted_iota(jnp.int32, (16, width), 0) == lax.broadcasted_iota(jnp.int32, (16, width), 1) // HD, 1.0, 0.0).astype(bf16)
    delta_ref[...] = dot_nt(sel, hi) + dot_nt(sel, lo)
    parts = [dy1 * n1, dy1, e * n2, e, da.astype(f32), dz.astype(f32)]
    for j, t in zip((0, 1, 2, 3, 6, 7), parts):
        dv_ref[j:j + 1, :] += jnp.sum(t, 0, keepdims=True)

def mid(x, c, e, wo, win, wd, vec, bin_, blk=256, chunk=768):
    n, width = x.shape
    ff = win.shape[1]
    tok = lambda w: pl.BlockSpec((blk, w), lambda i: (i, 0))
    full = lambda a: pl.BlockSpec(a.shape, lambda i: (0, 0), pipeline_mode=pl.Buffered(1))
    sh = jax.ShapeDtypeStruct
    return pl.pallas_call(
        functools.partial(mid_kernel, chunk), grid=(n // blk,),
        out_shape=(sh((n, width), bf16), sh((n, width), bf16), sh((n, ff), bf16), sh((n, width), bf16), sh((n, ff), bf16),
                   sh((n, width), bf16), sh((n, width), bf16), sh((n, width), f32), sh((16, n), f32), sh((8, width), f32), sh((1, ff), f32)),
        in_specs=[tok(width), tok(width), tok(width), full(wo), full(win), full(wd), full(vec), full(bin_)],
        out_specs=(tok(width), tok(width), tok(ff), tok(width), tok(ff), tok(width), tok(width), tok(width),
                   pl.BlockSpec((16, blk), lambda i: (0, i)), pl.BlockSpec((8, width), lambda i: (0, 0)), pl.BlockSpec((1, ff), lambda i: (0, 0))),
        scratch_shapes=[pltpu.VMEM((blk, ff), f32)],
        compiler_params=pltpu.CompilerParams(vmem_limit_bytes=BIG),
        name="middle",
    )(x, c, e, wo, win, wd, vec, bin_)

def wgrad_kernel(a_ref, b_ref, o_ref):
    o_ref[...] = dot_tn(a_ref[...], b_ref[...]).astype(bf16)

def wgrad(a, b, blk=768):
    n, m = a.shape
    k = b.shape[1]
    return pl.pallas_call(wgrad_kernel, grid=(k // blk,), out_shape=jax.ShapeDtypeStruct((m, k), bf16),
        in_specs=[pl.BlockSpec((n, m), lambda j: (0, 0)), pl.BlockSpec((n, blk), lambda j: (0, j))],
        out_specs=pl.BlockSpec((m, blk), lambda j: (0, j)),
        compiler_params=pltpu.CompilerParams(vmem_limit_bytes=BIG), name="wgrad")(a, b)


def pack_columns(attention, dense, vectors):
    count = vectors.shape[0]
    vector_cols = jnp.pad(vectors.T, ((0, 0), (0, 128 - count)))
    first = jnp.concatenate([attention[0], attention[1], attention[2], vector_cols], 1)
    second = jnp.concatenate([attention[3], dense[0], dense[1]], 1)
    return first, second


def advance(gradient, moment, weight, average, step_rate):
    moment_new = momentum_decay * moment + gradient
    weight_new = weight - step_rate * (gradient + momentum_decay * moment_new)
    average_new = average_decay * average + (1.0 - average_decay) * weight_new
    return (moment_new, weight_new, average_new)


def body(
    hidden_in,
    segment_ids,
    cotangent,
    attention_weights,
    attention_momentum,
    attention_average,
    dense_weights,
    dense_momentum,
    dense_average,
    vector_params,
    vector_momentum,
    vector_average,
):
    row_count, length, width = hidden_in.shape
    ff = dense_weights.shape[-1]
    vector_rows = vector_params.shape[0]
    x = hidden_in.reshape(-1, width)
    e = cotangent.reshape(-1, width)
    first, second = pack_columns(attention_weights, dense_weights, vector_params)
    first_full = lax.all_gather(first.astype(bf16), "wide", axis=0, tiled=True)
    second_full = lax.all_gather(second.astype(bf16), "wide", axis=0, tiled=True)
    vec = first_full[:, 3 * width : 3 * width + vector_rows].astype(f32).T
    bias_qkv = jnp.concatenate([vec[4:5], jnp.zeros((1, width), f32), vec[5:6]], 1)
    w_qkv = first_full[:, : 3 * width]
    wo, win, wd = (second_full[:, :width], second_full[:, width : width + ff], second_full[:, width + ff :])
    qkv, c, lse = attn_fwd(x, segment_ids, w_qkv, bias_qkv)
    out, y1, g, dz, du, da, dc, dh1, delta, dvec, dbin = mid(
        x, c, e, wo, win, wd, vec, vec[8:].reshape(1, ff)
    )
    grad_second = jnp.concatenate([wgrad(c, da), wgrad(y1, du), wgrad(dz, g)], 1)
    share_second = lax.psum_scatter(grad_second, "wide", scatter_dimension=0, tiled=True)
    dqkv, gin, dw, db = attn_bwd(segment_ids, qkv, dc, lse, delta, dh1, w_qkv, x)
    dvec = jnp.concatenate(
        [dvec[:4], db[:, :width], db[:, 2 * width :], dvec[6:8], dbin.reshape(-1, width)], 0
    )
    grad_first = jnp.concatenate(
        [dw, jnp.pad(dvec.T, ((0, 0), (0, 128 - vector_rows))).astype(bf16)], 1
    )
    share_first = lax.psum_scatter(grad_first, "wide", scatter_dimension=0, tiled=True)
    replicas = lax.axis_size("narrow")
    tokens_all = row_count * length * lax.axis_size("wide") * replicas
    grad_scale = math.sqrt(tokens_all) / replicas
    t1 = lax.psum(share_first, "narrow").astype(f32) / replicas
    t2 = lax.psum(share_second, "narrow").astype(f32) / replicas
    cut = lambda t, j: t[:, j * width : (j + 1) * width]
    attention_grad = jnp.stack([cut(t1, 0), cut(t1, 1), cut(t1, 2), cut(t2, 0)])
    dense_grad = jnp.stack([t2[:, width : width + ff], t2[:, width + ff :]])
    vector_grad = t1[:, 3 * width : 3 * width + vector_rows].T
    attention_new = advance(attention_grad, attention_momentum, attention_weights, attention_average, matrix_rate / grad_scale)
    dense_new = advance(dense_grad, dense_momentum, dense_weights, dense_average, matrix_rate / grad_scale)
    vector_new = advance(vector_grad, vector_momentum, vector_params, vector_average, vector_rate / grad_scale)
    return (out.reshape(hidden_in.shape), gin.reshape(hidden_in.shape)) + attention_new + dense_new + vector_new


def solution(mesh):
    token = P(("wide", "narrow"), None, None)
    matrix = P(None, "wide", None)
    vector = P(None, "wide")
    in_specs = (token, P(("wide", "narrow"), None), token) + (matrix,) * 6 + (vector,) * 3
    out_specs = (token, token) + (matrix,) * 6 + (vector,) * 3
    return jax.shard_map(body, mesh=mesh, in_specs=in_specs, out_specs=out_specs, check_vma=False)
```

time: 695 us -> 505 us (0.73)
  blocking collectives: 253 us -> 0 us
  matrix products: 170 us -> 0 us
  waiting for transfers between devices: 139 us -> 307 us
  Pallas kernels: 0 us -> 130 us
  local copies, waits for them, and re-layouts: 62.5 us -> 25.9 us
  other arithmetic: 53.3 us -> 26.5 us
    unnamed x1 -> x0, blocking collectives: 225 us -> none
    dot_general x32 -> x0, matrix products: 170 us -> none  [product(): jnp.einsum(form, left_side, right_side, preferred_element_type=jnp.float32)]
    reduce_scatter x1 -> x2, waiting for transfers between devices: 0.01 us -> 159 us  [the longest x1 123 us: body(): lax.psum_scatter(grad_second, 'wide', scatter_dimension=0, tiled=True)]
    pallas_call x0 -> x6, Pallas kernels: none -> 130 us  [the longest x1 46.4 us: attn_bwd(): pl.pallas_call(functools.partial(bwd_kernel, blk), grid=(rows,), out_shap...]
    all_gather x2, waiting for transfers between devices: 59.4 us -> 111 us  [the longest x1 61.5 us: body(): lax.all_gather(second.astype(bf16), 'wide', axis=0, tiled=True)]
    unnamed x6 -> x5, waiting for transfers between devices: 47.4 us -> 0.08 us
    all_gather x1 -> x0, blocking collectives: 23.5 us -> none  [body(): lax.all_gather(packed[2], 'wide', axis=1, tiled=True)]
    convert_element_type x6 -> x0, other arithmetic: 20.6 us -> none  [the longest x2 14.3 us: attend_backward(): (soft_weights * (grad_weights - inner_sum)).astype(jnp.bfloat16)]
  transfers between devices with their start and end apart: 5 -> 5, of which waited for: 4 -> 5; matrix products, arithmetic and copies ran while one was open for 26% -> 4% of each run, Pallas kernels for 0% -> 9%
where the time goes in v1:
time: 505 us; the launch traced here: 504 us
  waiting for transfers between devices  307 us (61%)
  Pallas kernels  130 us (26%)
  other arithmetic  26.5 us (5%)
  local copies, waits for them, and re-layouts  25.9 us (5%)
  between operations  14.1 us (3%)
    reduce_scatter x1, waiting for transfers between devices, body(): lax.psum_scatter(grad_second, 'wide', scatter_dimension=0, tiled=True)  123 us
    all_gather x1, waiting for transfers between devices, body(): lax.all_gather(second.astype(bf16), 'wide', axis=0, tiled=True)  61.5 us
    all_gather x1, waiting for transfers between devices, body(): first_full = lax.all_gather(first.astype(bf16), 'wide', axis=0, tiled=True)  49.6 us
    pallas_call x1, Pallas kernels, attn_bwd(): pl.pallas_call(functools.partial(bwd_kernel, blk), grid=(rows,), out_shap...  46.4 us
    pallas_call x1, Pallas kernels, mid(): pl.pallas_call(functools.partial(mid_kernel, chunk), grid=(n // blk,), ou...  38.9 us
    psum x1, waiting for transfers between devices, body(): t2 = lax.psum(share_second, 'narrow').astype(f32) / replicas  36.9 us
    reduce_scatter x1, waiting for transfers between devices, body(): lax.psum_scatter(grad_first, 'wide', scatter_dimension=0, tiled=True)  35.6 us
    pallas_call x3, Pallas kernels, wgrad(): pl.pallas_call(wgrad_kernel, grid=(k // blk,), out_shape=jax.ShapeDtypeSt...  23.5 us
  transfers between devices with their start and end apart: 5, of which 5 were waited for; matrix products, arithmetic and copies ran while one was open for 4% of the time, Pallas kernels for 9%

profile of v1, /device:TPU:0, one launch (start us, length us, event | category | flops | bytes accessed | tf_op | source)
XLA Modules:
  0.0 503.7 jit_solution(11484020791488657671)
XLA Ops:
  7.2 1.2 convert.48
  8.4 0.7 convert.49
  9.3 0.7 fusion.3
  10.2 0.9 pad_maximum_fusion.2
  11.8 49.6 %all-gather.3.cloned.1.call-done = bf16[768,2432]{1,0:T(8,128)(2,1)} async-done(((bf16[48,2432]{1,0:T(8,128)(2,1)}), bf16[768,2432]{1,0:T(8,128)(2,1)}) %all-gather.3.cloned.1.call-update) | async-done | bytes 3735568 | tf_op jit(solution)/shard_map/all_gather | solution.py:302
  61.3 1.0 convert_bitcast_fusion
  62.5 0.8 copy.67.v_ref
  64.6 4.0 slice.113.w_ref
  69.2 21.3 %attn_fwd.1 = (bf16[1024,2304]{1,0:T(8,128)(2,1)}, bf16[1024,768]{1,0:T(8,128)(2,1)}, f32[2,16,512]{2,1,0:T(8,128)}) custom-call(bf16[1024,768]{1,0:T(8,128)(2,1)} %bitcast.43, s32[2,1,512]{2,1,0:T(1,128)} %reshape.46.seg_ref, bf16[768,2304]{1,0:T(8,128)(2,1)} %slice.113.w_ref, f32[1,2304]{1,0:T(1,128)} %fusion.4.b_ref), custom_call_target="tpu_custom_call" | custom-call | tf_op jit(solution)/shard_map/attn_fwd/pallas_call | solution.py:78
  90.5 61.5 %all-gather.5.cloned.1.call-done = bf16[768,6912]{1,0:T(8,128)(2,1)} async-done(((bf16[48,6912]{1,0:T(8,128)(2,1)}), bf16[768,6912]{1,0:T(8,128)(2,1)}) %all-gather.5.cloned.1.call-update) | async-done | bytes 10616848 | tf_op jit(solution)/shard_map/all_gather | solution.py:303
  151.9 8.1 %fusion.5 = (bf16[768,3072]{1,0:T(8,128)(2,1)}, bf16[768,3072]{1,0:T(8,128)(2,1)}) fusion(bf16[768,6912]{1,0:T(8,128)(2,1)} %all-gather.5.cloned.1.call-done), kind=kLoop, calls=%fused_computation.38 | loop fusion | bytes 18874368 | tf_op jit(solution)/shard_map/slice | solution.py:307
  160.1 2.4 slice.120.wo_ref
  162.4 38.9 %middle.1 = (bf16[1024,768]{1,0:T(8,128)(2,1)}, bf16[1024,768]{1,0:T(8,128)(2,1)}, bf16[1024,3072]{1,0:T(8,128)(2,1)}, bf16[1024,768]{1,0:T(8,128)(2,1)}, bf16[1...) custom-call(bf16[1024,768]{1,0:T(8,128)(2,1)} %bitcast.44, ...), custom_call_target="tpu_custom_call" | custom-call | tf_op jit(solution)/shard_map/middle/pallas_call | solution.py:243
  201.3 0.7 convert.51
  202.1 46.4 %attn_bwd.1 = (bf16[1024,2304]{1,0:T(8,128)(2,1)}, bf16[1024,768]{1,0:T(8,128)(2,1)}, bf16[768,2304]{1,0:T(8,128)(2,1)}, f32[1,2304]{1,0:T(1,128)}) custom-call(s32[2,1,512]{2,1,0:T(1,128)} %reshape.46.seg_ref, bf16[1024,2304]{1,0:T(8,128)(2,1)} %get-tuple-element.30.qkv_ref, bf16[1024,768]{1,0:T(8,128)(2,1)} %get-tuple-element.31.dc_ref, ...), custom_call_target="tpu_custom_call" | custom-call | tf_op jit(solution)/shard_map/attn_bwd/pallas_call | solution.py:156
  248.5 0.7 convert.52
  249.5 4.2 fusion.1
  253.7 4.3 wgrad.3
  258.0 9.6 %wgrad.4 = bf16[768,3072]{1,0:T(8,128)(2,1)} custom-call(bf16[1024,768]{1,0:T(8,128)(2,1)} %get-tuple-element.41.a_ref, bf16[1024,3072]{1,0:T(8,128)(2,1)} %get-tuple-element.42.b_ref), custom_call_target="tpu_custom_call" | custom-call | tf_op jit(solution)/shard_map/wgrad/pallas_call | solution.py:261
  267.6 9.5 %wgrad.5 = bf16[768,3072]{1,0:T(8,128)(2,1)} custom-call(bf16[1024,768]{1,0:T(8,128)(2,1)} %get-tuple-element.43.a_ref, bf16[1024,3072]{1,0:T(8,128)(2,1)} %get-tuple-element.44.b_ref), custom_call_target="tpu_custom_call" | custom-call | tf_op jit(solution)/shard_map/wgrad/pallas_call | solution.py:261
  277.2 8.9 %pad_maximum_fusion = bf16[768,6912]{1,0:T(8,128)(2,1)} fusion(bf16[768,3072]{1,0:T(8,128)(2,1)} %wgrad.5, bf16[768,3072]{1,0:T(8,128)(2,1)} %wgrad.4, bf16[768,768]{1,0:T(8,128)(2,1)S(1)} %copy-done.1), kind=kLoop, calls=%fused_computation | loop fusion | flops 31850496 | bytes 21233664 | tf_op jit(solution)/shard_map/concatenate | solution.py:312
  286.2 35.6 %reduce-scatter.3.cloned.1.call-done = bf16[48,2432]{1,0:T(8,128)(2,1)} async-done(((bf16[768,2432]{1,0:T(8,128)(2,1)}), bf16[48,2432]{1,0:T(8,128)(2,1)}) %reduce-scatter.3.cloned.1.call-update) | async-done | bytes 233488 | tf_op jit(solution)/shard_map/reduce_scatter | solution.py:321
  321.7 123.4 %reduce-scatter.5.cloned.1.call-done = bf16[48,6912]{1,0:T(8,128)(2,1)} async-done(((bf16[768,6912]{1,0:T(8,128)(2,1)}), bf16[48,6912]{1,0:T(8,128)(2,1)}) %reduce-scatter.5.cloned.1.call-update) | async-done | bytes 663568 | tf_op jit(solution)/shard_map/reduce_scatter | solution.py:313
  447.3 36.9 %all-reduce.5.cloned.1.call-done = (bf16[48,6912]{1,0:T(8,128)(2,1)}, bf16[48,2432]{1,0:T(8,128)(2,1)}) async-done(((bf16[48,6912]{1,0:T(8,128)(2,1)}, bf16[48,2432]{1,0:T(8,128)(2,1)}), (bf16[48,6912]{1,0:T(8,128)(2,1)}, bf16[48,2432]{1,0:T(8,128)(2,1)})) %all-reduce.5.cloned.1.call-update) | async-done | bytes 897040 | tf_op jit(solution)/shard_map/psum | solution.py:326
  484.2 1.2 convert_multiply_fusion
  485.6 0.8 copy-done.10
  486.4 0.8 slice_bitcast_fusion.7
  487.8 1.4 copy.75
  489.3 1.4 copy.76
  490.7 1.4 copy.77
  492.1 3.6 add_multiply_fusion
  495.8 1.3 add_multiply_fusion.1
  (74 shorter events, 6.5 us)
Async XLA Ops:
  7.2 2.9 copy-start
  7.2 54.2 %all-gather.3.cloned.1.call-start = ((), (), s32[]{:S(2)}) async-start(), calls=%async_computation.2 | async-start | bytes 3969024 | tf_op jit(solution)/shard_map/all_gather | solution.py:302
  10.0 142.0 %all-gather.5.cloned.1.call-start = ((), (), s32[]{:S(2)}) async-start(), calls=%async_computation.3 | async-start | bytes 11280384 | tf_op jit(solution)/shard_map/all_gather | solution.py:303
  10.1 1.0 copy-start.18
  11.1 310.7 %reduce-scatter.3.cloned.1.call-start = ((), (), s32[]{:S(2)}) async-start(), calls=%async_computation.4 | async-start | bytes 3969024 | tf_op jit(solution)/shard_map/reduce_scatter | solution.py:321
  202.1 47.1 %copy-start.15 = (f32[1,3072]{1,0:T(1,128)S(1)}, f32[1,3072]{1,0:T(1,128)}, u32[]{:S(2)}) copy-start(f32[1,3072]{1,0:T(1,128)} %get-tuple-element.39) | copy-start | bytes 36868
  253.7 191.5 %reduce-scatter.5.cloned.1.call-start = ((), (), s32[]{:S(2)}) async-start(), calls=%async_computation.5 | async-start | bytes 11280384 | tf_op jit(solution)/shard_map/reduce_scatter | solution.py:313
  267.6 9.5 %copy-start.1 = (bf16[768,768]{1,0:T(8,128)(2,1)S(1)}, bf16[768,768]{1,0:T(8,128)(2,1)}, u32[]{:S(2)}) copy-start(bf16[768,768]{1,0:T(8,128)(2,1)} %wgrad.3) | copy-start | bytes 3538948
  286.1 159.1 %copy-start.14 = (f32[12,48]{1,0:T(8,128)S(1)}, f32[12,48]{1,0:T(8,128)}, u32[]{:S(2)}) copy-start(f32[12,48]{1,0:T(8,128)} %param.21) | copy-start | bytes 6916
  286.1 159.8 %copy-start.16 = (f32[12,48]{1,0:T(8,128)S(1)}, f32[12,48]{1,0:T(8,128)}, u32[]{:S(2)}) copy-start(f32[12,48]{1,0:T(8,128)} %param.22) | copy-start | bytes 6916
  286.1 160.5 %copy-start.17 = (f32[12,48]{1,0:T(8,128)S(1)}, f32[12,48]{1,0:T(8,128)}, u32[]{:S(2)}) copy-start(f32[12,48]{1,0:T(8,128)} %param.23) | copy-start | bytes 6916
  286.1 198.1 %all-reduce.5.cloned.1.call-start = ((), (), s32[]{:S(2)}) async-start(), calls=%async_computation.6 | async-start | bytes 1794048 | tf_op jit(solution)/shard_map/psum | solution.py:326
  485.4 0.9 copy-start.10
  485.4 1.8 copy-start.11
  485.4 1.8 copy-start.12
  485.4 1.8 copy-start.13
  485.6 6.5 %copy-start.3 = (f32[2,48,3072]{2,1,0:T(8,128)S(1)}, f32[2,48,3072]{2,1,0:T(8,128)}, u32[]{:S(2)}) copy-start(f32[2,48,3072]{2,1,0:T(8,128)} %param.20) | copy-start | bytes 3538948
  492.1 3.7 copy-start.2
  492.1 3.7 copy-start.4
  492.1 3.7 copy-start.5
  492.1 3.7 copy-start.6
  492.1 3.7 copy-start.7
  492.1 3.7 copy-start.8
  492.1 3.7 copy-start.9
Sparse Core Ops, SparseCore 0:
  10.8 50.5 all-gather.2
  64.2 87.7 all-gather.4
  253.8 67.9 reduce-scatter.2
  326.2 118.9 reduce-scatter.4
  447.5 36.6 all-reduce.4

commit v2 on v1

--- a/solution.py
+++ b/solution.py
@@ -264,6 +264,326 @@
         compiler_params=pltpu.CompilerParams(vmem_limit_bytes=BIG), name="wgrad")(a, b)
 
 
+MESH = pl.DeviceIdType.MESH
+LANES = 128
+PIECE = 3 * LANES
+LAG = 2
+AHEAD = 8
+
+
+class Place:
+    def __init__(self):
+        self.w = lax.axis_index("wide")
+        self.x = lax.axis_index("narrow")
+        self.core = lax.rem(self.w, 2)
+        self.y = lax.rem(self.w // 2, 2)
+        self.z = self.w // 4
+
+    def at(self, z=None, y=None, core=None):
+        z, y, core = (mine if v is None else v for v, mine in ((z, self.z), (y, self.y), (core, self.core)))
+        return (4 * z + 2 * y + core, self.x)
+
+    def z_peer(self, k):
+        return lax.rem(self.z + k, 4)
+
+    def greet(self):
+        barrier = pltpu.get_barrier_semaphore()
+        peers = [self.at(z=self.z_peer(k)) for k in (1, 2, 3)]
+        peers += [self.at(y=1 - self.y), self.at(core=1 - self.core), (self.w, 1 - self.x)]
+        for peer in peers:
+            pl.semaphore_signal(barrier, inc=1, device_id=peer, device_id_type=MESH)
+        pl.semaphore_wait(barrier, len(peers))
+
+
+def remote(src, dst, send, recv, device):
+    return pltpu.make_async_remote_copy(src_ref=src, dst_ref=dst, send_sem=send, recv_sem=recv, device_id=device, device_id_type=MESH)
+
+
+def window(col, size):
+    return pl.ds(pl.multiple_of(col, LANES), size)
+
+
+class Gather:
+    def __init__(self, place, shard, full, sems):
+        self.p, self.shard, self.full = place, shard, full
+        self.zs, self.zr, self.ys, self.yr, self.xs, self.xr, self.cs, self.cr = sems
+
+    def own(self, i, col, vec):
+        return window(col, LANES) if vec else window(col + self.p.x * LANES, 2 * LANES)
+
+    def split(self, col, x):
+        return window(col + 2 * LANES * x, LANES)
+
+    def z_copy(self, i, col, vec, k):
+        p = self.p
+        cols = self.own(i, col, vec)
+        return remote(self.shard.at[:, cols], self.full.at[p.z, p.y, p.core, :, cols], self.zs.at[i, k], self.zr.at[i, p.z], p.at(z=p.z_peer(k)))
+
+    def z_arrival(self, i, col, vec, k):
+        p = self.p
+        cols = self.own(i, col, vec)
+        src = p.z_peer(k)
+        return remote(self.shard.at[:, cols], self.full.at[src, p.y, p.core, :, cols], self.zs.at[i, k], self.zr.at[i, src], p.at(z=src))
+
+    def y_copy(self, i, col, vec, incoming):
+        p = self.p
+        part = self.full.at[:, 1 - p.y if incoming else p.y, p.core, :, self.own(i, col, vec)]
+        return remote(part, part, self.ys.at[i], self.yr.at[i], p.at(y=1 - p.y))
+
+    def x_copy(self, i, col, incoming):
+        p = self.p
+        part = self.full.at[:, :, p.core, :, self.split(col, 1 - p.x if incoming else p.x)]
+        return remote(part, part, self.xs.at[i], self.xr.at[i], (p.w, 1 - p.x))
+
+    def core_copy(self, i, col, vec, incoming):
+        p = self.p
+        part = self.full.at[:, :, 1 - p.core if incoming else p.core, :, window(col, LANES if vec else PIECE)]
+        return remote(part, part, self.cs.at[i], self.cr.at[i], p.at(core=1 - p.core))
+
+    def z_start(self, i, col, vec=False):
+        for k in (2, 1, 3):
+            self.z_copy(i, col, vec, k).start()
+
+    def y_step(self, i, col, vec=False):
+        for k in (1, 2, 3):
+            self.z_arrival(i, col, vec, k).wait_recv()
+        self.y_copy(i, col, vec, False).start()
+
+    def x_step(self, i, col, vec=False):
+        self.y_copy(i, col, vec, True).wait_recv()
+        if not vec:
+            self.x_copy(i, col, False).start()
+
+    def core_step(self, i, col, vec=False):
+        if not vec:
+            self.x_copy(i, col, True).wait_recv()
+        self.core_copy(i, col, vec, False).start()
+
+    def arrive(self, i, col, vec=False):
+        self.core_copy(i, col, vec, True).wait_recv()
+
+    def sent(self, i, col, vec=False):
+        for k in (1, 2, 3):
+            self.z_copy(i, col, vec, k).wait_send()
+        self.y_copy(i, col, vec, False).wait_send()
+        if not vec:
+            self.x_copy(i, col, False).wait_send()
+        self.core_copy(i, col, vec, False).wait_send()
+
+
+def gather_sems(pieces):
+    dma = pltpu.SemaphoreType.DMA
+    return [dma((pieces, 4)), dma((pieces, 4))] + [dma((pieces,))] * 6
+
+
+def gather_kernel(shard, full, own_sem, *sems):
+    place = Place()
+    total = shard.shape[1] // PIECE
+    vec_col = total * PIECE
+    g = Gather(place, shard, full, sems)
+
+    def keep(i, col, vec=False):
+        cols = g.own(i, col, vec)
+        return pltpu.make_async_copy(shard.at[:, cols], full.at[place.z, place.y, place.core, :, cols], own_sem.at[i])
+
+    lax.fori_loop(0, total, lambda i, _: (keep(i, i * PIECE).start(), 0)[1], 0)
+    keep(total, vec_col, True).start()
+    place.greet()
+    g.z_start(total, vec_col, True)
+
+    def each(step):
+        lax.fori_loop(0, total, lambda i, _: (step(i, i * PIECE), 0)[1], 0)
+
+    each(g.z_start)
+    lax.fori_loop(0, total, lambda i, _: (keep(i, i * PIECE).wait(), 0)[1], 0)
+    keep(total, vec_col, True).wait()
+    g.y_step(total, vec_col, True)
+
+    def turn(i, _):
+        def at(lag, step):
+            @pl.when((i >= lag) & (i < total + lag))
+            def _():
+                step(i - lag, (i - lag) * PIECE)
+
+        at(0, g.y_step)
+        at(LAG, g.x_step)
+        at(2 * LAG, g.core_step)
+        return 0
+
+    lax.fori_loop(0, total + 2 * LAG, turn, 0)
+    g.x_step(total, vec_col, True)
+    g.core_step(total, vec_col, True)
+    each(g.arrive)
+    g.arrive(total, vec_col, True)
+    each(g.sent)
+    g.sent(total, vec_col, True)
+
+
+def gather_all(shard):
+    rows, cols = shard.shape
+    total = cols // PIECE
+    assert cols == total * PIECE + LANES
+    full = pl.pallas_call(
+        gather_kernel,
+        out_shape=jax.ShapeDtypeStruct((4, 2, 2, rows, cols), bf16),
+        in_specs=[pl.BlockSpec(memory_space=pl.ANY)],
+        out_specs=pl.BlockSpec(memory_space=pl.ANY),
+        scratch_shapes=[pltpu.SemaphoreType.DMA((total + 1,))] + gather_sems(total + 1),
+        compiler_params=pltpu.CompilerParams(collective_id=0, has_side_effects=True),
+        name="gather",
+    )(shard)
+    return full.reshape(16 * rows, cols)
+
+
+class Reduce:
+    def __init__(self, place, part, own, fromc, fromx, fromy, fromz, fromp, done, sems):
+        self.p, self.part, self.own = place, part, own
+        self.fromc, self.fromx, self.fromy, self.fromz, self.fromp, self.done = fromc, fromx, fromy, fromz, fromp, done
+        self.ls, self.cs, self.cr, self.xs, self.xr, self.ys, self.yr, self.zs, self.zr, self.ps, self.pr = sems
+
+    def local(self, i, col):
+        return pltpu.make_async_copy(self.part.at[:, :, self.p.core, :, window(col, PIECE)], self.own.at[i], self.ls.at[i])
+
+    def core_copy(self, i, col):
+        p = self.p
+        return remote(self.part.at[:, :, 1 - p.core, :, window(col, PIECE)], self.fromc.at[i], self.cs.at[i], self.cr.at[i], p.at(core=1 - p.core))
+
+    def lanes(self, x):
+        return window(2 * LANES * x, LANES)
+
+    def mine(self):
+        return window(self.p.x * LANES, 2 * LANES)
+
+    def x_copy(self, i):
+        p = self.p
+        return remote(self.own.at[i, :, :, :, self.lanes(1 - p.x)], self.fromx.at[i], self.xs.at[i], self.xr.at[i], (p.w, 1 - p.x))
+
+    def y_copy(self, i):
+        p = self.p
+        return remote(self.own.at[i, :, 1 - p.y, :, self.mine()], self.fromy.at[i], self.ys.at[i], self.yr.at[i], p.at(y=1 - p.y))
+
+    def z_copy(self, i, k):
+        p = self.p
+        to = p.z_peer(k)
+        return remote(self.own.at[i, to, p.y, :, self.mine()], self.fromz.at[i, p.z], self.zs.at[i, k], self.zr.at[i, p.z], p.at(z=to))
+
+    def z_arrival(self, i, k):
+        p = self.p
+        src = p.z_peer(k)
+        return remote(self.own.at[i, p.z, p.y, :, self.mine()], self.fromz.at[i, src], self.zs.at[i, k], self.zr.at[i, src], p.at(z=src))
+
+    def p_copy(self, i):
+        p = self.p
+        return remote(self.done.at[i], self.fromp.at[i], self.ps.at[i], self.pr.at[i], (p.w, 1 - p.x))
+
+    def start(self, i, col):
+        self.local(i, col).start()
+        self.core_copy(i, col).start()
+
+    def x_step(self, i, col):
+        self.local(i, col).wait()
+        self.core_copy(i, col).wait_recv()
+        for z in range(4):
+            self.own[i, z] = self.own[i, z] + self.fromc[i, z]
+        self.x_copy(i).start()
+
+    def y_step(self, i):
+        p = self.p
+        self.x_copy(i).wait_recv()
+        cols = self.lanes(p.x)
+        for y in range(2):
+            self.own[i, :, y, :, cols] = self.own[i, :, y, :, cols] + self.fromx[i, :, y]
+        self.y_copy(i).start()
+
+    def z_step(self, i):
+        p = self.p
+        self.y_copy(i).wait_recv()
+        self.own[i, :, p.y, :, self.mine()] = self.own[i, :, p.y, :, self.mine()] + self.fromy[i]
+        for k in (2, 1, 3):
+            self.z_copy(i, k).start()
+
+    def p_step(self, i):
+        p = self.p
+        total = self.own[i, p.z, p.y, :, self.mine()].astype(f32)
+        for k in (1, 2, 3):
+            self.z_arrival(i, k).wait_recv()
+            total += self.fromz[i, p.z_peer(k)].astype(f32)
+        self.done[i] = total.astype(bf16)
+        self.p_copy(i).start()
+
+    def finish(self, i):
+        p = self.p
+        self.p_copy(i).wait_recv()
+        a, b = self.done[i].astype(f32), self.fromp[i].astype(f32)
+        low, high = jnp.where(p.x == 0, a, b), jnp.where(p.x == 0, b, a)
+        both = low[:, LANES:] + high[:, :LANES]
+        return jnp.concatenate([low[:, :LANES], both, high[:, LANES:]], 1)
+
+    def sent(self, i, col):
+        self.core_copy(i, col).wait_send()
+        self.x_copy(i).wait_send()
+        self.y_copy(i).wait_send()
+        for k in (1, 2, 3):
+            self.z_copy(i, k).wait_send()
+        self.p_copy(i).wait_send()
+
+
+def reduce_scratch(pieces, rows):
+    dma = pltpu.SemaphoreType.DMA
+    v = lambda *s: pltpu.VMEM((pieces,) + s, bf16)
+    bufs = [v(4, 2, rows, PIECE), v(4, 2, rows, PIECE), v(4, 2, rows, LANES), v(4, rows, 2 * LANES), v(4, rows, 2 * LANES), v(rows, 2 * LANES), v(rows, 2 * LANES)]
+    return bufs + [dma((pieces,))] * 7 + [dma((pieces, 4))] * 2 + [dma((pieces,))] * 2
+
+
+def reduce_kernel(part, out, own, fromc, fromx, fromy, fromz, fromp, done, *sems):
+    place = Place()
+    total = part.shape[-1] // PIECE
+    place.greet()
+    r = Reduce(place, part, own, fromc, fromx, fromy, fromz, fromp, done, sems)
+    lax.fori_loop(0, min(AHEAD, total), lambda i, _: (r.start(i, i * PIECE), 0)[1], 0)
+
+    def turn(i, _):
+        def at(lag, step):
+            @pl.when((i >= lag) & (i < total + lag))
+            def _():
+                step(i - lag)
+
+        @pl.when(i + AHEAD < total)
+        def _():
+            r.start(i + AHEAD, (i + AHEAD) * PIECE)
+
+        at(0, lambda j: r.x_step(j, j * PIECE))
+        at(LAG, r.y_step)
+        at(2 * LAG, r.z_step)
+        at(3 * LAG, r.p_step)
+
+        def last(j):
+            out[j] = r.finish(j)
+
+        at(4 * LAG, last)
+        return 0
+
+    lax.fori_loop(0, total + 4 * LAG, turn, 0)
+    lax.fori_loop(0, total, lambda i, _: (r.sent(i, i * PIECE), 0)[1], 0)
+
+
+def reduce_all(part):
+    rows16, cols = part.shape
+    rows = rows16 // 16
+    total = cols // PIECE
+    assert cols == total * PIECE
+    out = pl.pallas_call(
+        reduce_kernel,
+        out_shape=jax.ShapeDtypeStruct((total, rows, PIECE), f32),
+        in_specs=[pl.BlockSpec(memory_space=pl.ANY)],
+        out_specs=pl.BlockSpec(memory_space=pltpu.VMEM),
+        scratch_shapes=reduce_scratch(total, rows),
+        compiler_params=pltpu.CompilerParams(collective_id=1, has_side_effects=True, vmem_limit_bytes=BIG),
+        name="reduce",
+    )(part.reshape(4, 2, 2, rows, cols))
+    return out
+
+
 def pack_columns(attention, dense, vectors):
     count = vectors.shape[0]
     vector_cols = jnp.pad(vectors.T, ((0, 0), (0, 128 - count)))
@@ -299,8 +619,16 @@
     x = hidden_in.reshape(-1, width)
     e = cotangent.reshape(-1, width)
     first, second = pack_columns(attention_weights, dense_weights, vector_params)
-    first_full = lax.all_gather(first.astype(bf16), "wide", axis=0, tiled=True)
-    second_full = lax.all_gather(second.astype(bf16), "wide", axis=0, tiled=True)
+    ours = lax.axis_size("wide") == 16 and lax.axis_size("narrow") == 2
+    if ours:
+        cols = first.shape[1] - LANES
+        shard = jnp.concatenate([first[:, :cols], second, first[:, cols:]], 1).astype(bf16)
+        full = gather_all(shard)
+        first_full = jnp.concatenate([full[:, :cols], full[:, -LANES:]], 1)
+        second_full = full[:, cols:-LANES]
+    else:
+        first_full = lax.all_gather(first.astype(bf16), "wide", axis=0, tiled=True)
+        second_full = lax.all_gather(second.astype(bf16), "wide", axis=0, tiled=True)
     vec = first_full[:, 3 * width : 3 * width + vector_rows].astype(f32).T
     bias_qkv = jnp.concatenate([vec[4:5], jnp.zeros((1, width), f32), vec[5:6]], 1)
     w_qkv = first_full[:, : 3 * width]
@@ -310,20 +638,24 @@
         x, c, e, wo, win, wd, vec, vec[8:].reshape(1, ff)
     )
     grad_second = jnp.concatenate([wgrad(c, da), wgrad(y1, du), wgrad(dz, g)], 1)
-    share_second = lax.psum_scatter(grad_second, "wide", scatter_dimension=0, tiled=True)
     dqkv, gin, dw, db = attn_bwd(segment_ids, qkv, dc, lse, delta, dh1, w_qkv, x)
     dvec = jnp.concatenate(
         [dvec[:4], db[:, :width], db[:, 2 * width :], dvec[6:8], dbin.reshape(-1, width)], 0
     )
-    grad_first = jnp.concatenate(
-        [dw, jnp.pad(dvec.T, ((0, 0), (0, 128 - vector_rows))).astype(bf16)], 1
-    )
-    share_first = lax.psum_scatter(grad_first, "wide", scatter_dimension=0, tiled=True)
     replicas = lax.axis_size("narrow")
     tokens_all = row_count * length * lax.axis_size("wide") * replicas
     grad_scale = math.sqrt(tokens_all) / replicas
-    t1 = lax.psum(share_first, "narrow").astype(f32) / replicas
-    t2 = lax.psum(share_second, "narrow").astype(f32) / replicas
+    if ours:
+        vec_cols = jnp.pad(dvec.T, ((0, 0), (0, PIECE - vector_rows))).astype(bf16)
+        share = reduce_all(jnp.concatenate([dw, vec_cols, grad_second], 1))
+        share = jnp.swapaxes(share, 0, 1).reshape(share.shape[1], -1) / replicas
+        t1, t2 = share[:, : 3 * width + PIECE], share[:, 3 * width + PIECE :]
+    else:
+        vec_cols = jnp.pad(dvec.T, ((0, 0), (0, LANES - vector_rows))).astype(bf16)
+        share_first = lax.psum_scatter(jnp.concatenate([dw, vec_cols], 1), "wide", scatter_dimension=0, tiled=True)
+        share_second = lax.psum_scatter(grad_second, "wide", scatter_dimension=0, tiled=True)
+        t1 = lax.psum(share_first, "narrow").astype(f32) / replicas
+        t2 = lax.psum(share_second, "narrow").astype(f32) / replicas
     cut = lambda t, j: t[:, j * width : (j + 1) * width]
     attention_grad = jnp.stack([cut(t1, 0), cut(t1, 1), cut(t1, 2), cut(t2, 0)])
     dense_grad = jnp.stack([t2[:, width : width + ff], t2[:, width + ff :]])

time: 505 us -> 344 us (0.68)
  waiting for transfers between devices: 307 us -> 0 us
  Pallas kernels: 130 us -> 299 us
  other arithmetic: 26.5 us -> 11.2 us
  between operations: 14.1 us -> 0.92 us
  local copies, waits for them, and re-layouts: 25.9 us -> 31.5 us
    pallas_call x0 -> x2, Pallas kernels: none -> 170 us  [the longest x1 85.1 us: gather_all(): pl.pallas_call(gather_kernel, out_shape=jax.ShapeDtypeStruct((4, 2, 2, ro...]
    reduce_scatter x2 -> x0, waiting for transfers between devices: 159 us -> none  [the longest x1 123 us: body(): lax.psum_scatter(grad_second, 'wide', scatter_dimension=0, tiled=True)]
    all_gather x2 -> x0, waiting for transfers between devices: 111 us -> none  [the longest x1 61.5 us: body(): lax.all_gather(second.astype(bf16), 'wide', axis=0, tiled=True)]
    psum x1 -> x0, waiting for transfers between devices: 36.9 us -> none  [body(): t2 = lax.psum(share_second, 'narrow').astype(f32) / replicas]
    concatenate x4 -> x0, other arithmetic: 14.7 us -> none  [the longest x1 8.94 us: body(): jnp.concatenate([wgrad(c, da), wgrad(y1, du), wgrad(dz, g)], 1)]
    unnamed x45 -> x46, local copies, waits for them, and re-layouts: 7.81 us -> 10.7 us
  transfers between devices with their start and end apart: 5 -> 0, of which waited for: 5 -> 0; matrix products, arithmetic and copies ran while one was open for 4% -> 0% of each run, Pallas kernels for 9% -> 0%
where the time goes in v2:
time: 344 us; the launch traced here: 343 us
  Pallas kernels  299 us (87%)
  local copies, waits for them, and re-layouts  31.5 us (9%)
  other arithmetic  11.2 us (3%)
    pallas_call x1, Pallas kernels, gather_all(): pl.pallas_call(gather_kernel, out_shape=jax.ShapeDtypeStruct((4, 2, 2, ro...  85.1 us
    pallas_call x1, Pallas kernels, reduce_all(): pl.pallas_call(reduce_kernel, out_shape=jax.ShapeDtypeStruct((total, rows...  85 us
    pallas_call x1, Pallas kernels, attn_bwd(): pl.pallas_call(functools.partial(bwd_kernel, blk), grid=(rows,), out_shap...  46.4 us
    pallas_call x1, Pallas kernels, mid(): pl.pallas_call(functools.partial(mid_kernel, chunk), grid=(n // blk,), ou...  39 us
    pallas_call x3, Pallas kernels, wgrad(): pl.pallas_call(wgrad_kernel, grid=(k // blk,), out_shape=jax.ShapeDtypeSt...  22.9 us
    pallas_call x1, Pallas kernels, attn_fwd(): pl.pallas_call(functools.partial(fwd_kernel, blk), grid=(rows,), out_shap...  20.9 us
    unnamed x46, local copies, waits for them, and re-layouts  10.7 us
    slice x1, local copies, waits for them, and re-layouts, body(): second_full[:, width + ff:]  8.3 us

profile of v2, /device:TPU:0, one launch (start us, length us, event | category | flops | bytes accessed | tf_op | source)
XLA Modules:
  0.0 343.0 jit_solution(2654000129595991435)
XLA Ops:
  0.6 1.3 reshape.55.seg_ref
  1.9 0.7 convert.50
  2.7 1.1 convert.48
  3.8 1.3 convert.49
  5.3 0.9 copy-done.7
  6.2 85.1 %gather.1 = bf16[4,2,2,48,9344]{4,3,2,1,0:T(8,128)(2,1)} custom-call(bf16[48,9344]{1,0:T(8,128)(2,1)} %copy-done.7), custom_call_target="tpu_custom_call" | custom-call | tf_op jit(solution)/shard_map/gather/pallas_call | solution.py:426
  91.3 1.0 convert_bitcast_fusion
  92.3 0.8 copy.75.v_ref
  93.4 0.6 copy.81
  94.6 0.6 fusion.6.b_ref
  95.2 2.4 slice.135.wo_ref
  97.5 4.0 %slice.131.w_ref = bf16[768,2304]{1,0:T(8,128)(2,1)} slice(bf16[768,9344]{1,0:T(8,128)(2,1)} %bitcast.64), slice={[0:768], [0:2304]} | slice | bytes 7077888 | tf_op jit(solution)/shard_map/slice | solution.py:627
  101.5 8.3 %fusion.10 = (bf16[768,3072]{1,0:T(8,128)(2,1)}, bf16[768,3072]{1,0:T(8,128)(2,1)}) fusion(bf16[768,9344]{1,0:T(8,128)(2,1)} %bitcast.65), kind=kLoop, calls=%fused_computation.42 | loop fusion | bytes 18874368 | tf_op jit(solution)/shard_map/slice | solution.py:635
  109.8 20.9 %attn_fwd.1 = (bf16[1024,2304]{1,0:T(8,128)(2,1)}, bf16[1024,768]{1,0:T(8,128)(2,1)}, f32[2,16,512]{2,1,0:T(8,128)}) custom-call(bf16[1024,768]{1,0:T(8,128)(2,1)} %bitcast.68, s32[2,1,512]{2,1,0:T(1,128)} %reshape.55.seg_ref, bf16[768,2304]{1,0:T(8,128)(2,1)} %slice.131.w_ref, f32[1,2304]{1,0:T(1,128)} %fusion.6.b_ref), custom_call_target="tpu_custom_call" | custom-call | tf_op jit(solution)/shard_map/attn_fwd/pallas_call | solution.py:78
  130.7 39.0 %middle.1 = (bf16[1024,768]{1,0:T(8,128)(2,1)}, bf16[1024,768]{1,0:T(8,128)(2,1)}, bf16[1024,3072]{1,0:T(8,128)(2,1)}, bf16[1024,768]{1,0:T(8,128)(2,1)}, bf16[1...) custom-call(bf16[1024,768]{1,0:T(8,128)(2,1)} %bitcast.69, ...), custom_call_target="tpu_custom_call" | custom-call | tf_op jit(solution)/shard_map/middle/pallas_call | solution.py:243
  169.8 4.3 %wgrad.3 = bf16[768,768]{1,0:T(8,128)(2,1)} custom-call(bf16[1024,768]{1,0:T(8,128)(2,1)} %get-tuple-element.28.c_ref.a_ref, bf16[1024,768]{1,0:T(8,128)(2,1)} %get-tuple-element.40.b_ref), custom_call_target="tpu_custom_call" | custom-call | tf_op jit(solution)/shard_map/wgrad/pallas_call | solution.py:261
  174.2 46.4 %attn_bwd.1 = (bf16[1024,2304]{1,0:T(8,128)(2,1)}, bf16[1024,768]{1,0:T(8,128)(2,1)}, bf16[768,2304]{1,0:T(8,128)(2,1)}, f32[1,2304]{1,0:T(1,128)}) custom-call(s32[2,1,512]{2,1,0:T(1,128)} %reshape.55.seg_ref, bf16[1024,2304]{1,0:T(8,128)(2,1)} %get-tuple-element.30.qkv_ref, bf16[1024,768]{1,0:T(8,128)(2,1)} %get-tuple-element.31.dc_ref, ...), custom_call_target="tpu_custom_call" | custom-call | tf_op jit(solution)/shard_map/attn_bwd/pallas_call | solution.py:156
  220.7 0.7 convert.52
  221.6 9.2 %wgrad.4 = bf16[768,3072]{1,0:T(8,128)(2,1)} custom-call(bf16[1024,768]{1,0:T(8,128)(2,1)} %get-tuple-element.41.a_ref, bf16[1024,3072]{1,0:T(8,128)(2,1)} %get-tuple-element.42.b_ref), custom_call_target="tpu_custom_call" | custom-call | tf_op jit(solution)/shard_map/wgrad/pallas_call | solution.py:261
  230.9 9.4 %wgrad.5 = bf16[768,3072]{1,0:T(8,128)(2,1)} custom-call(bf16[1024,768]{1,0:T(8,128)(2,1)} %get-tuple-element.43.a_ref, bf16[1024,3072]{1,0:T(8,128)(2,1)} %get-tuple-element.44.b_ref), custom_call_target="tpu_custom_call" | custom-call | tf_op jit(solution)/shard_map/wgrad/pallas_call | solution.py:261
  240.3 2.2 constant_dynamic-update-slice_fusion.4
  242.4 1.0 pad_dynamic-update-slice_fusion
  243.4 1.1 constant_dynamic-update-slice_fusion.3
  244.6 2.5 constant_dynamic-update-slice_fusion.2
  247.1 2.6 constant_dynamic-update-slice_fusion.1
  249.7 85.0 %reduce.3 = f32[25,48,384]{2,1,0:T(8,128)} custom-call(bf16[4,2,2,48,9600]{4,3,2,1,0:T(8,128)(2,1)} %bitcast.14.part), custom_call_target="tpu_custom_call" | custom-call | tf_op jit(solution)/shard_map/reduce/pallas_call | solution.py:575
  334.7 1.6 multiply_bitcast_fusion
  336.6 0.4 copy-done.10
  337.1 0.6 add_multiply_fusion.2
  338.2 1.3 add_multiply_fusion.1
  340.0 0.5 copy-done.5
  340.9 2.1 add_multiply_fusion
  (60 shorter events, 3.0 us)
Async XLA Ops:
  5.3 0.9 copy-start.7
  169.8 4.4 %copy-start.12 = (f32[1,3072]{1,0:T(1,128)S(1)}, f32[1,3072]{1,0:T(1,128)}, u32[]{:S(2)}) copy-start(f32[1,3072]{1,0:T(1,128)} %get-tuple-element.39) | copy-start | bytes 36868
  169.8 4.4 %copy-start.11 = (f32[8,768]{1,0:T(8,128)S(1)}, f32[8,768]{1,0:T(8,128)}, u32[]{:S(2)}) copy-start(f32[8,768]{1,0:T(8,128)} %get-tuple-element.37) | copy-start | bytes 73732
  230.9 9.4 %copy-start.3 = (bf16[768,2304]{1,0:T(8,128)(2,1)S(1)}, bf16[768,2304]{1,0:T(8,128)(2,1)}, u32[]{:S(2)}) copy-start(bf16[768,2304]{1,0:T(8,128)(2,1)} %get-tuple-element.36) | copy-start | bytes 10616836
  240.3 3.2 copy-start.2
  240.3 4.3 %copy-start = (bf16[768,3072]{1,0:T(8,128)(2,1)S(1)}, bf16[768,3072]{1,0:T(8,128)(2,1)}, u32[]{:S(2)}) copy-start(bf16[768,3072]{1,0:T(8,128)(2,1)} %wgrad.4) | copy-start | bytes 14155780
  243.4 3.7 %slice-start = ((s8[4718592]{0:T(1024)(128)(4,1)}), s8[4194304]{0:T(1024)(128)(4,1)S(1)}, s32[]{:S(2)}) async-start(s8[4718592]{0:T(1024)(128)(4,1)} %bitcast.66), calls=%async_computation | async-start | bytes 8388608
  244.6 2.5 slice-start.1
  336.3 0.7 copy-start.10
  336.4 0.7 copy-start.13
  336.4 0.7 copy-start.14
  336.5 1.3 copy-start.4
  336.5 1.3 copy-start.8
  337.1 1.2 copy-start.9
  338.2 1.7 copy-start.1
  338.2 2.3 copy-start.5
  338.2 2.6 copy-start.6

commit v3 on v1

--- a/solution.py
+++ b/solution.py
@@ -264,6 +264,796 @@
         compiler_params=pltpu.CompilerParams(vmem_limit_bytes=BIG), name="wgrad")(a, b)
 
 
+LANES = 128
+PIECE = 3 * LANES
+LAG = 2
+AHEAD = 3
+MESH = pl.DeviceIdType.MESH
+
+
+class Place:
+    def __init__(self):
+        self.w = lax.axis_index("wide")
+        self.x = lax.axis_index("narrow")
+        self.core = lax.rem(self.w, 2)
+        self.y = lax.rem(self.w // 2, 2)
+        self.b = lax.rem(self.w // 4, 2)
+        self.a = self.w // 8
+
+    def over(self, name):
+        if name == "x":
+            return (self.w, 1 - self.x)
+        step = {"a": 8, "b": 4, "y": 2, "core": 1}[name]
+        return (self.w + step * (1 - 2 * getattr(self, name)), self.x)
+
+    def greet(self):
+        barrier = pltpu.get_barrier_semaphore()
+        names = ("a", "b", "y", "x", "core")
+        for name in names:
+            pl.semaphore_signal(barrier, inc=1, device_id=self.over(name), device_id_type=MESH)
+        pl.semaphore_wait(barrier, len(names))
+
+
+def remote(src, dst, send, recv, device):
+    return pltpu.make_async_remote_copy(src_ref=src, dst_ref=dst, send_sem=send, recv_sem=recv, device_id=device, device_id_type=MESH)
+
+
+def when(condition, step):
+    @pl.when(condition)
+    def _():
+        step()
+
+
+def loop(count, step):
+    lax.fori_loop(0, count, lambda i, _: (step(i), 0)[1], 0)
+
+
+class Gather:
+    def __init__(self, place, shard, full, sems, pieces):
+        self.p, self.shard, self.full, self.pieces = place, shard, full, pieces
+        self.sems = {name: (sems[2 * k], sems[2 * k + 1]) for k, name in enumerate(("a", "b", "y", "x", "core"))}
+        self.kept = sems[10]
+        self.own = pl.ds(place.x, 2)
+
+    def mine(self, i, a):
+        return self.full.at[i, self.own, a, self.p.b, self.p.y, self.p.core]
+
+    def keep(self, i):
+        return pltpu.make_async_copy(self.shard.at[i, self.own], self.mine(i, self.p.a), self.kept.at[i])
+
+    def copy(self, name, i, incoming=False):
+        p, f = self.p, self.full
+        at = {n: (1 - getattr(p, n) if incoming and n == name else getattr(p, n)) for n in ("a", "b", "y", "x", "core")}
+        every = slice(None)
+        if name == "a":
+            dst = self.mine(i, at["a"])
+            src = self.shard.at[i, self.own]
+        else:
+            if name == "b":
+                dst = f.at[i, self.own, :, at["b"], p.y, p.core]
+            elif name == "y":
+                dst = f.at[i, self.own, :, :, at["y"], p.core]
+            elif name == "x":
+                dst = f.at[i, 2 * at["x"], :, :, :, p.core]
+            else:
+                dst = f.at[i, :, :, :, :, at["core"]]
+            src = dst
+        send, recv = self.sems[name]
+        return remote(src, dst, send.at[i], recv.at[i], p.over(name))
+
+    def start(self, i):
+        self.keep(i).start()
+        self.copy("a", i).start()
+
+    def b_step(self, i):
+        self.keep(i).wait()
+        self.copy("a", i, True).wait_recv()
+        self.copy("b", i).start()
+
+    def y_step(self, i):
+        self.copy("b", i, True).wait_recv()
+        self.copy("y", i).start()
+
+    def x_step(self, i):
+        self.copy("y", i, True).wait_recv()
+        self.copy("x", i).start()
+
+    def core_step(self, i):
+        self.copy("x", i, True).wait_recv()
+        self.copy("core", i).start()
+
+    def arrive(self, i):
+        self.copy("core", i, True).wait_recv()
+
+    def turn(self, t):
+        for k in range(2):
+            ahead = AHEAD + 2 * t + k
+            when(ahead < self.pieces, lambda ahead=ahead: self.start(ahead))
+        for lag, step in enumerate((self.b_step, self.y_step, self.x_step, self.core_step)):
+            lag = lag * LAG
+            when((t >= lag) & (t < self.pieces + lag), lambda lag=lag, step=step: step(t - lag))
+
+    def sent(self, i):
+        for name in ("a", "b", "y", "x", "core"):
+            self.copy(name, i).wait_send()
+
+
+class GatherVector:
+    def __init__(self, place, shard, full, sems):
+        self.p, self.shard, self.full = place, shard, full
+        self.sems = {name: (sems[2 * k], sems[2 * k + 1]) for k, name in enumerate(("a", "b", "y", "core"))}
+        self.kept = sems[8]
+
+    def keep(self):
+        p = self.p
+        return pltpu.make_async_copy(self.shard, self.full.at[p.a, p.b, p.y, p.core], self.kept)
+
+    def copy(self, name, incoming=False):
+        p = self.p
+        at = {n: (1 - getattr(p, n) if incoming and n == name else getattr(p, n)) for n in ("a", "b", "y", "core")}
+        every = slice(None)
+        first = ("a", "b", "y", "core").index(name)
+        dst = self.full.at[tuple(at[n] if n == name or n == "core" or k > first else every for k, n in enumerate(("a", "b", "y", "core")))]
+        src = self.shard if name == "a" else dst
+        send, recv = self.sems[name]
+        return remote(src, dst, send, recv, p.over(name))
+
+    def start(self):
+        self.keep().start()
+        self.copy("a").start()
+
+    def step(self, name, then):
+        if name == "a":
+            self.keep().wait()
+        self.copy(name, True).wait_recv()
+        self.copy(then).start()
+
+    def arrive(self):
+        self.copy("core", True).wait_recv()
+
+    def sent(self):
+        for name in ("a", "b", "y", "core"):
+            self.copy(name).wait_send()
+
+
+def tile(ref, i, t):
+    rows = 16 * ref.shape[-2]
+    return ref[i, t].reshape(rows, LANES)
+
+
+def columns(ref, *pieces):
+    return jnp.concatenate([tile(ref, i, t) for i in pieces for t in range(3)], 1)
+
+
+def doc_bias(seg_row, bias_ref, r):
+    segf = seg_row.astype(f32)
+    seq = segf.shape[1]
+    rep = jnp.broadcast_to(segf, (LANES, seq)).T
+    for j in range(seq // LANES):
+        sl = slice(j * LANES, (j + 1) * LANES)
+        bias_ref[r, :, sl] = jnp.where(rep == segf[:, sl], 0.0, NEG)
+
+
+def stage_kernel(heads, x_hbm, seg_ref, e_hbm, aw_hbm, dw_hbm, vp_ref,
+                 qkv_o, c_o, lse_o, wq_o, out_o, y1_o, g_o, dz_o, du_o, da_o, dc_o, dh1_o, delta_o, dv_o, dbin_o,
+                 full, vfull, shard, vshard, square, xb, eb, cb, n1b, y1b, acc, gp, gb, dzb, bias, lsea, vrow, binr, r1b,
+                 in_sem, out_sem, *sems):
+    place = Place()
+    rows, _, seq = seg_ref.shape
+    tokens, width = x_hbm.shape
+    pairs = heads // 2
+    pieces = shard.shape[0]
+    chunks = gb.shape[0]
+    own_rows = aw_hbm.shape[1]
+    blk = 256
+    g = Gather(place, shard, full, sems[:11], pieces)
+    gv = GatherVector(place, vshard, vfull, sems[11:])
+
+    loads = [pltpu.make_async_copy(aw_hbm.at[k], gp.at[0, pl.ds(k * own_rows, own_rows)], in_sem.at[k]) for k in range(4)]
+    for k in range(2):
+        for j in range(chunks):
+            loads.append(pltpu.make_async_copy(
+                dw_hbm.at[k, :, pl.ds(j * width, width)], gp.at[1 + k, pl.ds(j * own_rows, own_rows)], in_sem.at[4 + k * chunks + j]))
+    n = len(loads)
+    x_load = pltpu.make_async_copy(x_hbm, xb, in_sem.at[n])
+    e_load = pltpu.make_async_copy(e_hbm, eb, in_sem.at[n + 1])
+    for c in loads:
+        c.start()
+    x_load.start()
+    e_load.start()
+    square[...] = jnp.zeros_like(square)
+    lsea[...] = jnp.zeros_like(lsea)
+    square[: vp_ref.shape[0], :own_rows] = vp_ref[...]
+    vshard[...] = square[...].T[:own_rows].astype(bf16)
+
+    def own_tile(k, j, t):
+        return gp[k, j * own_rows : (j + 1) * own_rows, t * LANES : (t + 1) * LANES].astype(bf16)
+
+    for c in loads[:3]:
+        c.wait()
+    for p in range(pairs):
+        for t in range(3):
+            shard[p, t] = own_tile(0, t, p)
+    place.greet()
+    gv.start()
+    for i in range(AHEAD):
+        g.start(i)
+    for c in loads[3:]:
+        c.wait()
+    for t in range(6):
+        shard[pairs + t // 3, t % 3] = own_tile(0, 3, t)
+        for j in range(chunks):
+            for k in range(2):
+                shard[pairs + 2 + 4 * j + 2 * k + t // 3, t % 3] = own_tile(1 + k, j, t)
+    for r in range(rows):
+        doc_bias(seg_ref[r], bias, r)
+    gv.step("a", "b")
+    fill = 3 * LAG + 1
+    for t in range(fill):
+        g.turn(t)
+        if t == LAG // 2:
+            gv.step("b", "y")
+        if t == 2 * LAG:
+            gv.step("y", "core")
+    gv.arrive()
+    vec = vfull[...].reshape(16 * own_rows, LANES).astype(f32).T
+    vrow[...] = vec[: vrow.shape[0]]
+    for j in range(chunks):
+        binr[j] = vrow[8 + j : 9 + j, :]
+    x_load.wait()
+
+    first = lax.broadcasted_iota(jnp.int32, (LANES, LANES), 1) < HD
+    lane = lax.broadcasted_iota(jnp.int32, (LANES, LANES), 1)
+    ones = jnp.ones((seq, LANES), bf16)
+
+    def qkv_at(p):
+        return gb.at[p // 2, :, pl.ds(pl.multiple_of(lax.rem(p, 2) * PIECE, LANES), PIECE)]
+
+    def qkv_out(p):
+        return pltpu.make_async_copy(qkv_at(p), qkv_o.at[p], out_sem.at[p])
+
+    def pair(p):
+        g.arrive(p)
+        head = pl.ds(pl.multiple_of(p * LANES, LANES), LANES)
+        w = columns(full, p)
+        b = jnp.concatenate([vrow[4:5, head], jnp.zeros((1, LANES), f32), vrow[5:6, head]], 1)
+        col = pl.multiple_of(lax.rem(p, 2) * PIECE, LANES)
+        gb[p // 2, :, pl.ds(col, PIECE)] = (dot(xb[...], w) + b).astype(bf16)
+        qkv_out(p).start()
+
+        def row(r):
+            tok = pl.ds(pl.multiple_of(r * seq, seq), seq)
+            q2 = gb[p // 2, tok, pl.ds(col, LANES)]
+            k2 = gb[p // 2, tok, pl.ds(col + LANES, LANES)]
+            v2 = jnp.concatenate([gb[p // 2, tok, pl.ds(col + 2 * LANES, LANES)], ones], 1)
+            for c in range(seq // LANES):
+                lo, hi = key_range(c, seq, LANES)
+                cut = slice(c * LANES, (c + 1) * LANES)
+                outs = []
+                la = lsea[r, cut, :]
+                for h in range(2):
+                    qm = jnp.where(first if h == 0 else ~first, q2[cut], jnp.zeros_like(q2[cut]))
+                    s = dot_nt(qm, k2[lo:hi]) + bias[r, cut, lo:hi]
+                    m = jnp.max(s, 1, keepdims=True)
+                    o = dot(jnp.exp2((s - m) * SCALE2).astype(bf16), v2[lo:hi])
+                    l = o[:, LANES:]
+                    outs.append(o[:, :LANES] / l)
+                    la = jnp.where(lane == 2 * p + h, m * SCALE2 + jnp.log(l) * LOG2E, la)
+                lsea[r, cut, :] = la
+                cb[pl.ds(pl.multiple_of(r * seq + c * LANES, LANES), LANES), head] = jnp.where(first, outs[0], outs[1]).astype(bf16)
+            g.turn(fill + 2 * p + r)
+
+        loop(rows, row)
+
+    loop(pairs, pair)
+    done = fill + 2 * pairs
+    for r in range(rows):
+        lse_o[r] = lsea[r].T[: lse_o.shape[1]]
+    c_out = pltpu.make_async_copy(cb, c_o, out_sem.at[pairs])
+    c_out.start()
+    wq_out = pltpu.make_async_copy(full.at[pl.ds(0, pairs)], wq_o, out_sem.at[pairs + 1])
+    wq_out.start()
+    g1, s1, g2, s2, bo, bd = (vrow[j : j + 1, :] for j in (0, 1, 2, 3, 6, 7))
+
+    def block(i):
+        return pl.ds(pl.multiple_of(i * blk, blk), blk)
+
+    g.arrive(pairs)
+    g.arrive(pairs + 1)
+
+    def norm_one(i):
+        at = block(i)
+        h1 = xb[at, :].astype(f32) + (dot(cb[at, :], columns(full, pairs, pairs + 1)) + bo)
+        cen = h1 - jnp.mean(h1, 1, keepdims=True)
+        r1 = lax.rsqrt(jnp.mean(cen * cen, 1, keepdims=True) + EPS)
+        n1 = cen * r1
+        y1 = n1 * g1 + s1
+        n1b[at, :] = n1
+        r1b[at, :] = r1
+        y1b[at, :] = y1.astype(bf16)
+        acc[at, :] = y1 + bd
+        when(lax.rem(i, 2) == 1, lambda: g.turn(done + i // 2))
+
+    loop(tokens // blk, norm_one)
+    done += 2
+    y1_out = pltpu.make_async_copy(y1b, y1_o, out_sem.at[pairs + 2])
+    y1_out.start()
+    loop(pairs, lambda p: qkv_out(p).wait())
+
+    def up(j):
+        return columns(full, pairs + 2 + 4 * j, pairs + 3 + 4 * j)
+
+    def down(j):
+        return columns(full, pairs + 4 + 4 * j, pairs + 5 + 4 * j)
+
+    def g_out(j):
+        return pltpu.make_async_copy(gb.at[j], g_o.at[j], out_sem.at[pairs + 3 + j])
+
+    def ff_chunk(j):
+        for t in range(4):
+            g.arrive(pairs + 2 + 4 * j + t)
+
+        def ff_block(i):
+            at = block(i)
+            u = dot(y1b[at, :], up(j)) + binr[j]
+            act, slope = gelu_parts(u)
+            gl = act.astype(bf16)
+            gb[j, at, :] = gl
+            gp[j, at, :] = slope
+            acc[at, :] += dot_nt(gl, down(j))
+            when(i < 3, lambda: g.turn(done + 3 * j + i))
+
+        loop(tokens // blk, ff_block)
+        g_out(j).start()
+
+    loop(chunks, ff_chunk)
+    e_load.wait()
+    dv_o[...] = jnp.zeros_like(dv_o)
+    dbin_o[...] = jnp.zeros_like(dbin_o)
+
+    def colsum(t):
+        return jnp.sum(t, 0, keepdims=True)
+
+    def norm_two(i):
+        at = block(i)
+        h2 = acc[at, :]
+        cen = h2 - jnp.mean(h2, 1, keepdims=True)
+        r2 = lax.rsqrt(jnp.mean(cen * cen, 1, keepdims=True) + EPS)
+        n2 = cen * r2
+        xb[at, :] = (n2 * g2 + s2).astype(bf16)
+        e = eb[at, :].astype(f32)
+        eg = e * g2
+        dh2 = r2 * (eg - jnp.mean(eg, 1, keepdims=True) - n2 * jnp.mean(eg * n2, 1, keepdims=True))
+        dz = dh2.astype(bf16)
+        dzb[at, :] = dz
+        acc[at, :] = dh2
+        dv_o[2:3, :] += colsum(e * n2)
+        dv_o[3:4, :] += colsum(e)
+        dv_o[7:8, :] += colsum(dz.astype(f32))
+
+    loop(tokens // blk, norm_two)
+    out_out = pltpu.make_async_copy(xb, out_o, out_sem.at[pairs + 3 + chunks])
+    dz_out = pltpu.make_async_copy(dzb, dz_o, out_sem.at[pairs + 4 + chunks])
+    out_out.start()
+    dz_out.start()
+
+    def du_out(j):
+        return pltpu.make_async_copy(gb.at[j], du_o.at[j], out_sem.at[pairs + 5 + chunks + j])
+
+    def back_chunk(j):
+        g_out(j).wait()
+
+        def back_block(i):
+            at = block(i)
+            du = (dot(dzb[at, :], down(j)) * gp[j, at, :]).astype(bf16)
+            gb[j, at, :] = du
+            dbin_o[j] += colsum(du.astype(f32))
+            acc[at, :] += dot_nt(du, up(j))
+
+        loop(tokens // blk, back_block)
+        du_out(j).start()
+
+    loop(chunks, back_chunk)
+    c_out.wait()
+    y1_out.wait()
+    sel_shape = (delta_o.shape[0], width)
+    sel = jnp.where(lax.broadcasted_iota(jnp.int32, sel_shape, 0) == lax.broadcasted_iota(jnp.int32, sel_shape, 1) // HD, 1.0, 0.0).astype(bf16)
+
+    def norm_one_back(i):
+        at = block(i)
+        dy1 = acc[at, :]
+        n1 = n1b[at, :]
+        dn = dy1 * g1
+        dh1 = r1b[at, :] * (dn - jnp.mean(dn, 1, keepdims=True) - n1 * jnp.mean(dn * n1, 1, keepdims=True))
+        acc[at, :] = dh1
+        da = dh1.astype(bf16)
+        eb[at, :] = da
+        dc = dot_nt(da, columns(full, pairs, pairs + 1)).astype(bf16)
+        y1b[at, :] = dc
+        prod = dc.astype(f32) * cb[at, :].astype(f32)
+        hi = prod.astype(bf16)
+        lo = (prod - hi.astype(f32)).astype(bf16)
+        delta_o[:, at] = dot_nt(sel, hi) + dot_nt(sel, lo)
+        dv_o[0:1, :] += colsum(dy1 * n1)
+        dv_o[1:2, :] += colsum(dy1)
+        dv_o[6:7, :] += colsum(da.astype(f32))
+
+    loop(tokens // blk, norm_one_back)
+    base = pairs + 5 + 2 * chunks
+    last = [pltpu.make_async_copy(s, d, out_sem.at[base + k]) for k, (s, d) in enumerate(((acc, dh1_o), (eb, da_o), (y1b, dc_o)))]
+    for c in last:
+        c.start()
+    gv.sent()
+    loop(pieces, g.sent)
+    wq_out.wait()
+    out_out.wait()
+    dz_out.wait()
+    loop(chunks, lambda j: du_out(j).wait())
+    for c in last:
+        c.wait()
+
+
+def stage(x, seg, e, aw, dw, vp):
+    rows, seq = seg.shape
+    tokens, width = x.shape
+    own_rows, ff = dw.shape[1:]
+    heads, chunks = width // HD, ff // width
+    pairs = heads // 2
+    pieces = pairs + 2 + 4 * chunks
+    sh = jax.ShapeDtypeStruct
+    dma = pltpu.SemaphoreType.DMA
+    v = pltpu.VMEM
+    hbm = pl.BlockSpec(memory_space=pl.ANY)
+    vmem = pl.BlockSpec(memory_space=pltpu.VMEM)
+    tok = sh((tokens, width), bf16)
+    wide = sh((chunks, tokens, width), bf16)
+    block = (2, 2, 2, 2, own_rows, LANES)
+    scratch = [
+        v((pieces, 3) + block, bf16), v(block, bf16), v((pieces, 3, own_rows, LANES), bf16), v((own_rows, LANES), bf16),
+        v((LANES, LANES), f32), v((tokens, width), bf16), v((tokens, width), bf16), v((tokens, width), bf16),
+        v((tokens, width), f32), v((tokens, width), bf16), v((tokens, width), f32), v((chunks, tokens, width), f32),
+        v((chunks, tokens, width), bf16), v((tokens, width), bf16), v((rows, seq, seq), f32), v((rows, seq, LANES), f32),
+        v((16, width), f32), v((chunks, 1, width), f32), v((tokens, 1), f32),
+        dma((6 + 2 * chunks,)), dma((pairs + 8 + 2 * chunks,)),
+    ] + [dma((pieces,))] * 11 + [dma(())] * 9
+    return pl.pallas_call(
+        functools.partial(stage_kernel, heads),
+        out_shape=(sh((pairs, tokens, PIECE), bf16), tok, sh((rows, 16, seq), f32), sh((pairs, 3) + block, bf16), tok, tok, wide,
+                   tok, wide, tok, tok, sh((tokens, width), f32), sh((16, tokens), f32), sh((8, width), f32), sh((chunks, 1, width), f32)),
+        in_specs=[hbm, vmem, hbm, hbm, hbm, vmem],
+        out_specs=(hbm, hbm, vmem, hbm, hbm, hbm, hbm, hbm, hbm, hbm, hbm, hbm, vmem, vmem, vmem),
+        scratch_shapes=scratch,
+        compiler_params=pltpu.CompilerParams(collective_id=0, has_side_effects=True, vmem_limit_bytes=BIG),
+        name="stage",
+    )(x, seg.reshape(rows, 1, seq), e, aw, dw, vp)
+
+
+class Reduce:
+    names = ("core", "x", "y", "b", "a", "p")
+
+    def __init__(self, place, part, froms, done, sems, pieces):
+        self.p, self.part, self.done, self.pieces = place, part, done, pieces
+        self.froms = dict(zip(self.names, froms))
+        self.sems = {name: (sems[2 * k], sems[2 * k + 1]) for k, name in enumerate(self.names)}
+        self.own = pl.ds(place.x, 2)
+
+    def copy(self, name, i):
+        p, f = self.p, self.part
+        if name == "core":
+            src = f.at[i, :, :, :, :, 1 - p.core]
+        elif name == "x":
+            src = f.at[i, 2 * (1 - p.x), :, :, :, p.core]
+        elif name == "y":
+            src = f.at[i, self.own, :, :, 1 - p.y, p.core]
+        elif name == "b":
+            src = f.at[i, self.own, :, 1 - p.b, p.y, p.core]
+        elif name == "a":
+            src = f.at[i, self.own, 1 - p.a, p.b, p.y, p.core]
+        else:
+            src = self.done.at[i]
+        send, recv = self.sems[name]
+        return remote(src, self.froms[name].at[i], send.at[i], recv.at[i], p.over("x" if name == "p" else name))
+
+    def start(self, i):
+        self.copy("core", i).start()
+
+    def x_step(self, i):
+        p, f = self.p, self.part
+        self.copy("core", i).wait_recv()
+        for t in range(3):
+            f[i, t, :, :, :, p.core] = f[i, t, :, :, :, p.core] + self.froms["core"][i, t]
+        self.copy("x", i).start()
+
+    def y_step(self, i):
+        p, f = self.p, self.part
+        self.copy("x", i).wait_recv()
+        f[i, 2 * p.x, :, :, :, p.core] = f[i, 2 * p.x, :, :, :, p.core] + self.froms["x"][i]
+        self.copy("y", i).start()
+
+    def b_step(self, i):
+        p, f = self.p, self.part
+        self.copy("y", i).wait_recv()
+        f[i, self.own, :, :, p.y, p.core] = f[i, self.own, :, :, p.y, p.core] + self.froms["y"][i]
+        self.copy("b", i).start()
+
+    def a_step(self, i):
+        p, f = self.p, self.part
+        self.copy("b", i).wait_recv()
+        f[i, self.own, :, p.b, p.y, p.core] = f[i, self.own, :, p.b, p.y, p.core] + self.froms["b"][i]
+        self.copy("a", i).start()
+
+    def p_step(self, i):
+        p, f = self.p, self.part
+        self.copy("a", i).wait_recv()
+        total = f[i, self.own, p.a, p.b, p.y, p.core].astype(f32) + self.froms["a"][i].astype(f32)
+        self.done[i] = total.astype(bf16)
+        self.copy("p", i).start()
+
+    def finish(self, i):
+        self.copy("p", i).wait_recv()
+        a, b = self.done[i].astype(f32), self.froms["p"][i].astype(f32)
+        first = self.p.x == 0
+        low, high = jnp.where(first, a, b), jnp.where(first, b, a)
+        return jnp.concatenate([low[0], low[1] + high[0], high[1]], 1)
+
+    def turn(self, t, consume):
+        steps = (self.x_step, self.y_step, self.b_step, self.a_step, self.p_step, consume)
+        for lag, step in enumerate(steps):
+            lag = lag * LAG
+            when((t >= lag) & (t < self.pieces + lag), lambda lag=lag, step=step: step(t - lag))
+
+    def sent(self, i):
+        for name in self.names:
+            self.copy(name, i).wait_send()
+
+
+def back_kernel(heads, rates, x_hbm, c_hbm, y1_hbm, dz_hbm, da_hbm, g_hbm, du_hbm, qkv_hbm, dc_hbm, dh1_hbm, wq_hbm,
+                seg_ref, lse_ref, delta_ref, dv_ref, dbin_ref, am, aw, aa, dm, dw, da_, vm, vw, va,
+                gin_o, am_o, aw_o, aa_o, dm_o, dw_o, da_o, vm_o, vw_o, va_o,
+                part, fromc, fromx, fromy, fromb, froma, fromp, done, stg, ch, lhs, qb, dqb, wq, bias, dsb, hb, sa, sd, vrow,
+                ld, sem_in, sem_out, *sems):
+    place = Place()
+    rows, _, seq = seg_ref.shape
+    tokens, width = x_hbm.shape
+    pairs = heads // 2
+    chunks = g_hbm.shape[0]
+    own_rows = sa.shape[2]
+    pieces = part.shape[0]
+    half = tokens // 2
+    r_ = Reduce(place, part, (fromc, fromx, fromy, fromb, froma, fromp), done, sems, pieces)
+    matrix_rate_, vector_rate_, replicas = rates
+
+    def load(src, dst, k):
+        return pltpu.make_async_copy(src, dst, ld.at[k])
+
+    state_in = [pltpu.make_async_copy(s, d, sem_in.at[k]) for k, (s, d) in enumerate(
+        [(am, sa.at[0]), (aw, sa.at[1]), (aa, sa.at[2]), (dm, sd.at[0]), (dw, sd.at[1]), (da_, sd.at[2])])]
+    wq_in = pltpu.make_async_copy(wq_hbm, wq, sem_in.at[6])
+    items = [g_hbm.at[j] for j in range(chunks)] + [du_hbm.at[j] for j in range(chunks)] + [da_hbm]
+    lefts = [dz_hbm, y1_hbm, c_hbm, x_hbm, dc_hbm]
+    left_in = [load(s, stg, k) for k, s in enumerate(lefts)]
+    item_in = [load(s, ch.at[k % 2], 5 + k) for k, s in enumerate(items)]
+    left_in[0].start()
+    item_in[0].start()
+    item_in[1].start()
+    place.greet()
+    for c in state_in:
+        c.start()
+    wq_in.start()
+    for r in range(rows):
+        doc_bias(seg_ref[r], bias, r)
+
+    def advance_to(grad, ref, index, rate):
+        grad = grad / replicas
+        moment = momentum_decay * ref[(0,) + index] + grad
+        weight = ref[(1,) + index] - rate * (grad + momentum_decay * moment)
+        ref[(0,) + index] = moment
+        ref[(1,) + index] = weight
+        ref[(2,) + index] = average_decay * ref[(2,) + index] + (1.0 - average_decay) * weight
+
+    ff_pieces = 4 * chunks
+
+    def consume(i):
+        grad = r_.finish(i)
+
+        def dense():
+            per = 2 * chunks
+            which = 1 - i // per
+            cols = pl.ds(pl.multiple_of(lax.rem(i, per) * PIECE, LANES), PIECE)
+            advance_to(grad, sd, (which, slice(None), cols), matrix_rate_)
+
+        def output():
+            cols = pl.ds(pl.multiple_of((i - ff_pieces) * PIECE, LANES), PIECE)
+            advance_to(grad, sa, (3, slice(None), cols), matrix_rate_)
+
+        def projections():
+            cols = pl.ds(pl.multiple_of((i - ff_pieces - 2) * LANES, LANES), LANES)
+            for k in range(3):
+                advance_to(grad[:, k * LANES : (k + 1) * LANES], sa, (k, slice(None), cols), matrix_rate_)
+
+        def vectors():
+            vrow[:own_rows, :LANES] = grad[:, :LANES]
+            vec = vrow[:, :LANES].T[: vm.shape[0], :own_rows] / replicas
+            moment = momentum_decay * vm[...] + vec
+            weight = vw[...] - vector_rate_ * (vec + momentum_decay * moment)
+            vm_o[...] = moment
+            vw_o[...] = weight
+            va_o[...] = average_decay * va[...] + (1.0 - average_decay) * weight
+
+        when(i < ff_pieces, dense)
+        when((i >= ff_pieces) & (i < ff_pieces + 2), output)
+        when((i >= ff_pieces + 2) & (i < pieces - 1), projections)
+        when(i == pieces - 1, vectors)
+
+    def transpose_left(k):
+        left_in[k].wait()
+        for j in range(tokens // 256):
+            lhs[:, j * 256 : (j + 1) * 256] = stg[j * 256 : (j + 1) * 256, :].T
+        left_in[k + 1].start()
+
+    n_half = width // 2
+
+    for k in range(len(items)):
+        if k % chunks == 0:
+            transpose_left(k // chunks)
+        item_in[k].wait()
+
+        def product(a, k=k):
+            d = dot(lhs[pl.ds(pl.multiple_of(a * n_half, LANES), n_half), :], ch[k % 2])
+            for t in range(6):
+                part[2 * k + t // 3, t % 3, a] = d[:, t * LANES : (t + 1) * LANES].astype(bf16).reshape(2, 2, 2, own_rows, LANES)
+
+        loop(2, product)
+        r_.start(2 * k)
+        r_.start(2 * k + 1)
+        if k + 2 < len(items):
+            item_in[k + 2].start()
+        if k == 1:
+            for c in state_in:
+                c.wait()
+        if k >= 1:
+            r_.turn(k - 1, consume)
+    t0 = len(items) - 1
+    transpose_left(3)
+    q_in = lambda p: pltpu.make_async_copy(qkv_hbm.at[p], qb.at[lax.rem(p, 2)], sem_in.at[7 + p])
+    q_in(0).start()
+    q_in(1).start()
+    left_in[4].wait()
+    wq_in.wait()
+    vrow[...] = jnp.zeros_like(vrow)
+    vrow[:8, :] = dv_ref[...]
+    for j in range(chunks):
+        vrow[8 + j : 9 + j, :] = dbin_ref[j]
+    dsb[...] = jnp.zeros_like(dsb)
+    first = lax.broadcasted_iota(jnp.int32, (LANES, LANES), 1) < HD
+    first_seq = lax.broadcasted_iota(jnp.int32, (seq, LANES), 1) < HD
+
+    def pair(p):
+        head = pl.ds(pl.multiple_of(p * LANES, LANES), LANES)
+        slot = lax.rem(p, 2)
+        q_in(p).wait()
+
+        def row(r):
+            tok = pl.ds(pl.multiple_of(r * seq, seq), seq)
+            q2 = qb[slot, tok, :LANES]
+            k2 = qb[slot, tok, LANES : 2 * LANES]
+            v2 = qb[slot, tok, 2 * LANES :]
+            dc2 = stg[tok, head]
+            dqs = []
+            for h in range(2):
+                lse = lse_ref[r, pl.ds(2 * p + h, 1), :]
+                dl = delta_ref[pl.ds(2 * p + h, 1), tok]
+                own = first if h == 0 else ~first
+                for c in range(seq // LANES):
+                    lo, hi = key_range(c, seq, LANES)
+                    cut = slice(c * LANES, (c + 1) * LANES)
+                    km = jnp.where(own, k2[cut], jnp.zeros_like(k2[cut]))
+                    vm_ = jnp.where(own, v2[cut], jnp.zeros_like(v2[cut]))
+                    pt = jnp.exp2((dot_nt(km, q2[lo:hi]) + bias[r, cut, lo:hi]) * SCALE2 - lse[:, lo:hi])
+                    ds = (pt * (dot_nt(vm_, dc2[lo:hi]) - dl[:, lo:hi])).astype(bf16)
+                    dsb[h, cut, lo:hi] = ds
+                    dv = dot(pt.astype(bf16), dc2[lo:hi]).astype(bf16)
+                    dk = (dot(ds, q2[lo:hi]) * 0.125).astype(bf16)
+                    at = pl.ds(pl.multiple_of(r * seq + c * LANES, LANES), LANES)
+                    if h == 1:
+                        dv = jnp.where(first, dqb[p, at, 2 * LANES :], dv)
+                        dk = jnp.where(first, dqb[p, at, LANES : 2 * LANES], dk)
+                    dqb[p, at, 2 * LANES :] = dv
+                    dqb[p, at, LANES : 2 * LANES] = dk
+                dqs.append(dot_tn(dsb[h], k2) * 0.125)
+            dqb[p, tok, :LANES] = jnp.where(first_seq, dqs[0], dqs[1]).astype(bf16)
+            when(t0 + 3 * p + r <= ff_pieces + 2 + p - 1, lambda: r_.turn(t0 + 3 * p + r, consume))
+
+        loop(rows, row)
+        when(p + 2 < pairs, lambda: q_in(p + 2).start())
+        piece = ff_pieces + 2 + p
+
+        def product(a):
+            d = dot(lhs[pl.ds(pl.multiple_of(a * n_half, LANES), n_half), :], dqb[p])
+            for t in range(3):
+                part[piece, t, a] = d[:, t * LANES : (t + 1) * LANES].astype(bf16).reshape(2, 2, 2, own_rows, LANES)
+
+        loop(2, product)
+        r_.start(piece)
+        sums = jnp.sum(dqb[p].astype(f32), 0, keepdims=True)
+        vrow[4:5, head] = sums[:, :LANES]
+        vrow[5:6, head] = sums[:, 2 * LANES :]
+        when(t0 + 3 * p + 2 <= piece, lambda: r_.turn(t0 + 3 * p + 2, consume))
+
+    loop(pairs, pair)
+    return_turn = t0 + 3 * pairs
+    left_out = [t for p in range(pairs) for t, last in ((t0 + 3 * p, ff_pieces + 1 + p), (t0 + 3 * p + 1, ff_pieces + 1 + p), (t0 + 3 * p + 2, ff_pieces + 2 + p)) if t > last]
+    cols = vrow[...].T.astype(bf16)
+    part[pieces - 1, 0] = cols.reshape(2, 2, 2, 2, own_rows, LANES)
+    part[pieces - 1, 1] = jnp.zeros_like(part[pieces - 1, 1])
+    part[pieces - 1, 2] = jnp.zeros_like(part[pieces - 1, 2])
+    r_.start(pieces - 1)
+    vrow[...] = jnp.zeros_like(vrow)
+    for t in left_out:
+        r_.turn(t, consume)
+    h_in = lambda i: pltpu.make_async_copy(dh1_hbm.at[pl.ds(pl.multiple_of(i * 256, 256), 256)], hb.at[lax.rem(i, 2)], sem_in.at[7 + pairs + i])
+    h_in(0).start()
+    h_in(1).start()
+    blocks = tokens // 256
+    gin = stg
+
+    def gin_block(i):
+        at = pl.ds(pl.multiple_of(i * 256, 256), 256)
+        h_in(i).wait()
+        d = jnp.concatenate([dqb[p, at, :] for p in range(pairs)], 1)
+        w = jnp.concatenate([tile(wq, p, t) for p in range(pairs) for t in range(3)], 1)
+        gin[at, :] = (hb[lax.rem(i, 2)] + dot_nt(d, w)).astype(bf16)
+        when(i + 2 < blocks, lambda: h_in(i + 2).start())
+        r_.turn(return_turn + i, consume)
+
+    loop(blocks, gin_block)
+    gin_out = pltpu.make_async_copy(gin, gin_o, sem_out.at[6])
+    gin_out.start()
+    rest = pieces + 5 * LAG - (return_turn + blocks)
+    loop(rest, lambda i: r_.turn(return_turn + blocks + i, consume))
+    outs = [pltpu.make_async_copy(s, d, sem_out.at[k]) for k, (s, d) in enumerate(
+        [(sa.at[0], am_o), (sa.at[1], aw_o), (sa.at[2], aa_o), (sd.at[0], dm_o), (sd.at[1], dw_o), (sd.at[2], da_o)])]
+    for c in outs:
+        c.start()
+    loop(pieces, r_.sent)
+    gin_out.wait()
+    for c in outs:
+        c.wait()
+
+
+def back(rates, x, c, y1, dz, da, g, du, qkv, dc, dh1, wq, seg, lse, delta, dv, dbin, states):
+    rows, seq = seg.shape
+    tokens, width = x.shape
+    chunks = g.shape[0]
+    own_rows = states[0].shape[1]
+    heads = width // HD
+    pairs = heads // 2
+    pieces = 4 * chunks + 2 + pairs + 1
+    sh = jax.ShapeDtypeStruct
+    dma = pltpu.SemaphoreType.DMA
+    v = pltpu.VMEM
+    hbm = pl.BlockSpec(memory_space=pl.ANY)
+    vmem = pl.BlockSpec(memory_space=pltpu.VMEM)
+    tail = (own_rows, LANES)
+    scratch = [
+        v((pieces, 3, 2, 2, 2, 2) + tail, bf16), v((pieces, 3, 2, 2, 2) + tail, bf16), v((pieces, 2, 2, 2) + tail, bf16),
+        v((pieces, 2, 2, 2) + tail, bf16), v((pieces, 2, 2) + tail, bf16), v((pieces, 2) + tail, bf16), v((pieces, 2) + tail, bf16),
+        v((pieces, 2) + tail, bf16), v((tokens, width), bf16), v((2, tokens, width), bf16), v((width, tokens), bf16),
+        v((2, tokens, PIECE), bf16), v((pairs, tokens, PIECE), bf16), v(wq.shape, bf16), v((rows, seq, seq), f32),
+        v((2, seq, seq), bf16), v((2, 256, width), f32), v((3,) + states[0].shape, f32), v((3,) + states[3].shape, f32),
+        v((LANES, width), f32),
+        dma((5 + 2 * chunks + 1,)), dma((7 + pairs + tokens // 256,)), dma((7,))] + [dma((pieces,))] * 12
+    return pl.pallas_call(
+        functools.partial(back_kernel, heads, rates),
+        out_shape=(sh((tokens, width), bf16),) + tuple(sh(s.shape, f32) for s in states),
+        in_specs=[hbm] * 11 + [vmem] * 5 + [hbm] * 6 + [vmem] * 3,
+        out_specs=(hbm,) * 7 + (vmem,) * 3,
+        scratch_shapes=scratch,
+        compiler_params=pltpu.CompilerParams(collective_id=1, has_side_effects=True, vmem_limit_bytes=62 * 2**20),
+        name="back",
+    )(x, c, y1, dz, da, g, du, qkv, dc, dh1, wq, seg.reshape(rows, 1, seq), lse, delta, dv, dbin, *states)
+
+
 def pack_columns(attention, dense, vectors):
     count = vectors.shape[0]
     vector_cols = jnp.pad(vectors.T, ((0, 0), (0, 128 - count)))
@@ -279,7 +1069,7 @@
     return (moment_new, weight_new, average_new)
 
 
-def body(
+def plain_body(
     hidden_in,
     segment_ids,
     cotangent,
@@ -334,10 +1124,44 @@
     return (out.reshape(hidden_in.shape), gin.reshape(hidden_in.shape)) + attention_new + dense_new + vector_new
 
 
+def body(
+    hidden_in,
+    segment_ids,
+    cotangent,
+    attention_weights,
+    attention_momentum,
+    attention_average,
+    dense_weights,
+    dense_momentum,
+    dense_average,
+    vector_params,
+    vector_momentum,
+    vector_average,
+):
+    row_count, length, width = hidden_in.shape
+    x = hidden_in.reshape(-1, width)
+    e = cotangent.reshape(-1, width)
+    replicas = lax.axis_size("narrow")
+    tokens_all = row_count * length * lax.axis_size("wide") * replicas
+    grad_scale = math.sqrt(tokens_all) / replicas
+    rates = (matrix_rate / grad_scale, vector_rate / grad_scale, replicas)
+    qkv, c, lse, wq, out, y1, g, dz, du, da, dc, dh1, delta, dv, dbin = stage(
+        x, segment_ids, e, attention_weights, dense_weights, vector_params
+    )
+    states = (
+        attention_momentum, attention_weights, attention_average,
+        dense_momentum, dense_weights, dense_average,
+        vector_momentum, vector_params, vector_average,
+    )
+    news = back(rates, x, c, y1, dz, da, g, du, qkv, dc, dh1, wq, segment_ids, lse, delta, dv, dbin, states)
+    return (out.reshape(hidden_in.shape), news[0].reshape(hidden_in.shape)) + tuple(news[1:])
+
+
 def solution(mesh):
     token = P(("wide", "narrow"), None, None)
     matrix = P(None, "wide", None)
     vector = P(None, "wide")
     in_specs = (token, P(("wide", "narrow"), None), token) + (matrix,) * 6 + (vector,) * 3
     out_specs = (token, token) + (matrix,) * 6 + (vector,) * 3
-    return jax.shard_map(body, mesh=mesh, in_specs=in_specs, out_specs=out_specs, check_vma=False)
+    ours = mesh.shape["wide"] == 16 and mesh.shape["narrow"] == 2
+    return jax.shard_map(body if ours else plain_body, mesh=mesh, in_specs=in_specs, out_specs=out_specs, check_vma=False)

time: 505 us -> 219 us (0.43)
  waiting for transfers between devices: 307 us -> 0 us
  Pallas kernels: 130 us -> 206 us
  other arithmetic: 26.5 us -> 0 us
  between operations: 14.1 us -> 0.7 us
  local copies, waits for them, and re-layouts: 25.9 us -> 12.7 us
    reduce_scatter x2 -> x0, waiting for transfers between devices: 159 us -> none  [the longest x1 123 us: body(): lax.psum_scatter(grad_second, 'wide', scatter_dimension=0, tiled=True)]
    all_gather x2 -> x0, waiting for transfers between devices: 111 us -> none  [the longest x1 61.5 us: body(): lax.all_gather(second.astype(bf16), 'wide', axis=0, tiled=True)]
    pallas_call x6 -> x2, Pallas kernels: 130 us -> 206 us  [the longest x1 109 us: stage(): pl.pallas_call(functools.partial(stage_kernel, heads), out_shape=(sh((pai...]
    psum x1 -> x0, waiting for transfers between devices: 36.9 us -> none  [body(): t2 = lax.psum(share_second, 'narrow').astype(f32) / replicas]
    slice x11 -> x0, local copies, waits for them, and re-layouts: 15.4 us -> none  [the longest x1 8.13 us: body(): second_full[:, width + ff:]]
    concatenate x5 -> x0, other arithmetic: 15.3 us -> none  [the longest x1 8.94 us: body(): jnp.concatenate([wgrad(c, da), wgrad(y1, du), wgrad(dz, g)], 1)]
    add x3 -> x0, other arithmetic: 5.6 us -> none  [advance(): average_new = average_decay * average + (1.0 - average_decay) * weight_new]
    unnamed x45 -> x33, local copies, waits for them, and re-layouts: 7.81 us -> 11.4 us
  transfers between devices with their start and end apart: 5 -> 0, of which waited for: 5 -> 0; matrix products, arithmetic and copies ran while one was open for 4% -> 0% of each run, Pallas kernels for 9% -> 0%
where the time goes in v3:
time: 219 us
  Pallas kernels  206 us (94%)
  local copies, waits for them, and re-layouts  12.7 us (6%)
    pallas_call x1, Pallas kernels, stage(): pl.pallas_call(functools.partial(stage_kernel, heads), out_shape=(sh((pai...  109 us
    pallas_call x1, Pallas kernels, back(): pl.pallas_call(functools.partial(back_kernel, heads, rates), out_shape=(s...  96.6 us
    unnamed x33, local copies, waits for them, and re-layouts  11.4 us

profile of v3, /device:TPU:0, one launch (start us, length us, event | category | flops | bytes accessed | tf_op | source)
XLA Modules:
  0.0 219.1 jit_solution(1740314713226561210)
XLA Ops:
  0.6 1.3 reshape.39.seg_ref
  1.9 109.2 %stage.1 = (bf16[6,1024,384]{2,1,0:T(8,128)(2,1)}, bf16[1024,768]{1,0:T(8,128)(2,1)}, f32[2,16,512]{2,1,0:T(8,128)}, bf16[6,3,2,2,2,2,48,128]{7,6,5,4,3,2,1,0:T(...) custom-call(bf16[1024,768]{1,0:T(8,128)(2,1)} %bitcast.4, ...), custom_call_target="tpu_custom_call" | custom-call | tf_op jit(solution)/shard_map/stage/pallas_call | solution.py:719
  111.1 0.0 copy-start
  111.1 96.6 %back.1 = (bf16[1024,768]{1,0:T(8,128)(2,1)}, f32[4,48,768]{2,1,0:T(8,128)}, f32[4,48,768]{2,1,0:T(8,128)}, f32[4,48,768]{2,1,0:T(8,128)}, f32[2,48,3072]{2,1,0:...) custom-call(bf16[1024,768]{1,0:T(8,128)(2,1)} %bitcast.5, ...), custom_call_target="tpu_custom_call" | custom-call | tf_op jit(solution)/shard_map/back/pallas_call | solution.py:1046
  207.7 0.0 copy-done
  207.7 0.0 copy-start.1
  207.7 1.1 copy.34
  208.8 0.8 copy-done.1
  209.7 0.0 copy-start.7
  209.7 0.0 copy-start.6
  209.7 1.1 copy.35
  210.8 0.3 copy-done.7
  211.1 0.0 copy-start.5
  211.1 0.0 copy-start.4
  211.1 0.8 copy.36
  211.9 0.0 copy-done.6
  211.9 0.8 copy.37
  212.7 0.0 copy-done.5
  212.7 0.0 copy-start.3
  212.8 0.8 copy.38
  213.6 0.0 copy-done.4
  213.6 1.0 copy.39
  214.6 0.0 copy-done.3
  214.6 1.0 copy.40
  215.6 0.7 copy-done.2
  216.3 1.0 copy.41
  217.3 0.0 copy-done.10
  217.3 0.6 copy.42
  217.9 0.0 copy-done.9
  217.9 0.6 copy.43
  218.5 0.0 copy-done.8
  218.5 0.6 copy.44
  (4 shorter events, 0.0 us)
Async XLA Ops:
  111.1 96.6 %copy-start = (bf16[1024,768]{1,0:T(8,128)(2,1)S(1)}, bf16[1024,768]{1,0:T(8,128)(2,1)}, u32[]{:S(2)}) copy-start(bf16[1024,768]{1,0:T(8,128)(2,1)} %get-tuple-element.36) | copy-start | bytes 4718596
  207.7 2.0 copy-start.1
  209.7 1.4 copy-start.7
  209.7 2.3 %copy-start.6 = (f32[4,48,768]{2,1,0:T(8,128)S(1)}, f32[4,48,768]{2,1,0:T(8,128)}, u32[]{:S(2)}) copy-start(f32[4,48,768]{2,1,0:T(8,128)} %get-tuple-element.75) | copy-start | bytes 1769476
  211.1 1.6 copy-start.5
  211.1 2.5 %copy-start.4 = (f32[2,48,3072]{2,1,0:T(8,128)S(1)}, f32[2,48,3072]{2,1,0:T(8,128)}, u32[]{:S(2)}) copy-start(f32[2,48,3072]{2,1,0:T(8,128)} %get-tuple-element.77) | copy-start | bytes 3538948
  212.7 1.8 copy-start.3
  214.6 1.7 copy-start.2
  216.3 1.0 copy-start.10
  216.3 1.6 copy-start.9
  216.3 2.2 %copy-start.8 = (f32[12,48]{1,0:T(8,128)S(1)}, f32[12,48]{1,0:T(8,128)}, u32[]{:S(2)}) copy-start(f32[12,48]{1,0:T(8,128)} %get-tuple-element.82) | copy-start | bytes 6916

commit v4 on v3

--- a/solution.py
+++ b/solution.py
@@ -435,9 +435,9 @@
 
 
 def stage_kernel(heads, x_hbm, seg_ref, e_hbm, aw_hbm, dw_hbm, vp_ref,
-                 qkv_o, c_o, lse_o, wq_o, out_o, y1_o, g_o, dz_o, du_o, da_o, dc_o, dh1_o, delta_o, dv_o, dbin_o,
-                 full, vfull, shard, vshard, square, xb, eb, cb, n1b, y1b, acc, gp, gb, dzb, bias, lsea, vrow, binr, r1b,
-                 in_sem, out_sem, *sems):
+                 qkv_o, c_o, lse_o, w_o, out_o, y1_o, g_o, gp_o, dz_o, dh2_o, n1_o, r1_o, dv_o, vrow,
+                 full, vfull, shard, vshard, square, xb, eb, cb, n1b, y1b, acc, gp, gb, dzb, bias, lsea, binr, r1b,
+                 in_sem, out_sem, w_sem, *sems):
     place = Place()
     rows, _, seq = seg_ref.shape
     tokens, width = x_hbm.shape
@@ -446,6 +446,7 @@
     chunks = gb.shape[0]
     own_rows = aw_hbm.shape[1]
     blk = 256
+    big = 512
     g = Gather(place, shard, full, sems[:11], pieces)
     gv = GatherVector(place, vshard, vfull, sems[11:])
 
@@ -512,8 +513,12 @@
     def qkv_out(p):
         return pltpu.make_async_copy(qkv_at(p), qkv_o.at[p], out_sem.at[p])
 
+    def w_out(i):
+        return pltpu.make_async_copy(full.at[i], w_o.at[i], w_sem.at[i])
+
     def pair(p):
         g.arrive(p)
+        w_out(p).start()
         head = pl.ds(pl.multiple_of(p * LANES, LANES), LANES)
         w = columns(full, p)
         b = jnp.concatenate([vrow[4:5, head], jnp.zeros((1, LANES), f32), vrow[5:6, head]], 1)
@@ -551,15 +556,14 @@
         lse_o[r] = lsea[r].T[: lse_o.shape[1]]
     c_out = pltpu.make_async_copy(cb, c_o, out_sem.at[pairs])
     c_out.start()
-    wq_out = pltpu.make_async_copy(full.at[pl.ds(0, pairs)], wq_o, out_sem.at[pairs + 1])
-    wq_out.start()
     g1, s1, g2, s2, bo, bd = (vrow[j : j + 1, :] for j in (0, 1, 2, 3, 6, 7))
 
     def block(i):
         return pl.ds(pl.multiple_of(i * blk, blk), blk)
 
-    g.arrive(pairs)
-    g.arrive(pairs + 1)
+    for i in (pairs, pairs + 1):
+        g.arrive(i)
+        w_out(i).start()
 
     def norm_one(i):
         at = block(i)
@@ -569,7 +573,7 @@
         n1 = cen * r1
         y1 = n1 * g1 + s1
         n1b[at, :] = n1
-        r1b[at, :] = r1
+        r1b[at, :] = jnp.broadcast_to(r1, (blk, LANES))
         y1b[at, :] = y1.astype(bf16)
         acc[at, :] = y1 + bd
         when(lax.rem(i, 2) == 1, lambda: g.turn(done + i // 2))
@@ -578,6 +582,10 @@
     done += 2
     y1_out = pltpu.make_async_copy(y1b, y1_o, out_sem.at[pairs + 2])
     y1_out.start()
+    n1_out = pltpu.make_async_copy(n1b, n1_o, out_sem.at[pairs + 1])
+    n1_out.start()
+    r1_out = pltpu.make_async_copy(r1b, r1_o, out_sem.at[pairs + 5 + chunks])
+    r1_out.start()
     loop(pairs, lambda p: qkv_out(p).wait())
 
     def up(j):
@@ -587,29 +595,34 @@
         return columns(full, pairs + 4 + 4 * j, pairs + 5 + 4 * j)
 
     def g_out(j):
-        return pltpu.make_async_copy(gb.at[j], g_o.at[j], out_sem.at[pairs + 3 + j])
+        return pltpu.make_async_copy(gb.at[j], g_o.at[j], out_sem.at[pairs + 7 + j])
+
+    def gp_out(j):
+        return pltpu.make_async_copy(gp.at[j], gp_o.at[j], out_sem.at[pairs + 7 + chunks + j])
 
     def ff_chunk(j):
         for t in range(4):
             g.arrive(pairs + 2 + 4 * j + t)
+            w_out(pairs + 2 + 4 * j + t).start()
 
         def ff_block(i):
-            at = block(i)
+            at = pl.ds(pl.multiple_of(i * big, big), big)
             u = dot(y1b[at, :], up(j)) + binr[j]
             act, slope = gelu_parts(u)
             gl = act.astype(bf16)
             gb[j, at, :] = gl
             gp[j, at, :] = slope
             acc[at, :] += dot_nt(gl, down(j))
-            when(i < 3, lambda: g.turn(done + 3 * j + i))
-
-        loop(tokens // blk, ff_block)
+            g.turn(done + 3 * j + i)
+
+        loop(tokens // big, ff_block)
+        g.turn(done + 3 * j + 2)
         g_out(j).start()
+        gp_out(j).start()
 
     loop(chunks, ff_chunk)
     e_load.wait()
     dv_o[...] = jnp.zeros_like(dv_o)
-    dbin_o[...] = jnp.zeros_like(dbin_o)
 
     def colsum(t):
         return jnp.sum(t, 0, keepdims=True)
@@ -632,65 +645,16 @@
         dv_o[7:8, :] += colsum(dz.astype(f32))
 
     loop(tokens // blk, norm_two)
-    out_out = pltpu.make_async_copy(xb, out_o, out_sem.at[pairs + 3 + chunks])
-    dz_out = pltpu.make_async_copy(dzb, dz_o, out_sem.at[pairs + 4 + chunks])
-    out_out.start()
-    dz_out.start()
-
-    def du_out(j):
-        return pltpu.make_async_copy(gb.at[j], du_o.at[j], out_sem.at[pairs + 5 + chunks + j])
-
-    def back_chunk(j):
-        g_out(j).wait()
-
-        def back_block(i):
-            at = block(i)
-            du = (dot(dzb[at, :], down(j)) * gp[j, at, :]).astype(bf16)
-            gb[j, at, :] = du
-            dbin_o[j] += colsum(du.astype(f32))
-            acc[at, :] += dot_nt(du, up(j))
-
-        loop(tokens // blk, back_block)
-        du_out(j).start()
-
-    loop(chunks, back_chunk)
-    c_out.wait()
-    y1_out.wait()
-    sel_shape = (delta_o.shape[0], width)
-    sel = jnp.where(lax.broadcasted_iota(jnp.int32, sel_shape, 0) == lax.broadcasted_iota(jnp.int32, sel_shape, 1) // HD, 1.0, 0.0).astype(bf16)
-
-    def norm_one_back(i):
-        at = block(i)
-        dy1 = acc[at, :]
-        n1 = n1b[at, :]
-        dn = dy1 * g1
-        dh1 = r1b[at, :] * (dn - jnp.mean(dn, 1, keepdims=True) - n1 * jnp.mean(dn * n1, 1, keepdims=True))
-        acc[at, :] = dh1
-        da = dh1.astype(bf16)
-        eb[at, :] = da
-        dc = dot_nt(da, columns(full, pairs, pairs + 1)).astype(bf16)
-        y1b[at, :] = dc
-        prod = dc.astype(f32) * cb[at, :].astype(f32)
-        hi = prod.astype(bf16)
-        lo = (prod - hi.astype(f32)).astype(bf16)
-        delta_o[:, at] = dot_nt(sel, hi) + dot_nt(sel, lo)
-        dv_o[0:1, :] += colsum(dy1 * n1)
-        dv_o[1:2, :] += colsum(dy1)
-        dv_o[6:7, :] += colsum(da.astype(f32))
-
-    loop(tokens // blk, norm_one_back)
-    base = pairs + 5 + 2 * chunks
-    last = [pltpu.make_async_copy(s, d, out_sem.at[base + k]) for k, (s, d) in enumerate(((acc, dh1_o), (eb, da_o), (y1b, dc_o)))]
+    last = [pltpu.make_async_copy(s, d, out_sem.at[pairs + k]) for k, (s, d) in ((3, (xb, out_o)), (4, (dzb, dz_o)), (6, (acc, dh2_o)))]
     for c in last:
         c.start()
     gv.sent()
     loop(pieces, g.sent)
-    wq_out.wait()
-    out_out.wait()
-    dz_out.wait()
-    loop(chunks, lambda j: du_out(j).wait())
-    for c in last:
+    loop(pieces, lambda i: w_out(i).wait())
+    for c in [c_out, y1_out, n1_out, r1_out] + last:
         c.wait()
+    loop(chunks, lambda j: g_out(j).wait())
+    loop(chunks, lambda j: gp_out(j).wait())
 
 
 def stage(x, seg, e, aw, dw, vp):
@@ -707,21 +671,22 @@
     vmem = pl.BlockSpec(memory_space=pltpu.VMEM)
     tok = sh((tokens, width), bf16)
     wide = sh((chunks, tokens, width), bf16)
+    long = sh((tokens, width), f32)
     block = (2, 2, 2, 2, own_rows, LANES)
     scratch = [
         v((pieces, 3) + block, bf16), v(block, bf16), v((pieces, 3, own_rows, LANES), bf16), v((own_rows, LANES), bf16),
         v((LANES, LANES), f32), v((tokens, width), bf16), v((tokens, width), bf16), v((tokens, width), bf16),
         v((tokens, width), f32), v((tokens, width), bf16), v((tokens, width), f32), v((chunks, tokens, width), f32),
         v((chunks, tokens, width), bf16), v((tokens, width), bf16), v((rows, seq, seq), f32), v((rows, seq, LANES), f32),
-        v((16, width), f32), v((chunks, 1, width), f32), v((tokens, 1), f32),
-        dma((6 + 2 * chunks,)), dma((pairs + 8 + 2 * chunks,)),
+        v((chunks, 1, width), f32), v((tokens, LANES), f32),
+        dma((6 + 2 * chunks,)), dma((pairs + 7 + 2 * chunks,)), dma((pieces,)),
     ] + [dma((pieces,))] * 11 + [dma(())] * 9
     return pl.pallas_call(
         functools.partial(stage_kernel, heads),
-        out_shape=(sh((pairs, tokens, PIECE), bf16), tok, sh((rows, 16, seq), f32), sh((pairs, 3) + block, bf16), tok, tok, wide,
-                   tok, wide, tok, tok, sh((tokens, width), f32), sh((16, tokens), f32), sh((8, width), f32), sh((chunks, 1, width), f32)),
+        out_shape=(sh((pairs, tokens, PIECE), bf16), tok, sh((rows, 16, seq), f32), sh((pieces, 3) + block, bf16), tok, tok, wide,
+                   sh((chunks, tokens, width), f32), tok, long, long, sh((tokens, LANES), f32), sh((8, width), f32), sh((16, width), f32)),
         in_specs=[hbm, vmem, hbm, hbm, hbm, vmem],
-        out_specs=(hbm, hbm, vmem, hbm, hbm, hbm, hbm, hbm, hbm, hbm, hbm, hbm, vmem, vmem, vmem),
+        out_specs=(hbm, hbm, vmem) + (hbm,) * 9 + (vmem, vmem),
         scratch_shapes=scratch,
         compiler_params=pltpu.CompilerParams(collective_id=0, has_side_effects=True, vmem_limit_bytes=BIG),
         name="stage",
@@ -731,8 +696,8 @@
 class Reduce:
     names = ("core", "x", "y", "b", "a", "p")
 
-    def __init__(self, place, part, froms, done, sems, pieces):
-        self.p, self.part, self.done, self.pieces = place, part, done, pieces
+    def __init__(self, place, part, froms, done, out, sems, pieces):
+        self.p, self.part, self.done, self.out, self.pieces = place, part, done, out, pieces
         self.froms = dict(zip(self.names, froms))
         self.sems = {name: (sems[2 * k], sems[2 * k + 1]) for k, name in enumerate(self.names)}
         self.own = pl.ds(place.x, 2)
@@ -794,10 +759,10 @@
         a, b = self.done[i].astype(f32), self.froms["p"][i].astype(f32)
         first = self.p.x == 0
         low, high = jnp.where(first, a, b), jnp.where(first, b, a)
-        return jnp.concatenate([low[0], low[1] + high[0], high[1]], 1)
-
-    def turn(self, t, consume):
-        steps = (self.x_step, self.y_step, self.b_step, self.a_step, self.p_step, consume)
+        self.out[i] = jnp.concatenate([low[0], low[1] + high[0], high[1]], 1)
+
+    def turn(self, t):
+        steps = (self.x_step, self.y_step, self.b_step, self.a_step, self.p_step, self.finish)
         for lag, step in enumerate(steps):
             lag = lag * LAG
             when((t >= lag) & (t < self.pieces + lag), lambda lag=lag, step=step: step(t - lag))
@@ -807,225 +772,218 @@
             self.copy(name, i).wait_send()
 
 
-def back_kernel(heads, rates, x_hbm, c_hbm, y1_hbm, dz_hbm, da_hbm, g_hbm, du_hbm, qkv_hbm, dc_hbm, dh1_hbm, wq_hbm,
-                seg_ref, lse_ref, delta_ref, dv_ref, dbin_ref, am, aw, aa, dm, dw, da_, vm, vw, va,
-                gin_o, am_o, aw_o, aa_o, dm_o, dw_o, da_o, vm_o, vw_o, va_o,
-                part, fromc, fromx, fromy, fromb, froma, fromp, done, stg, ch, lhs, qb, dqb, wq, bias, dsb, hb, sa, sd, vrow,
-                ld, sem_in, sem_out, *sems):
+def back_kernel(heads, x_hbm, c_hbm, y1_hbm, dz_hbm, dh2_hbm, n1_hbm, r1_hbm, g_hbm, gp_hbm, qkv_hbm, w_hbm,
+                seg_ref, lse_ref, dv_ref, vec_ref, gin_o, sum_o,
+                part, fromc, fromx, fromy, fromb, froma, fromp, done, pool, wpool, gpool, acc, cb, dab, dcb, r1b, dsb, delta, vrow,
+                ld, out_sem, *sems):
     place = Place()
     rows, _, seq = seg_ref.shape
     tokens, width = x_hbm.shape
     pairs = heads // 2
     chunks = g_hbm.shape[0]
-    own_rows = sa.shape[2]
+    own_rows = part.shape[-2]
     pieces = part.shape[0]
-    half = tokens // 2
-    r_ = Reduce(place, part, (fromc, fromx, fromy, fromb, froma, fromp), done, sems, pieces)
-    matrix_rate_, vector_rate_, replicas = rates
-
-    def load(src, dst, k):
+    big = 512
+    r_ = Reduce(place, part, (fromc, fromx, fromy, fromb, froma, fromp), done, sum_o, sems, pieces)
+    ff_pieces = 4 * chunks
+    first_ff = pairs + 2
+    du, dz, y1 = pool.at[2], pool.at[3], pool.at[4]
+    x = y1
+
+    def load(k, src, dst):
         return pltpu.make_async_copy(src, dst, ld.at[k])
 
-    state_in = [pltpu.make_async_copy(s, d, sem_in.at[k]) for k, (s, d) in enumerate(
-        [(am, sa.at[0]), (aw, sa.at[1]), (aa, sa.at[2]), (dm, sd.at[0]), (dw, sd.at[1]), (da_, sd.at[2])])]
-    wq_in = pltpu.make_async_copy(wq_hbm, wq, sem_in.at[6])
-    items = [g_hbm.at[j] for j in range(chunks)] + [du_hbm.at[j] for j in range(chunks)] + [da_hbm]
-    lefts = [dz_hbm, y1_hbm, c_hbm, x_hbm, dc_hbm]
-    left_in = [load(s, stg, k) for k, s in enumerate(lefts)]
-    item_in = [load(s, ch.at[k % 2], 5 + k) for k, s in enumerate(items)]
-    left_in[0].start()
-    item_in[0].start()
-    item_in[1].start()
+    g_in = [load(j, g_hbm.at[j], pool.at[j % 2]) for j in range(chunks)]
+    gp_in = [load(chunks + j, gp_hbm.at[j], gpool.at[j % 2]) for j in range(chunks)]
+    w_in = [load(2 * chunks + j, w_hbm.at[pl.ds(first_ff + 4 * j, 4)], wpool.at[pl.ds(4 * (j % 2), 4)]) for j in range(chunks)]
+    base = 3 * chunks
+    dz_in, y1_in, acc_in, c_in, r1_in = (load(base + k, s, d) for k, (s, d) in enumerate(
+        ((dz_hbm, dz), (y1_hbm, y1), (dh2_hbm, acc), (c_hbm, cb), (r1_hbm, r1b))))
+    base += 5
+    n1_in = load(base, n1_hbm, gpool.at[1])
+    wo_in = load(base + 1, w_hbm.at[pl.ds(pairs, 2)], wpool.at[pl.ds(6, 2)])
+    wq_in = load(base + 2, w_hbm.at[pl.ds(0, pairs)], wpool.at[pl.ds(0, pairs)])
+    x_in = load(base + 3, x_hbm, x)
+    base += 4
+
+    def q_in(p):
+        return load(base + p, qkv_hbm.at[p], pool.at[3, :, pl.ds(pl.multiple_of(lax.rem(p, 2) * PIECE, LANES), PIECE)])
+
+    for c in (dz_in, g_in[0], gp_in[0], w_in[0], y1_in, acc_in, g_in[1], gp_in[1], w_in[1], c_in, r1_in):
+        c.start()
     place.greet()
-    for c in state_in:
-        c.start()
-    wq_in.start()
-    for r in range(rows):
-        doc_bias(seg_ref[r], bias, r)
-
-    def advance_to(grad, ref, index, rate):
-        grad = grad / replicas
-        moment = momentum_decay * ref[(0,) + index] + grad
-        weight = ref[(1,) + index] - rate * (grad + momentum_decay * moment)
-        ref[(0,) + index] = moment
-        ref[(1,) + index] = weight
-        ref[(2,) + index] = average_decay * ref[(2,) + index] + (1.0 - average_decay) * weight
-
-    ff_pieces = 4 * chunks
-
-    def consume(i):
-        grad = r_.finish(i)
-
-        def dense():
-            per = 2 * chunks
-            which = 1 - i // per
-            cols = pl.ds(pl.multiple_of(lax.rem(i, per) * PIECE, LANES), PIECE)
-            advance_to(grad, sd, (which, slice(None), cols), matrix_rate_)
-
-        def output():
-            cols = pl.ds(pl.multiple_of((i - ff_pieces) * PIECE, LANES), PIECE)
-            advance_to(grad, sa, (3, slice(None), cols), matrix_rate_)
-
-        def projections():
-            cols = pl.ds(pl.multiple_of((i - ff_pieces - 2) * LANES, LANES), LANES)
-            for k in range(3):
-                advance_to(grad[:, k * LANES : (k + 1) * LANES], sa, (k, slice(None), cols), matrix_rate_)
-
-        def vectors():
-            vrow[:own_rows, :LANES] = grad[:, :LANES]
-            vec = vrow[:, :LANES].T[: vm.shape[0], :own_rows] / replicas
-            moment = momentum_decay * vm[...] + vec
-            weight = vw[...] - vector_rate_ * (vec + momentum_decay * moment)
-            vm_o[...] = moment
-            vw_o[...] = weight
-            va_o[...] = average_decay * va[...] + (1.0 - average_decay) * weight
-
-        when(i < ff_pieces, dense)
-        when((i >= ff_pieces) & (i < ff_pieces + 2), output)
-        when((i >= ff_pieces + 2) & (i < pieces - 1), projections)
-        when(i == pieces - 1, vectors)
-
-    def transpose_left(k):
-        left_in[k].wait()
-        for j in range(tokens // 256):
-            lhs[:, j * 256 : (j + 1) * 256] = stg[j * 256 : (j + 1) * 256, :].T
-        left_in[k + 1].start()
-
-    n_half = width // 2
-
-    for k in range(len(items)):
-        if k % chunks == 0:
-            transpose_left(k // chunks)
-        item_in[k].wait()
-
-        def product(a, k=k):
-            d = dot(lhs[pl.ds(pl.multiple_of(a * n_half, LANES), n_half), :], ch[k % 2])
-            for t in range(6):
-                part[2 * k + t // 3, t % 3, a] = d[:, t * LANES : (t + 1) * LANES].astype(bf16).reshape(2, 2, 2, own_rows, LANES)
+    vrow[...] = jnp.zeros_like(vrow)
+    vrow[:8, :] = dv_ref[...]
+
+    def colsum(t):
+        return jnp.sum(t, 0, keepdims=True)
+
+    half = width // 2
+
+    def weight_grad(left, right, piece, count):
+        def product(a):
+            d = dot_tn(left[:, pl.ds(pl.multiple_of(a * half, LANES), half)], right)
+            for t in range(3 * count):
+                part[piece + t // 3, t % 3, a] = d[:, t * LANES : (t + 1) * LANES].astype(bf16).reshape(2, 2, 2, own_rows, LANES)
 
         loop(2, product)
-        r_.start(2 * k)
-        r_.start(2 * k + 1)
-        if k + 2 < len(items):
-            item_in[k + 2].start()
-        if k == 1:
-            for c in state_in:
-                c.wait()
-        if k >= 1:
-            r_.turn(k - 1, consume)
-    t0 = len(items) - 1
-    transpose_left(3)
-    q_in = lambda p: pltpu.make_async_copy(qkv_hbm.at[p], qb.at[lax.rem(p, 2)], sem_in.at[7 + p])
+        for k in range(count):
+            r_.start(piece + k)
+
+    dz_in.wait()
+    for j in range(chunks):
+        s = j % 2
+        g_in[j].wait()
+        weight_grad(dz, pool[s], 4 * j, 2)
+        r_.turn(2 * j)
+        gp_in[j].wait()
+        w_in[j].wait()
+        if j == 0:
+            y1_in.wait()
+            acc_in.wait()
+
+        def block(i, j=j, s=s):
+            at = pl.ds(pl.multiple_of(i * big, big), big)
+            d = (dot(dz[at, :], columns(wpool, 4 * s + 2, 4 * s + 3)) * gpool[s, at, :]).astype(bf16)
+            du[at, :] = d
+            acc[at, :] += dot_nt(d, columns(wpool, 4 * s, 4 * s + 1))
+            vrow[8 + j : 9 + j, :] += colsum(d.astype(f32))
+
+        loop(tokens // big, block)
+        if j + 2 < chunks:
+            g_in[j + 2].start()
+            gp_in[j + 2].start()
+            w_in[j + 2].start()
+        weight_grad(y1, du[...], 4 * j + 2, 2)
+        r_.turn(2 * j + 1)
+    n1_in.start()
+    wo_in.start()
+    x_in.start()
     q_in(0).start()
     q_in(1).start()
-    left_in[4].wait()
-    wq_in.wait()
-    vrow[...] = jnp.zeros_like(vrow)
-    vrow[:8, :] = dv_ref[...]
-    for j in range(chunks):
-        vrow[8 + j : 9 + j, :] = dbin_ref[j]
+    for r in range(rows):
+        segf = seg_ref[r].astype(f32)
+        rep = jnp.broadcast_to(segf, (LANES, seq)).T
+        for k in range(seq // LANES):
+            sl = slice(k * LANES, (k + 1) * LANES)
+            gpool[0, r * seq : (r + 1) * seq, sl] = jnp.where(rep == segf[:, sl], 0.0, NEG)
     dsb[...] = jnp.zeros_like(dsb)
+    c_in.wait()
+    r1_in.wait()
+    n1_in.wait()
+    wo_in.wait()
+    g1 = vec_ref[0:1, :]
+    sel_shape = (delta.shape[0], width)
+    sel = jnp.where(lax.broadcasted_iota(jnp.int32, sel_shape, 0) == lax.broadcasted_iota(jnp.int32, sel_shape, 1) // HD, 1.0, 0.0).astype(bf16)
+
+    def norm_one_back(i):
+        at = pl.ds(pl.multiple_of(i * 256, 256), 256)
+        dy1 = acc[at, :]
+        n1 = gpool[1, at, :]
+        dn = dy1 * g1
+        r1 = r1b[at, :1]
+        dh1 = r1 * (dn - jnp.mean(dn, 1, keepdims=True) - n1 * jnp.mean(dn * n1, 1, keepdims=True))
+        acc[at, :] = dh1
+        da = dh1.astype(bf16)
+        dab[at, :] = da
+        dc = dot_nt(da, columns(wpool, 6, 7)).astype(bf16)
+        dcb[at, :] = dc
+        prod = dc.astype(f32) * cb[at, :].astype(f32)
+        hi = prod.astype(bf16)
+        lo = (prod - hi.astype(f32)).astype(bf16)
+        delta[:, at] = dot_nt(sel, hi) + dot_nt(sel, lo)
+        vrow[0:1, :] += colsum(dy1 * n1)
+        vrow[1:2, :] += colsum(dy1)
+        vrow[6:7, :] += colsum(da.astype(f32))
+
+    loop(tokens // 256, norm_one_back)
+    wq_in.start()
+    r_.turn(2 * chunks)
+    weight_grad(cb, dab[...], ff_pieces, 2)
+    r_.turn(2 * chunks + 1)
+    t0 = 2 * chunks + 2
+    x_in.wait()
     first = lax.broadcasted_iota(jnp.int32, (LANES, LANES), 1) < HD
     first_seq = lax.broadcasted_iota(jnp.int32, (seq, LANES), 1) < HD
 
     def pair(p):
         head = pl.ds(pl.multiple_of(p * LANES, LANES), LANES)
-        slot = lax.rem(p, 2)
+        col = pl.multiple_of(lax.rem(p, 2) * PIECE, LANES)
+        to = p // 2
         q_in(p).wait()
 
         def row(r):
             tok = pl.ds(pl.multiple_of(r * seq, seq), seq)
-            q2 = qb[slot, tok, :LANES]
-            k2 = qb[slot, tok, LANES : 2 * LANES]
-            v2 = qb[slot, tok, 2 * LANES :]
-            dc2 = stg[tok, head]
+            q2 = pool[3, tok, pl.ds(col, LANES)]
+            k2 = pool[3, tok, pl.ds(col + LANES, LANES)]
+            v2 = pool[3, tok, pl.ds(col + 2 * LANES, LANES)]
+            dc2 = dcb[tok, head]
             dqs = []
             for h in range(2):
                 lse = lse_ref[r, pl.ds(2 * p + h, 1), :]
-                dl = delta_ref[pl.ds(2 * p + h, 1), tok]
+                dl = delta[pl.ds(2 * p + h, 1), tok]
                 own = first if h == 0 else ~first
                 for c in range(seq // LANES):
                     lo, hi = key_range(c, seq, LANES)
                     cut = slice(c * LANES, (c + 1) * LANES)
+                    at = pl.ds(pl.multiple_of(r * seq + c * LANES, LANES), LANES)
                     km = jnp.where(own, k2[cut], jnp.zeros_like(k2[cut]))
                     vm_ = jnp.where(own, v2[cut], jnp.zeros_like(v2[cut]))
-                    pt = jnp.exp2((dot_nt(km, q2[lo:hi]) + bias[r, cut, lo:hi]) * SCALE2 - lse[:, lo:hi])
+                    pt = jnp.exp2((dot_nt(km, q2[lo:hi]) + gpool[0, at, lo:hi]) * SCALE2 - lse[:, lo:hi])
                     ds = (pt * (dot_nt(vm_, dc2[lo:hi]) - dl[:, lo:hi])).astype(bf16)
                     dsb[h, cut, lo:hi] = ds
                     dv = dot(pt.astype(bf16), dc2[lo:hi]).astype(bf16)
                     dk = (dot(ds, q2[lo:hi]) * 0.125).astype(bf16)
-                    at = pl.ds(pl.multiple_of(r * seq + c * LANES, LANES), LANES)
                     if h == 1:
-                        dv = jnp.where(first, dqb[p, at, 2 * LANES :], dv)
-                        dk = jnp.where(first, dqb[p, at, LANES : 2 * LANES], dk)
-                    dqb[p, at, 2 * LANES :] = dv
-                    dqb[p, at, LANES : 2 * LANES] = dk
+                        dv = jnp.where(first, pool[to, at, pl.ds(col + 2 * LANES, LANES)], dv)
+                        dk = jnp.where(first, pool[to, at, pl.ds(col + LANES, LANES)], dk)
+                    pool[to, at, pl.ds(col + 2 * LANES, LANES)] = dv
+                    pool[to, at, pl.ds(col + LANES, LANES)] = dk
                 dqs.append(dot_tn(dsb[h], k2) * 0.125)
-            dqb[p, tok, :LANES] = jnp.where(first_seq, dqs[0], dqs[1]).astype(bf16)
-            when(t0 + 3 * p + r <= ff_pieces + 2 + p - 1, lambda: r_.turn(t0 + 3 * p + r, consume))
+            pool[to, tok, pl.ds(col, LANES)] = jnp.where(first_seq, dqs[0], dqs[1]).astype(bf16)
+            when(r == 0, lambda: r_.turn(t0 + 2 * p))
 
         loop(rows, row)
         when(p + 2 < pairs, lambda: q_in(p + 2).start())
-        piece = ff_pieces + 2 + p
-
-        def product(a):
-            d = dot(lhs[pl.ds(pl.multiple_of(a * n_half, LANES), n_half), :], dqb[p])
-            for t in range(3):
-                part[piece, t, a] = d[:, t * LANES : (t + 1) * LANES].astype(bf16).reshape(2, 2, 2, own_rows, LANES)
-
-        loop(2, product)
-        r_.start(piece)
-        sums = jnp.sum(dqb[p].astype(f32), 0, keepdims=True)
+        d = pool[to, :, pl.ds(col, PIECE)]
+        weight_grad(x, d, ff_pieces + 2 + p, 1)
+        sums = colsum(d.astype(f32))
         vrow[4:5, head] = sums[:, :LANES]
         vrow[5:6, head] = sums[:, 2 * LANES :]
-        when(t0 + 3 * p + 2 <= piece, lambda: r_.turn(t0 + 3 * p + 2, consume))
+        r_.turn(t0 + 2 * p + 1)
 
     loop(pairs, pair)
-    return_turn = t0 + 3 * pairs
-    left_out = [t for p in range(pairs) for t, last in ((t0 + 3 * p, ff_pieces + 1 + p), (t0 + 3 * p + 1, ff_pieces + 1 + p), (t0 + 3 * p + 2, ff_pieces + 2 + p)) if t > last]
+    t0 += 2 * pairs
     cols = vrow[...].T.astype(bf16)
     part[pieces - 1, 0] = cols.reshape(2, 2, 2, 2, own_rows, LANES)
     part[pieces - 1, 1] = jnp.zeros_like(part[pieces - 1, 1])
     part[pieces - 1, 2] = jnp.zeros_like(part[pieces - 1, 2])
     r_.start(pieces - 1)
-    vrow[...] = jnp.zeros_like(vrow)
-    for t in left_out:
-        r_.turn(t, consume)
-    h_in = lambda i: pltpu.make_async_copy(dh1_hbm.at[pl.ds(pl.multiple_of(i * 256, 256), 256)], hb.at[lax.rem(i, 2)], sem_in.at[7 + pairs + i])
-    h_in(0).start()
-    h_in(1).start()
+    left = pieces - t0
+    loop(left, lambda i: r_.turn(t0 + i))
+    t0 += left
+    wq_in.wait()
     blocks = tokens // 256
-    gin = stg
 
     def gin_block(i):
         at = pl.ds(pl.multiple_of(i * 256, 256), 256)
-        h_in(i).wait()
-        d = jnp.concatenate([dqb[p, at, :] for p in range(pairs)], 1)
-        w = jnp.concatenate([tile(wq, p, t) for p in range(pairs) for t in range(3)], 1)
-        gin[at, :] = (hb[lax.rem(i, 2)] + dot_nt(d, w)).astype(bf16)
-        when(i + 2 < blocks, lambda: h_in(i + 2).start())
-        r_.turn(return_turn + i, consume)
+        d = jnp.concatenate([pool[k, at, :] for k in range(pairs // 2)], 1)
+        dcb[at, :] = (acc[at, :] + dot_nt(d, columns(wpool, *range(pairs)))).astype(bf16)
+        r_.turn(t0 + i)
 
     loop(blocks, gin_block)
-    gin_out = pltpu.make_async_copy(gin, gin_o, sem_out.at[6])
+    gin_out = pltpu.make_async_copy(dcb, gin_o, out_sem)
     gin_out.start()
-    rest = pieces + 5 * LAG - (return_turn + blocks)
-    loop(rest, lambda i: r_.turn(return_turn + blocks + i, consume))
-    outs = [pltpu.make_async_copy(s, d, sem_out.at[k]) for k, (s, d) in enumerate(
-        [(sa.at[0], am_o), (sa.at[1], aw_o), (sa.at[2], aa_o), (sd.at[0], dm_o), (sd.at[1], dw_o), (sd.at[2], da_o)])]
-    for c in outs:
-        c.start()
+    loop(5 * LAG - blocks, lambda i: r_.turn(t0 + blocks + i))
     loop(pieces, r_.sent)
     gin_out.wait()
-    for c in outs:
-        c.wait()
-
-
-def back(rates, x, c, y1, dz, da, g, du, qkv, dc, dh1, wq, seg, lse, delta, dv, dbin, states):
+
+
+def back(x, c, y1, dz, dh2, n1, r1, g, gp, qkv, w, seg, lse, dv, vec):
     rows, seq = seg.shape
     tokens, width = x.shape
     chunks = g.shape[0]
-    own_rows = states[0].shape[1]
+    own_rows = w.shape[-2]
     heads = width // HD
     pairs = heads // 2
     pieces = 4 * chunks + 2 + pairs + 1
@@ -1035,23 +993,86 @@
     hbm = pl.BlockSpec(memory_space=pl.ANY)
     vmem = pl.BlockSpec(memory_space=pltpu.VMEM)
     tail = (own_rows, LANES)
+    tok = v((tokens, width), bf16)
     scratch = [
         v((pieces, 3, 2, 2, 2, 2) + tail, bf16), v((pieces, 3, 2, 2, 2) + tail, bf16), v((pieces, 2, 2, 2) + tail, bf16),
         v((pieces, 2, 2, 2) + tail, bf16), v((pieces, 2, 2) + tail, bf16), v((pieces, 2) + tail, bf16), v((pieces, 2) + tail, bf16),
-        v((pieces, 2) + tail, bf16), v((tokens, width), bf16), v((2, tokens, width), bf16), v((width, tokens), bf16),
-        v((2, tokens, PIECE), bf16), v((pairs, tokens, PIECE), bf16), v(wq.shape, bf16), v((rows, seq, seq), f32),
-        v((2, seq, seq), bf16), v((2, 256, width), f32), v((3,) + states[0].shape, f32), v((3,) + states[3].shape, f32),
+        v((pieces, 2) + tail, bf16), v((5, tokens, width), bf16), v((8,) + w.shape[1:], bf16), v((2, tokens, width), f32),
+        v((tokens, width), f32), tok, tok, tok, v((tokens, LANES), f32), v((2, seq, seq), bf16), v((16, tokens), f32),
         v((LANES, width), f32),
-        dma((5 + 2 * chunks + 1,)), dma((7 + pairs + tokens // 256,)), dma((7,))] + [dma((pieces,))] * 12
+        dma((3 * chunks + 9 + pairs,)), dma(())] + [dma((pieces,))] * 12
     return pl.pallas_call(
-        functools.partial(back_kernel, heads, rates),
-        out_shape=(sh((tokens, width), bf16),) + tuple(sh(s.shape, f32) for s in states),
-        in_specs=[hbm] * 11 + [vmem] * 5 + [hbm] * 6 + [vmem] * 3,
-        out_specs=(hbm,) * 7 + (vmem,) * 3,
+        functools.partial(back_kernel, heads),
+        out_shape=(sh((tokens, width), bf16), sh((pieces, own_rows, PIECE), f32)),
+        in_specs=[hbm] * 11 + [vmem] * 4,
+        out_specs=(hbm, vmem),
         scratch_shapes=scratch,
-        compiler_params=pltpu.CompilerParams(collective_id=1, has_side_effects=True, vmem_limit_bytes=62 * 2**20),
+        compiler_params=pltpu.CompilerParams(collective_id=1, has_side_effects=True, vmem_limit_bytes=63 * 2**20),
         name="back",
-    )(x, c, y1, dz, da, g, du, qkv, dc, dh1, wq, seg.reshape(rows, 1, seq), lse, delta, dv, dbin, *states)
+    )(x, c, y1, dz, dh2, n1, r1, g, gp, qkv, w, seg.reshape(rows, 1, seq), lse, dv, vec)
+
+
+def update_kernel(rates, sum_ref, gin_ref, out_ref, am, aw, aa, dm, dw, da, vm, vw, va,
+                  gin_o, out_o, am_o, aw_o, aa_o, dm_o, dw_o, da_o, vm_o, vw_o, va_o, square):
+    matrix, vector, replicas = rates
+    j = pl.program_id(0)
+    gin_o[...] = gin_ref[...]
+    out_o[...] = out_ref[...]
+
+    def advance_to(grad, rate, ins, outs, index):
+        grad = grad / replicas
+        moment = momentum_decay * ins[0][index] + grad
+        weight = ins[1][index] - rate * (grad + momentum_decay * moment)
+        outs[0][index] = moment
+        outs[1][index] = weight
+        outs[2][index] = average_decay * ins[2][index] + (1.0 - average_decay) * weight
+
+    for k in range(4):
+        cols = slice(k % 2 * PIECE, (k % 2 + 1) * PIECE)
+        advance_to(sum_ref[4 * j + k], matrix, (dm, dw, da), (dm_o, dw_o, da_o), (1 - k // 2, slice(None), cols))
+    last = pl.num_programs(0) - 1
+    ff_pieces = sum_ref.shape[0] - 3 - am_o.shape[2] // LANES
+    pairs = am_o.shape[2] // LANES
+
+    @pl.when(j < last)
+    def _():
+        for p in range(pairs):
+            cols = slice(p * LANES, (p + 1) * LANES)
+            grad = sum_ref[ff_pieces + 2 + p, :, pl.ds(pl.multiple_of(j * LANES, LANES), LANES)]
+            advance_to(grad, matrix, (am, aw, aa), (am_o, aw_o, aa_o), (0, slice(None), cols))
+
+    @pl.when(j == last)
+    def _():
+        for k in range(2):
+            cols = slice(k * PIECE, (k + 1) * PIECE)
+            advance_to(sum_ref[ff_pieces + k], matrix, (am, aw, aa), (am_o, aw_o, aa_o), (0, slice(None), cols))
+        rows, own = vm.shape
+        square[...] = jnp.zeros_like(square)
+        square[:own, :] = sum_ref[ff_pieces + pairs + 2, :, :LANES]
+        every = (slice(None), slice(None))
+        advance_to(square[...].T[:rows, :own], vector, (vm, vw, va), (vm_o, vw_o, va_o), every)
+
+
+def update(rates, sums, gin, out, states):
+    am, dm, vm = states[0], states[3], states[6]
+    pieces, own_rows, _ = sums.shape
+    tokens, width = gin.shape
+    steps = am.shape[0]
+    chunks = dm.shape[2] // width
+    assert steps == chunks == 4
+    tok = pl.BlockSpec((tokens // steps, width), lambda j: (j, 0))
+    att = pl.BlockSpec((1, own_rows, width), lambda j: (j, 0, 0))
+    den = pl.BlockSpec((2, own_rows, width), lambda j: (0, 0, j))
+    vec = pl.BlockSpec(vm.shape, lambda j: (0, 0))
+    sh = jax.ShapeDtypeStruct
+    return pl.pallas_call(
+        functools.partial(update_kernel, rates), grid=(steps,),
+        out_shape=(sh(gin.shape, bf16), sh(out.shape, bf16)) + tuple(sh(s.shape, f32) for s in states),
+        in_specs=[pl.BlockSpec(sums.shape, lambda j: (0, 0, 0)), tok, tok] + [att] * 3 + [den] * 3 + [vec] * 3,
+        out_specs=(tok, tok) + (att,) * 3 + (den,) * 3 + (vec,) * 3,
+        scratch_shapes=[pltpu.VMEM((LANES, LANES), f32)],
+        name="update",
+    )(sums, gin, out, *states)
 
 
 def pack_columns(attention, dense, vectors):
@@ -1145,7 +1166,7 @@
     tokens_all = row_count * length * lax.axis_size("wide") * replicas
     grad_scale = math.sqrt(tokens_all) / replicas
     rates = (matrix_rate / grad_scale, vector_rate / grad_scale, replicas)
-    qkv, c, lse, wq, out, y1, g, dz, du, da, dc, dh1, delta, dv, dbin = stage(
+    qkv, c, lse, w, out, y1, g, gp, dz, dh2, n1, r1, dv, vec = stage(
         x, segment_ids, e, attention_weights, dense_weights, vector_params
     )
     states = (
@@ -1153,8 +1174,9 @@
         dense_momentum, dense_weights, dense_average,
         vector_momentum, vector_params, vector_average,
     )
-    news = back(rates, x, c, y1, dz, da, g, du, qkv, dc, dh1, wq, segment_ids, lse, delta, dv, dbin, states)
-    return (out.reshape(hidden_in.shape), news[0].reshape(hidden_in.shape)) + tuple(news[1:])
+    gin, sums = back(x, c, y1, dz, dh2, n1, r1, g, gp, qkv, w, segment_ids, lse, dv, vec)
+    news = update(rates, sums, gin, out, states)
+    return (news[1].reshape(hidden_in.shape), news[0].reshape(hidden_in.shape)) + tuple(news[2:])
 
 
 def solution(mesh):

time: 219 us -> 209 us (0.954)
  local copies, waits for them, and re-layouts: 12.7 us -> 1.28 us
    pallas_call x1 -> x2, Pallas kernels: 96.6 us -> 119 us  [the longest x1 111 us: back(): pl.pallas_call(functools.partial(back_kernel, heads), out_shape=(sh((toke...]
    pallas_call x1, Pallas kernels: 109 us -> 87.8 us  [stage(): pl.pallas_call(functools.partial(stage_kernel, heads), out_shape=(sh((pai...]
    unnamed x33 -> x0, local copies, waits for them, and re-layouts: 11.4 us -> none
where the time goes in v4:
time: 209 us
  Pallas kernels  207 us (99%)
    pallas_call x1, Pallas kernels, back(): pl.pallas_call(functools.partial(back_kernel, heads), out_shape=(sh((toke...  111 us
    pallas_call x1, Pallas kernels, stage(): pl.pallas_call(functools.partial(stage_kernel, heads), out_shape=(sh((pai...  87.8 us
    pallas_call x1, Pallas kernels, update(): pl.pallas_call(functools.partial(update_kernel, rates), grid=(steps,), ou...  8.09 us

profile of v4, /device:TPU:0, one launch (start us, length us, event | category | flops | bytes accessed | tf_op | source)
XLA Modules:
  0.0 208.8 jit_solution(11834722441069108559)
XLA Ops:
  0.6 1.3 reshape.39.seg_ref
  1.9 87.8 %stage.1 = (bf16[6,1024,384]{2,1,0:T(8,128)(2,1)}, bf16[1024,768]{1,0:T(8,128)(2,1)}, f32[2,16,512]{2,1,0:T(8,128)}, bf16[24,3,2,2,2,2,48,128]{7,6,5,4,3,2,1,0:T...) custom-call(bf16[1024,768]{1,0:T(8,128)(2,1)} %bitcast.4, ...), custom_call_target="tpu_custom_call" | custom-call | tf_op jit(solution)/shard_map/stage/pallas_call | solution.py:684
  89.7 110.8 %back.1 = (bf16[1024,768]{1,0:T(8,128)(2,1)}, f32[25,48,384]{2,1,0:T(8,128)}) custom-call(bf16[1024,768]{1,0:T(8,128)(2,1)} %bitcast.5, bf16[1024,768]{1,0:T(8,128)(2,1)} %get-tuple-element.38.c_hbm, bf16[1024,768]{1,0:T(8,128)(2,1)} %get-tuple-element.39.y1_hbm, bf16[1024,768]{1,0:T(8,128)(2,1)} %get-tuple-element.40.dz_hbm, ...), custom_call_target="tpu_custom_call" | custom-call | tf_op jit(solution)/shard_map/back/pallas_call | solution.py:1004
  200.5 8.1 %update.1 = (bf16[1024,768]{1,0:T(8,128)(2,1)}, bf16[1024,768]{1,0:T(8,128)(2,1)}, f32[4,48,768]{2,1,0:T(8,128)}, f32[4,48,768]{2,1,0:T(8,128)}, f32[4,48,768]{2...) custom-call(f32[25,48,384]{2,1,0:T(8,128)} %get-tuple-element.51.sum, ...), custom_call_target="tpu_custom_call" | custom-call | tf_op jit(solution)/shard_map/update/pallas_call | solution.py:1068

commit v5 on v4

--- a/solution.py
+++ b/solution.py
@@ -266,7 +266,8 @@
 
 LANES = 128
 PIECE = 3 * LANES
-LAG = 2
+GATHER_LAGS = (0, 2, 4, 6)
+REDUCE_LAGS = (0, 2, 4, 6, 8)
 AHEAD = 3
 MESH = pl.DeviceIdType.MESH
 
@@ -279,19 +280,28 @@
         self.y = lax.rem(self.w // 2, 2)
         self.b = lax.rem(self.w // 4, 2)
         self.a = self.w // 8
+        self.z = self.w // 4
+
+    def z_peer(self, k):
+        return lax.rem(self.z + k, 4)
 
     def over(self, name):
         if name == "x":
             return (self.w, 1 - self.x)
+        if name in (1, 2, 3):
+            return (4 * self.z_peer(name) + lax.rem(self.w, 4), self.x)
         step = {"a": 8, "b": 4, "y": 2, "core": 1}[name]
         return (self.w + step * (1 - 2 * getattr(self, name)), self.x)
 
-    def greet(self):
-        barrier = pltpu.get_barrier_semaphore()
-        names = ("a", "b", "y", "x", "core")
+    near = ("a", "b", "y", "x", "core")
+    reduce_peers = (1, 2, 3, "y", "x", "core")
+
+    def greet(self, names):
         for name in names:
-            pl.semaphore_signal(barrier, inc=1, device_id=self.over(name), device_id_type=MESH)
-        pl.semaphore_wait(barrier, len(names))
+            pl.semaphore_signal(pltpu.get_barrier_semaphore(), inc=1, device_id=self.over(name), device_id_type=MESH)
+
+    def met(self, names):
+        pl.semaphore_wait(pltpu.get_barrier_semaphore(), len(names))
 
 
 def remote(src, dst, send, recv, device):
@@ -369,8 +379,7 @@
         for k in range(2):
             ahead = AHEAD + 2 * t + k
             when(ahead < self.pieces, lambda ahead=ahead: self.start(ahead))
-        for lag, step in enumerate((self.b_step, self.y_step, self.x_step, self.core_step)):
-            lag = lag * LAG
+        for lag, step in zip(GATHER_LAGS, (self.b_step, self.y_step, self.x_step, self.core_step)):
             when((t >= lag) & (t < self.pieces + lag), lambda lag=lag, step=step: step(t - lag))
 
     def sent(self, i):
@@ -439,7 +448,7 @@
                  full, vfull, shard, vshard, square, xb, eb, cb, n1b, y1b, acc, gp, gb, dzb, bias, lsea, binr, r1b,
                  in_sem, out_sem, w_sem, *sems):
     place = Place()
-    rows, _, seq = seg_ref.shape
+    rows, seq = seg_ref.shape
     tokens, width = x_hbm.shape
     pairs = heads // 2
     pieces = shard.shape[0]
@@ -460,6 +469,7 @@
     e_load = pltpu.make_async_copy(e_hbm, eb, in_sem.at[n + 1])
     for c in loads:
         c.start()
+    place.greet(place.near)
     x_load.start()
     e_load.start()
     square[...] = jnp.zeros_like(square)
@@ -475,7 +485,7 @@
     for p in range(pairs):
         for t in range(3):
             shard[p, t] = own_tile(0, t, p)
-    place.greet()
+    place.met(place.near)
     gv.start()
     for i in range(AHEAD):
         g.start(i)
@@ -487,14 +497,14 @@
             for k in range(2):
                 shard[pairs + 2 + 4 * j + 2 * k + t // 3, t % 3] = own_tile(1 + k, j, t)
     for r in range(rows):
-        doc_bias(seg_ref[r], bias, r)
+        doc_bias(seg_ref[r : r + 1, :], bias, r)
     gv.step("a", "b")
-    fill = 3 * LAG + 1
+    fill = GATHER_LAGS[-1] + 1
     for t in range(fill):
         g.turn(t)
-        if t == LAG // 2:
+        if t == 1:
             gv.step("b", "y")
-        if t == 2 * LAG:
+        if t == 4:
             gv.step("y", "core")
     gv.arrive()
     vec = vfull[...].reshape(16 * own_rows, LANES).astype(f32).T
@@ -601,24 +611,29 @@
         return pltpu.make_async_copy(gp.at[j], gp_o.at[j], out_sem.at[pairs + 7 + chunks + j])
 
     def ff_chunk(j):
-        for t in range(4):
-            g.arrive(pairs + 2 + 4 * j + t)
-            w_out(pairs + 2 + 4 * j + t).start()
-
-        def ff_block(i):
+        def ready(k):
+            for t in (k, k + 1):
+                g.arrive(pairs + 2 + 4 * j + t)
+                w_out(pairs + 2 + 4 * j + t).start()
+
+        def up_block(i):
             at = pl.ds(pl.multiple_of(i * big, big), big)
-            u = dot(y1b[at, :], up(j)) + binr[j]
-            act, slope = gelu_parts(u)
-            gl = act.astype(bf16)
-            gb[j, at, :] = gl
+            act, slope = gelu_parts(dot(y1b[at, :], up(j)) + binr[j])
+            gb[j, at, :] = act.astype(bf16)
             gp[j, at, :] = slope
-            acc[at, :] += dot_nt(gl, down(j))
-            g.turn(done + 3 * j + i)
-
-        loop(tokens // big, ff_block)
-        g.turn(done + 3 * j + 2)
+            g.turn(done + 4 * j + i)
+
+        def down_block(i):
+            at = pl.ds(pl.multiple_of(i * big, big), big)
+            acc[at, :] += dot_nt(gb[j, at, :], down(j))
+            g.turn(done + 4 * j + 2 + i)
+
+        ready(0)
+        loop(tokens // big, up_block)
         g_out(j).start()
         gp_out(j).start()
+        ready(2)
+        loop(tokens // big, down_block)
 
     loop(chunks, ff_chunk)
     e_load.wait()
@@ -690,101 +705,104 @@
         scratch_shapes=scratch,
         compiler_params=pltpu.CompilerParams(collective_id=0, has_side_effects=True, vmem_limit_bytes=BIG),
         name="stage",
-    )(x, seg.reshape(rows, 1, seq), e, aw, dw, vp)
+    )(x, seg, e, aw, dw, vp)
 
 
 class Reduce:
-    names = ("core", "x", "y", "b", "a", "p")
-
-    def __init__(self, place, part, froms, done, out, sems, pieces):
-        self.p, self.part, self.done, self.out, self.pieces = place, part, done, out, pieces
-        self.froms = dict(zip(self.names, froms))
-        self.sems = {name: (sems[2 * k], sems[2 * k + 1]) for k, name in enumerate(self.names)}
-        self.own = pl.ds(place.x, 2)
+    def __init__(self, place, part, froms, done, out, sems, pieces, tiles=3):
+        self.p, self.part, self.done, self.out, self.pieces, self.whole = place, part, done, out, pieces, tiles == 1
+        self.names = ("core", "y", "p") if self.whole else ("core", "y", "p", "x")
+        self.froms = dict(zip(("core", "y", "p", "z", "x"), froms))
+        self.zs, self.zr = sems[:2]
+        self.sems = {name: (sems[2 + 2 * k], sems[3 + 2 * k]) for k, name in enumerate(self.names)}
+        self.own = pl.ds(0, 1) if self.whole else pl.ds(place.x, 2)
 
     def copy(self, name, i):
         p, f = self.p, self.part
         if name == "core":
-            src = f.at[i, :, :, :, :, 1 - p.core]
+            src = f.at[i, :, :, :, 1 - p.core]
         elif name == "x":
-            src = f.at[i, 2 * (1 - p.x), :, :, :, p.core]
+            src = f.at[i, 2 * (1 - p.x), :, :, p.core]
         elif name == "y":
-            src = f.at[i, self.own, :, :, 1 - p.y, p.core]
-        elif name == "b":
-            src = f.at[i, self.own, :, 1 - p.b, p.y, p.core]
-        elif name == "a":
-            src = f.at[i, self.own, 1 - p.a, p.b, p.y, p.core]
+            src = f.at[i, self.own, :, 1 - p.y, p.core]
         else:
             src = self.done.at[i]
         send, recv = self.sems[name]
         return remote(src, self.froms[name].at[i], send.at[i], recv.at[i], p.over("x" if name == "p" else name))
 
+    def z_copy(self, i, k, incoming=False):
+        p = self.p
+        peer = p.z_peer(k)
+        came = peer if incoming else p.z
+        return remote(self.part.at[i, self.own, peer, p.y, p.core], self.froms["z"].at[i, came], self.zs.at[i, k], self.zr.at[i, came], p.over(k))
+
     def start(self, i):
         self.copy("core", i).start()
 
     def x_step(self, i):
         p, f = self.p, self.part
         self.copy("core", i).wait_recv()
-        for t in range(3):
-            f[i, t, :, :, :, p.core] = f[i, t, :, :, :, p.core] + self.froms["core"][i, t]
-        self.copy("x", i).start()
+        for t in range(1 if self.whole else 3):
+            f[i, t, :, :, p.core] = f[i, t, :, :, p.core] + self.froms["core"][i, t]
+        self.copy("y" if self.whole else "x", i).start()
 
     def y_step(self, i):
         p, f = self.p, self.part
         self.copy("x", i).wait_recv()
-        f[i, 2 * p.x, :, :, :, p.core] = f[i, 2 * p.x, :, :, :, p.core] + self.froms["x"][i]
+        f[i, 2 * p.x, :, :, p.core] = f[i, 2 * p.x, :, :, p.core] + self.froms["x"][i]
         self.copy("y", i).start()
 
-    def b_step(self, i):
+    def z_step(self, i):
         p, f = self.p, self.part
         self.copy("y", i).wait_recv()
-        f[i, self.own, :, :, p.y, p.core] = f[i, self.own, :, :, p.y, p.core] + self.froms["y"][i]
-        self.copy("b", i).start()
-
-    def a_step(self, i):
-        p, f = self.p, self.part
-        self.copy("b", i).wait_recv()
-        f[i, self.own, :, p.b, p.y, p.core] = f[i, self.own, :, p.b, p.y, p.core] + self.froms["b"][i]
-        self.copy("a", i).start()
+        f[i, self.own, :, p.y, p.core] = f[i, self.own, :, p.y, p.core] + self.froms["y"][i]
+        for k in (2, 1, 3):
+            self.z_copy(i, k).start()
 
     def p_step(self, i):
         p, f = self.p, self.part
-        self.copy("a", i).wait_recv()
-        total = f[i, self.own, p.a, p.b, p.y, p.core].astype(f32) + self.froms["a"][i].astype(f32)
+        total = f[i, self.own, p.z, p.y, p.core].astype(f32)
+        for k in (1, 2, 3):
+            self.z_copy(i, k, True).wait_recv()
+            total += self.froms["z"][i, p.z_peer(k)].astype(f32)
         self.done[i] = total.astype(bf16)
         self.copy("p", i).start()
 
     def finish(self, i):
         self.copy("p", i).wait_recv()
         a, b = self.done[i].astype(f32), self.froms["p"][i].astype(f32)
+        if self.whole:
+            self.out[i] = a[0] + b[0]
+            return
         first = self.p.x == 0
         low, high = jnp.where(first, a, b), jnp.where(first, b, a)
         self.out[i] = jnp.concatenate([low[0], low[1] + high[0], high[1]], 1)
 
     def turn(self, t):
-        steps = (self.x_step, self.y_step, self.b_step, self.a_step, self.p_step, self.finish)
-        for lag, step in enumerate(steps):
-            lag = lag * LAG
+        for lag, step in zip(REDUCE_LAGS, (self.x_step, self.y_step, self.z_step, self.p_step, self.finish)):
             when((t >= lag) & (t < self.pieces + lag), lambda lag=lag, step=step: step(t - lag))
 
     def sent(self, i):
         for name in self.names:
             self.copy(name, i).wait_send()
+        for k in (1, 2, 3):
+            self.z_copy(i, k).wait_send()
 
 
 def back_kernel(heads, x_hbm, c_hbm, y1_hbm, dz_hbm, dh2_hbm, n1_hbm, r1_hbm, g_hbm, gp_hbm, qkv_hbm, w_hbm,
-                seg_ref, lse_ref, dv_ref, vec_ref, gin_o, sum_o,
-                part, fromc, fromx, fromy, fromb, froma, fromp, done, pool, wpool, gpool, acc, cb, dab, dcb, r1b, dsb, delta, vrow,
+                seg_ref, lse_ref, dv_ref, vec_ref, gin_o, sum_o, vsum_o,
+                part, fromc, fromy, fromp, fromz, fromx, done, vpart, vfromc, vfromy, vfromp, vfromz, vdone, pool, wpool, gpool, acc, cb, dab, dcb, r1b, delta, vrow,
                 ld, out_sem, *sems):
     place = Place()
-    rows, _, seq = seg_ref.shape
+    rows, seq = seg_ref.shape
     tokens, width = x_hbm.shape
     pairs = heads // 2
     chunks = g_hbm.shape[0]
     own_rows = part.shape[-2]
     pieces = part.shape[0]
     big = 512
-    r_ = Reduce(place, part, (fromc, fromx, fromy, fromb, froma, fromp), done, sum_o, sems, pieces)
+    r_ = Reduce(place, part, (fromc, fromy, fromp, fromz, fromx), done, sum_o, sems[:10], pieces)
+    rv = Reduce(place, vpart, (vfromc, vfromy, vfromp, vfromz), vdone, vsum_o, sems[10:], 1, 1)
     ff_pieces = 4 * chunks
     first_ff = pairs + 2
     du, dz, y1 = pool.at[2], pool.at[3], pool.at[4]
@@ -800,18 +818,19 @@
     dz_in, y1_in, acc_in, c_in, r1_in = (load(base + k, s, d) for k, (s, d) in enumerate(
         ((dz_hbm, dz), (y1_hbm, y1), (dh2_hbm, acc), (c_hbm, cb), (r1_hbm, r1b))))
     base += 5
-    n1_in = load(base, n1_hbm, gpool.at[1])
-    wo_in = load(base + 1, w_hbm.at[pl.ds(pairs, 2)], wpool.at[pl.ds(6, 2)])
-    wq_in = load(base + 2, w_hbm.at[pl.ds(0, pairs)], wpool.at[pl.ds(0, pairs)])
+    n1_in = load(base, n1_hbm, gpool.at[0])
+    wo_in = load(base + 1, w_hbm.at[pl.ds(pairs, 2)], wpool.at[pl.ds(0, 2)])
+    wq_in = load(base + 2, w_hbm.at[pl.ds(0, pairs)], wpool.at[pl.ds(2, pairs)])
     x_in = load(base + 3, x_hbm, x)
     base += 4
 
     def q_in(p):
         return load(base + p, qkv_hbm.at[p], pool.at[3, :, pl.ds(pl.multiple_of(lax.rem(p, 2) * PIECE, LANES), PIECE)])
 
-    for c in (dz_in, g_in[0], gp_in[0], w_in[0], y1_in, acc_in, g_in[1], gp_in[1], w_in[1], c_in, r1_in):
+    for c in (dz_in, g_in[0]):
         c.start()
-    place.greet()
+    place.greet(place.reduce_peers)
+    place.met(place.reduce_peers)
     vrow[...] = jnp.zeros_like(vrow)
     vrow[:8, :] = dv_ref[...]
 
@@ -824,7 +843,7 @@
         def product(a):
             d = dot_tn(left[:, pl.ds(pl.multiple_of(a * half, LANES), half)], right)
             for t in range(3 * count):
-                part[piece + t // 3, t % 3, a] = d[:, t * LANES : (t + 1) * LANES].astype(bf16).reshape(2, 2, 2, own_rows, LANES)
+                part[piece + t // 3, t % 3, pl.ds(2 * a, 2)] = d[:, t * LANES : (t + 1) * LANES].astype(bf16).reshape(2, 2, 2, own_rows, LANES)
 
         loop(2, product)
         for k in range(count):
@@ -834,8 +853,11 @@
     for j in range(chunks):
         s = j % 2
         g_in[j].wait()
+        if j == 0:
+            for c in (gp_in[0], w_in[0], acc_in, y1_in, g_in[1], gp_in[1], w_in[1], c_in, r1_in):
+                c.start()
         weight_grad(dz, pool[s], 4 * j, 2)
-        r_.turn(2 * j)
+        r_.turn(3 * j)
         gp_in[j].wait()
         w_in[j].wait()
         if j == 0:
@@ -850,24 +872,26 @@
             vrow[8 + j : 9 + j, :] += colsum(d.astype(f32))
 
         loop(tokens // big, block)
+        r_.turn(3 * j + 1)
         if j + 2 < chunks:
             g_in[j + 2].start()
             gp_in[j + 2].start()
             w_in[j + 2].start()
+        if j == chunks - 2:
+            n1_in.start()
+            wo_in.start()
         weight_grad(y1, du[...], 4 * j + 2, 2)
-        r_.turn(2 * j + 1)
-    n1_in.start()
-    wo_in.start()
+        r_.turn(3 * j + 2)
+    wq_in.start()
     x_in.start()
     q_in(0).start()
     q_in(1).start()
     for r in range(rows):
-        segf = seg_ref[r].astype(f32)
+        segf = seg_ref[r : r + 1, :].astype(f32)
         rep = jnp.broadcast_to(segf, (LANES, seq)).T
         for k in range(seq // LANES):
             sl = slice(k * LANES, (k + 1) * LANES)
-            gpool[0, r * seq : (r + 1) * seq, sl] = jnp.where(rep == segf[:, sl], 0.0, NEG)
-    dsb[...] = jnp.zeros_like(dsb)
+            gpool[1, r * seq : (r + 1) * seq, sl] = jnp.where(rep == segf[:, sl], 0.0, NEG)
     c_in.wait()
     r1_in.wait()
     n1_in.wait()
@@ -879,14 +903,14 @@
     def norm_one_back(i):
         at = pl.ds(pl.multiple_of(i * 256, 256), 256)
         dy1 = acc[at, :]
-        n1 = gpool[1, at, :]
+        n1 = gpool[0, at, :]
         dn = dy1 * g1
         r1 = r1b[at, :1]
         dh1 = r1 * (dn - jnp.mean(dn, 1, keepdims=True) - n1 * jnp.mean(dn * n1, 1, keepdims=True))
         acc[at, :] = dh1
         da = dh1.astype(bf16)
         dab[at, :] = da
-        dc = dot_nt(da, columns(wpool, 6, 7)).astype(bf16)
+        dc = dot_nt(da, columns(wpool, 0, 1)).astype(bf16)
         dcb[at, :] = dc
         prod = dc.astype(f32) * cb[at, :].astype(f32)
         hi = prod.astype(bf16)
@@ -897,13 +921,12 @@
         vrow[6:7, :] += colsum(da.astype(f32))
 
     loop(tokens // 256, norm_one_back)
-    wq_in.start()
-    r_.turn(2 * chunks)
+    r_.turn(3 * chunks)
     weight_grad(cb, dab[...], ff_pieces, 2)
-    r_.turn(2 * chunks + 1)
-    t0 = 2 * chunks + 2
+    r_.turn(3 * chunks + 1)
+    t0 = 3 * chunks + 2
+    twice = ff_pieces + 2 - t0
     x_in.wait()
-    first = lax.broadcasted_iota(jnp.int32, (LANES, LANES), 1) < HD
     first_seq = lax.broadcasted_iota(jnp.int32, (seq, LANES), 1) < HD
 
     def pair(p):
@@ -918,30 +941,20 @@
             k2 = pool[3, tok, pl.ds(col + LANES, LANES)]
             v2 = pool[3, tok, pl.ds(col + 2 * LANES, LANES)]
             dc2 = dcb[tok, head]
-            dqs = []
+            zero = jnp.zeros_like(k2)
+            near = gpool[1, tok, :seq]
+            grads = []
             for h in range(2):
                 lse = lse_ref[r, pl.ds(2 * p + h, 1), :]
                 dl = delta[pl.ds(2 * p + h, 1), tok]
-                own = first if h == 0 else ~first
-                for c in range(seq // LANES):
-                    lo, hi = key_range(c, seq, LANES)
-                    cut = slice(c * LANES, (c + 1) * LANES)
-                    at = pl.ds(pl.multiple_of(r * seq + c * LANES, LANES), LANES)
-                    km = jnp.where(own, k2[cut], jnp.zeros_like(k2[cut]))
-                    vm_ = jnp.where(own, v2[cut], jnp.zeros_like(v2[cut]))
-                    pt = jnp.exp2((dot_nt(km, q2[lo:hi]) + gpool[0, at, lo:hi]) * SCALE2 - lse[:, lo:hi])
-                    ds = (pt * (dot_nt(vm_, dc2[lo:hi]) - dl[:, lo:hi])).astype(bf16)
-                    dsb[h, cut, lo:hi] = ds
-                    dv = dot(pt.astype(bf16), dc2[lo:hi]).astype(bf16)
-                    dk = (dot(ds, q2[lo:hi]) * 0.125).astype(bf16)
-                    if h == 1:
-                        dv = jnp.where(first, pool[to, at, pl.ds(col + 2 * LANES, LANES)], dv)
-                        dk = jnp.where(first, pool[to, at, pl.ds(col + LANES, LANES)], dk)
-                    pool[to, at, pl.ds(col + 2 * LANES, LANES)] = dv
-                    pool[to, at, pl.ds(col + LANES, LANES)] = dk
-                dqs.append(dot_tn(dsb[h], k2) * 0.125)
-            pool[to, tok, pl.ds(col, LANES)] = jnp.where(first_seq, dqs[0], dqs[1]).astype(bf16)
-            when(r == 0, lambda: r_.turn(t0 + 2 * p))
+                own = first_seq if h == 0 else ~first_seq
+                pt = jnp.exp2((dot_nt(jnp.where(own, k2, zero), q2) + near) * SCALE2 - lse)
+                ds = (pt * (dot_nt(jnp.where(own, v2, zero), dc2) - dl)).astype(bf16)
+                dv = dot(pt.astype(bf16), dc2)
+                grads.append((dot_tn(ds, k2) * 0.125, dot(ds, q2) * 0.125, dv))
+            for k, (a, b) in enumerate(zip(*grads)):
+                pool[to, tok, pl.ds(col + k * LANES, LANES)] = jnp.where(first_seq, a, b).astype(bf16)
+            when((r == 0) & (p < twice), lambda: r_.turn(t0 + 2 * p))
 
         loop(rows, row)
         when(p + 2 < pairs, lambda: q_in(p + 2).start())
@@ -950,15 +963,12 @@
         sums = colsum(d.astype(f32))
         vrow[4:5, head] = sums[:, :LANES]
         vrow[5:6, head] = sums[:, 2 * LANES :]
-        r_.turn(t0 + 2 * p + 1)
+        r_.turn(t0 + p + jnp.minimum(p + 1, twice))
 
     loop(pairs, pair)
-    t0 += 2 * pairs
-    cols = vrow[...].T.astype(bf16)
-    part[pieces - 1, 0] = cols.reshape(2, 2, 2, 2, own_rows, LANES)
-    part[pieces - 1, 1] = jnp.zeros_like(part[pieces - 1, 1])
-    part[pieces - 1, 2] = jnp.zeros_like(part[pieces - 1, 2])
-    r_.start(pieces - 1)
+    t0 += pairs + twice
+    vpart[0, 0] = vrow[...].T.astype(bf16).reshape(4, 2, 2, own_rows, LANES)
+    rv.start(0)
     left = pieces - t0
     loop(left, lambda i: r_.turn(t0 + i))
     t0 += left
@@ -968,14 +978,19 @@
     def gin_block(i):
         at = pl.ds(pl.multiple_of(i * 256, 256), 256)
         d = jnp.concatenate([pool[k, at, :] for k in range(pairs // 2)], 1)
-        dcb[at, :] = (acc[at, :] + dot_nt(d, columns(wpool, *range(pairs)))).astype(bf16)
+        dcb[at, :] = (acc[at, :] + dot_nt(d, columns(wpool, *range(2, 2 + pairs)))).astype(bf16)
         r_.turn(t0 + i)
+        for k, step in ((0, rv.x_step), (2, rv.z_step)):
+            when(i == k, lambda step=step: step(0))
 
     loop(blocks, gin_block)
     gin_out = pltpu.make_async_copy(dcb, gin_o, out_sem)
     gin_out.start()
-    loop(5 * LAG - blocks, lambda i: r_.turn(t0 + blocks + i))
+    rv.p_step(0)
+    loop(REDUCE_LAGS[-1] - blocks, lambda i: r_.turn(t0 + blocks + i))
+    rv.finish(0)
     loop(pieces, r_.sent)
+    rv.sent(0)
     gin_out.wait()
 
 
@@ -986,7 +1001,7 @@
     own_rows = w.shape[-2]
     heads = width // HD
     pairs = heads // 2
-    pieces = 4 * chunks + 2 + pairs + 1
+    pieces = 4 * chunks + 2 + pairs
     sh = jax.ShapeDtypeStruct
     dma = pltpu.SemaphoreType.DMA
     v = pltpu.VMEM
@@ -995,84 +1010,91 @@
     tail = (own_rows, LANES)
     tok = v((tokens, width), bf16)
     scratch = [
-        v((pieces, 3, 2, 2, 2, 2) + tail, bf16), v((pieces, 3, 2, 2, 2) + tail, bf16), v((pieces, 2, 2, 2) + tail, bf16),
-        v((pieces, 2, 2, 2) + tail, bf16), v((pieces, 2, 2) + tail, bf16), v((pieces, 2) + tail, bf16), v((pieces, 2) + tail, bf16),
-        v((pieces, 2) + tail, bf16), v((5, tokens, width), bf16), v((8,) + w.shape[1:], bf16), v((2, tokens, width), f32),
-        v((tokens, width), f32), tok, tok, tok, v((tokens, LANES), f32), v((2, seq, seq), bf16), v((16, tokens), f32),
+        v((pieces, 3, 4, 2, 2) + tail, bf16), v((pieces, 3, 4, 2) + tail, bf16), v((pieces, 2, 4) + tail, bf16), v((pieces, 2) + tail, bf16),
+        v((pieces, 4, 2) + tail, bf16), v((pieces, 4, 2) + tail, bf16), v((pieces, 2) + tail, bf16),
+        v((1, 1, 4, 2, 2) + tail, bf16), v((1, 1, 4, 2) + tail, bf16), v((1, 1, 4) + tail, bf16), v((1, 1) + tail, bf16),
+        v((1, 4, 1) + tail, bf16), v((1, 1) + tail, bf16), v((5, tokens, width), bf16), v((8,) + w.shape[1:], bf16), v((2, tokens, width), f32),
+        v((tokens, width), f32), tok, tok, tok, v((tokens, LANES), f32), v((16, tokens), f32),
         v((LANES, width), f32),
-        dma((3 * chunks + 9 + pairs,)), dma(())] + [dma((pieces,))] * 12
+        dma((3 * chunks + 9 + pairs,)), dma(())] + [dma((pieces, 4))] * 2 + [dma((pieces,))] * 8 + [dma((1, 4))] * 2 + [dma((1,))] * 6
     return pl.pallas_call(
         functools.partial(back_kernel, heads),
-        out_shape=(sh((tokens, width), bf16), sh((pieces, own_rows, PIECE), f32)),
+        out_shape=(sh((tokens, width), bf16), sh((pieces, own_rows, PIECE), f32), sh((1, own_rows, LANES), f32)),
         in_specs=[hbm] * 11 + [vmem] * 4,
-        out_specs=(hbm, vmem),
+        out_specs=(hbm, vmem, vmem),
         scratch_shapes=scratch,
         compiler_params=pltpu.CompilerParams(collective_id=1, has_side_effects=True, vmem_limit_bytes=63 * 2**20),
         name="back",
-    )(x, c, y1, dz, dh2, n1, r1, g, gp, qkv, w, seg.reshape(rows, 1, seq), lse, dv, vec)
-
-
-def update_kernel(rates, sum_ref, gin_ref, out_ref, am, aw, aa, dm, dw, da, vm, vw, va,
-                  gin_o, out_o, am_o, aw_o, aa_o, dm_o, dw_o, da_o, vm_o, vw_o, va_o, square):
+    )(x, c, y1, dz, dh2, n1, r1, g, gp, qkv, w, seg, lse, dv, vec)
+
+
+def update_kernel(rates, sum_ref, vsum_ref, gin_hbm, out_hbm, am, aw, aa, dm, dw, da, vm, vw, va,
+                  gin_o, out_o, am_o, aw_o, aa_o, dm_o, dw_o, da_o, vm_o, vw_o, va_o, square, tok, att, den, ld, st):
     matrix, vector, replicas = rates
-    j = pl.program_id(0)
-    gin_o[...] = gin_ref[...]
-    out_o[...] = out_ref[...]
-
-    def advance_to(grad, rate, ins, outs, index):
+    moves = [(dm, den.at[0], dm_o), (dw, den.at[1], dw_o), (da, den.at[2], da_o), (am, att.at[0], am_o), (aw, att.at[1], aw_o),
+             (aa, att.at[2], aa_o), (gin_hbm, tok.at[0], gin_o), (out_hbm, tok.at[1], out_o)]
+    loads = [pltpu.make_async_copy(s, d, ld.at[k]) for k, (s, d, _) in enumerate(moves)]
+    stores = [pltpu.make_async_copy(d, o, st.at[k]) for k, (_, d, o) in enumerate(moves)]
+    for c in loads:
+        c.start()
+
+    def advance(grad, rate, moment, weight, average):
         grad = grad / replicas
-        moment = momentum_decay * ins[0][index] + grad
-        weight = ins[1][index] - rate * (grad + momentum_decay * moment)
-        outs[0][index] = moment
-        outs[1][index] = weight
-        outs[2][index] = average_decay * ins[2][index] + (1.0 - average_decay) * weight
-
-    for k in range(4):
-        cols = slice(k % 2 * PIECE, (k % 2 + 1) * PIECE)
-        advance_to(sum_ref[4 * j + k], matrix, (dm, dw, da), (dm_o, dw_o, da_o), (1 - k // 2, slice(None), cols))
-    last = pl.num_programs(0) - 1
-    ff_pieces = sum_ref.shape[0] - 3 - am_o.shape[2] // LANES
-    pairs = am_o.shape[2] // LANES
-
-    @pl.when(j < last)
-    def _():
-        for p in range(pairs):
-            cols = slice(p * LANES, (p + 1) * LANES)
-            grad = sum_ref[ff_pieces + 2 + p, :, pl.ds(pl.multiple_of(j * LANES, LANES), LANES)]
-            advance_to(grad, matrix, (am, aw, aa), (am_o, aw_o, aa_o), (0, slice(None), cols))
-
-    @pl.when(j == last)
-    def _():
-        for k in range(2):
-            cols = slice(k * PIECE, (k + 1) * PIECE)
-            advance_to(sum_ref[ff_pieces + k], matrix, (am, aw, aa), (am_o, aw_o, aa_o), (0, slice(None), cols))
-        rows, own = vm.shape
-        square[...] = jnp.zeros_like(square)
-        square[:own, :] = sum_ref[ff_pieces + pairs + 2, :, :LANES]
-        every = (slice(None), slice(None))
-        advance_to(square[...].T[:rows, :own], vector, (vm, vw, va), (vm_o, vw_o, va_o), every)
-
-
-def update(rates, sums, gin, out, states):
-    am, dm, vm = states[0], states[3], states[6]
-    pieces, own_rows, _ = sums.shape
-    tokens, width = gin.shape
-    steps = am.shape[0]
-    chunks = dm.shape[2] // width
-    assert steps == chunks == 4
-    tok = pl.BlockSpec((tokens // steps, width), lambda j: (j, 0))
-    att = pl.BlockSpec((1, own_rows, width), lambda j: (j, 0, 0))
-    den = pl.BlockSpec((2, own_rows, width), lambda j: (0, 0, j))
-    vec = pl.BlockSpec(vm.shape, lambda j: (0, 0))
+        moment = momentum_decay * moment + grad
+        weight = weight - rate * (grad + momentum_decay * moment)
+        return moment, weight, average_decay * average + (1.0 - average_decay) * weight
+
+    def advance_in(grad, ref, index):
+        news = advance(grad, matrix, *(ref[(k,) + index] for k in range(3)))
+        for k in range(3):
+            ref[(k,) + index] = news[k]
+
+    rows, own = vm.shape
+    square[...] = jnp.zeros_like(square)
+    square[:own, :] = vsum_ref[0]
+    vm_o[...], vw_o[...], va_o[...] = advance(square[...].T[:rows, :own], vector, vm[...], vw[...], va[...])
+    every = slice(None)
+    pairs = att.shape[3] // LANES
+    ff_pieces = sum_ref.shape[0] - 2 - pairs
+    for c in loads[:3]:
+        c.wait()
+    for i in range(ff_pieces):
+        col = i // 4 * 2 * PIECE + i % 2 * PIECE
+        advance_in(sum_ref[i], den, (1 - i % 4 // 2, every, slice(col, col + PIECE)))
+    for c in stores[:3]:
+        c.start()
+    for c in loads[3:6]:
+        c.wait()
+    for i in range(2):
+        advance_in(sum_ref[ff_pieces + i], att, (3, every, slice(i * PIECE, (i + 1) * PIECE)))
+    for p in range(pairs):
+        for k in range(3):
+            advance_in(sum_ref[ff_pieces + 2 + p, :, k * LANES : (k + 1) * LANES], att, (k, every, slice(p * LANES, (p + 1) * LANES)))
+    for c in loads[6:]:
+        c.wait()
+    for c in stores[3:]:
+        c.start()
+    for c in stores:
+        c.wait()
+
+
+def update(rates, sums, vsums, gin, out, states):
+    am, dm = states[0], states[3]
     sh = jax.ShapeDtypeStruct
+    v = pltpu.VMEM
+    hbm = pl.BlockSpec(memory_space=pl.ANY)
+    vmem = pl.BlockSpec(memory_space=pltpu.VMEM)
+    places = [hbm] * 8 + [vmem] * 3
     return pl.pallas_call(
-        functools.partial(update_kernel, rates), grid=(steps,),
+        functools.partial(update_kernel, rates),
         out_shape=(sh(gin.shape, bf16), sh(out.shape, bf16)) + tuple(sh(s.shape, f32) for s in states),
-        in_specs=[pl.BlockSpec(sums.shape, lambda j: (0, 0, 0)), tok, tok] + [att] * 3 + [den] * 3 + [vec] * 3,
-        out_specs=(tok, tok) + (att,) * 3 + (den,) * 3 + (vec,) * 3,
-        scratch_shapes=[pltpu.VMEM((LANES, LANES), f32)],
+        in_specs=[vmem, vmem] + places,
+        out_specs=tuple(places),
+        scratch_shapes=[v((LANES, LANES), f32), v((2,) + gin.shape, bf16), v((3,) + am.shape, f32), v((3,) + dm.shape, f32),
+                        pltpu.SemaphoreType.DMA((8,)), pltpu.SemaphoreType.DMA((8,))],
+        compiler_params=pltpu.CompilerParams(vmem_limit_bytes=BIG),
         name="update",
-    )(sums, gin, out, *states)
+    )(sums, vsums, gin, out, *states)
 
 
 def pack_columns(attention, dense, vectors):
@@ -1174,8 +1196,8 @@
         dense_momentum, dense_weights, dense_average,
         vector_momentum, vector_params, vector_average,
     )
-    gin, sums = back(x, c, y1, dz, dh2, n1, r1, g, gp, qkv, w, segment_ids, lse, dv, vec)
-    news = update(rates, sums, gin, out, states)
+    gin, sums, vsums = back(x, c, y1, dz, dh2, n1, r1, g, gp, qkv, w, segment_ids, lse, dv, vec)
+    news = update(rates, sums, vsums, gin, out, states)
     return (news[1].reshape(hidden_in.shape), news[0].reshape(hidden_in.shape)) + tuple(news[2:])
 
 

time: 209 us -> 199 us (0.952)
  Pallas kernels: 207 us -> 198 us
    pallas_call x1, Pallas kernels: 111 us -> 100 us  [back(): pl.pallas_call(functools.partial(back_kernel, heads), out_shape=(sh((toke...]
where the time goes in v5:
time: 199 us
  Pallas kernels  198 us (99%)
    pallas_call x1, Pallas kernels, back(): pl.pallas_call(functools.partial(back_kernel, heads), out_shape=(sh((toke...  100 us
    pallas_call x1, Pallas kernels, stage(): pl.pallas_call(functools.partial(stage_kernel, heads), out_shape=(sh((pai...  89.3 us
    pallas_call x1, Pallas kernels, update(): pl.pallas_call(functools.partial(update_kernel, rates), out_shape=(sh(gin...  8.17 us

profile of v5, /device:TPU:0, one launch (start us, length us, event | category | flops | bytes accessed | tf_op | source)
XLA Modules:
  0.0 198.6 jit_solution(534776059653645533)
XLA Ops:
  0.6 89.3 %stage.1 = (bf16[6,1024,384]{2,1,0:T(8,128)(2,1)}, bf16[1024,768]{1,0:T(8,128)(2,1)}, f32[2,16,512]{2,1,0:T(8,128)}, bf16[24,3,2,2,2,2,48,128]{7,6,5,4,3,2,1,0:T...) custom-call(bf16[1024,768]{1,0:T(8,128)(2,1)} %bitcast.4, ...), custom_call_target="tpu_custom_call" | custom-call | tf_op jit(solution)/shard_map/stage/pallas_call | solution.py:699
  90.0 100.3 %back.1 = (bf16[1024,768]{1,0:T(8,128)(2,1)}, f32[24,48,384]{2,1,0:T(8,128)}, f32[1,48,128]{2,1,0:T(8,128)}) custom-call(bf16[1024,768]{1,0:T(8,128)(2,1)} %bitcast.5, bf16[1024,768]{1,0:T(8,128)(2,1)} %get-tuple-element.39.c_hbm, bf16[1024,768]{1,0:T(8,128)(2,1)} %get-tuple-element.40.y1_hbm, bf16[1024,768]{1,0:T(8,128)(2,1)} %get-tuple-element.41.dz_hbm, ...), custom_call_target="tpu_custom_call" | custom-call | tf_op jit(solution)/shard_map/back/pallas_call | solution.py:1020
  190.3 8.2 %update.1 = (bf16[1024,768]{1,0:T(8,128)(2,1)}, bf16[1024,768]{1,0:T(8,128)(2,1)}, f32[4,48,768]{2,1,0:T(8,128)}, f32[4,48,768]{2,1,0:T(8,128)}, f32[4,48,768]{2...) custom-call(f32[24,48,384]{2,1,0:T(8,128)} %get-tuple-element.52.sum, ...), custom_call_target="tpu_custom_call" | custom-call | tf_op jit(solution)/shard_map/update/pallas_call | solution.py:1088

commit v6 on v5

--- a/solution.py
+++ b/solution.py
@@ -446,7 +446,7 @@
 def stage_kernel(heads, x_hbm, seg_ref, e_hbm, aw_hbm, dw_hbm, vp_ref,
                  qkv_o, c_o, lse_o, w_o, out_o, y1_o, g_o, gp_o, dz_o, dh2_o, n1_o, r1_o, dv_o, vrow,
                  full, vfull, shard, vshard, square, xb, eb, cb, n1b, y1b, acc, gp, gb, dzb, bias, lsea, binr, r1b,
-                 in_sem, out_sem, w_sem, *sems):
+                 in_sem, out_sem, w_sem, two_sem, *sems):
     place = Place()
     rows, seq = seg_ref.shape
     tokens, width = x_hbm.shape
@@ -659,15 +659,25 @@
         dv_o[3:4, :] += colsum(e)
         dv_o[7:8, :] += colsum(dz.astype(f32))
 
-    loop(tokens // blk, norm_two)
-    last = [pltpu.make_async_copy(s, d, out_sem.at[pairs + k]) for k, (s, d) in ((3, (xb, out_o)), (4, (dzb, dz_o)), (6, (acc, dh2_o)))]
-    for c in last:
-        c.start()
+    def norm_two_out(i):
+        at = block(i)
+        pairs_of = ((xb, out_o), (dzb, dz_o), (acc, dh2_o))
+        return [pltpu.make_async_copy(src.at[at], dst.at[at], two_sem.at[k, i]) for k, (src, dst) in enumerate(pairs_of)]
+
+    def norm_two_step(i):
+        norm_two(i)
+        for c in norm_two_out(i):
+            c.start()
+
+    loop(tokens // blk, norm_two_step)
     gv.sent()
     loop(pieces, g.sent)
     loop(pieces, lambda i: w_out(i).wait())
-    for c in [c_out, y1_out, n1_out, r1_out] + last:
+    for c in [c_out, y1_out, n1_out, r1_out]:
         c.wait()
+    for i in range(tokens // blk):
+        for c in norm_two_out(i):
+            c.wait()
     loop(chunks, lambda j: g_out(j).wait())
     loop(chunks, lambda j: gp_out(j).wait())
 
@@ -694,7 +704,7 @@
         v((tokens, width), f32), v((tokens, width), bf16), v((tokens, width), f32), v((chunks, tokens, width), f32),
         v((chunks, tokens, width), bf16), v((tokens, width), bf16), v((rows, seq, seq), f32), v((rows, seq, LANES), f32),
         v((chunks, 1, width), f32), v((tokens, LANES), f32),
-        dma((6 + 2 * chunks,)), dma((pairs + 7 + 2 * chunks,)), dma((pieces,)),
+        dma((6 + 2 * chunks,)), dma((pairs + 7 + 2 * chunks,)), dma((pieces,)), dma((3, tokens // 256)),
     ] + [dma((pieces,))] * 11 + [dma(())] * 9
     return pl.pallas_call(
         functools.partial(stage_kernel, heads),
@@ -711,24 +721,30 @@
 class Reduce:
     def __init__(self, place, part, froms, done, out, sems, pieces, tiles=3):
         self.p, self.part, self.done, self.out, self.pieces, self.whole = place, part, done, out, pieces, tiles == 1
-        self.names = ("core", "y", "p") if self.whole else ("core", "y", "p", "x")
-        self.froms = dict(zip(("core", "y", "p", "z", "x"), froms))
+        self.names = ("core", "y", "p") if self.whole else ("core", "y", "p", "x", "early_y", "late_x")
+        self.froms = dict(zip(("core", "y", "p", "z", "x", "early_y"), froms))
         self.zs, self.zr = sems[:2]
         self.sems = {name: (sems[2 + 2 * k], sems[3 + 2 * k]) for k, name in enumerate(self.names)}
         self.own = pl.ds(0, 1) if self.whole else pl.ds(place.x, 2)
+        self.most = slice(None) if self.whole else pl.ds(0, 3)
 
     def copy(self, name, i):
-        p, f = self.p, self.part
+        p, f, landing = self.p, self.part, self.froms
         if name == "core":
-            src = f.at[i, :, :, :, 1 - p.core]
+            src, dst = f.at[i, :, :, :, 1 - p.core], landing[name].at[i]
         elif name == "x":
-            src = f.at[i, 2 * (1 - p.x), :, :, p.core]
+            src, dst = f.at[i, 2 * (1 - p.x), self.most, :, p.core], landing[name].at[i, self.most]
+        elif name == "late_x":
+            src, dst = f.at[i, 2 * (1 - p.x), 3, p.y, p.core], landing["x"].at[i, 3, 0]
         elif name == "y":
-            src = f.at[i, self.own, :, 1 - p.y, p.core]
+            src, dst = f.at[i, self.own, self.most, 1 - p.y, p.core], landing[name].at[i, :, self.most]
+        elif name == "early_y":
+            src, dst = f.at[i, :, 3, 1 - p.y, p.core], landing[name].at[i]
         else:
-            src = self.done.at[i]
+            src, dst = self.done.at[i], landing[name].at[i]
         send, recv = self.sems[name]
-        return remote(src, self.froms[name].at[i], send.at[i], recv.at[i], p.over("x" if name == "p" else name))
+        axis = {"p": "x", "early_y": "y", "late_x": "x"}.get(name, name)
+        return remote(src, dst, send.at[i], recv.at[i], p.over(axis))
 
     def z_copy(self, i, k, incoming=False):
         p = self.p
@@ -739,23 +755,33 @@
     def start(self, i):
         self.copy("core", i).start()
 
+    def add(self, at, term):
+        self.part[at] = self.part[at] + term
+
     def x_step(self, i):
-        p, f = self.p, self.part
+        p = self.p
         self.copy("core", i).wait_recv()
         for t in range(1 if self.whole else 3):
-            f[i, t, :, :, p.core] = f[i, t, :, :, p.core] + self.froms["core"][i, t]
-        self.copy("y" if self.whole else "x", i).start()
+            self.add((i, t, slice(None), slice(None), p.core), self.froms["core"][i, t])
+        for name in ("y",) if self.whole else ("x", "early_y"):
+            self.copy(name, i).start()
 
     def y_step(self, i):
-        p, f = self.p, self.part
+        p = self.p
+        self.copy("early_y", i).wait_recv()
+        self.add((i, slice(None), 3, p.y, p.core), self.froms["early_y"][i])
+        self.copy("late_x", i).start()
         self.copy("x", i).wait_recv()
-        f[i, 2 * p.x, :, :, p.core] = f[i, 2 * p.x, :, :, p.core] + self.froms["x"][i]
+        self.add((i, 2 * p.x, self.most, slice(None), p.core), self.froms["x"][i, :3])
         self.copy("y", i).start()
 
     def z_step(self, i):
-        p, f = self.p, self.part
+        p = self.p
         self.copy("y", i).wait_recv()
-        f[i, self.own, :, p.y, p.core] = f[i, self.own, :, p.y, p.core] + self.froms["y"][i]
+        self.add((i, self.own, self.most, p.y, p.core), self.froms["y"][i, :, self.most])
+        if not self.whole:
+            self.copy("late_x", i).wait_recv()
+            self.add((i, 2 * p.x, 3, p.y, p.core), self.froms["x"][i, 3, 0])
         for k in (2, 1, 3):
             self.z_copy(i, k).start()
 
@@ -791,7 +817,7 @@
 
 def back_kernel(heads, x_hbm, c_hbm, y1_hbm, dz_hbm, dh2_hbm, n1_hbm, r1_hbm, g_hbm, gp_hbm, qkv_hbm, w_hbm,
                 seg_ref, lse_ref, dv_ref, vec_ref, gin_o, sum_o, vsum_o,
-                part, fromc, fromy, fromp, fromz, fromx, done, vpart, vfromc, vfromy, vfromp, vfromz, vdone, pool, wpool, gpool, acc, cb, dab, dcb, r1b, delta, vrow,
+                part, fromc, fromy, fromp, fromz, fromx, frome, done, vpart, vfromc, vfromy, vfromp, vfromz, vdone, pool, wpool, gpool, acc, cb, dab, dcb, r1b, delta, vrow,
                 ld, out_sem, *sems):
     place = Place()
     rows, seq = seg_ref.shape
@@ -801,8 +827,8 @@
     own_rows = part.shape[-2]
     pieces = part.shape[0]
     big = 512
-    r_ = Reduce(place, part, (fromc, fromy, fromp, fromz, fromx), done, sum_o, sems[:10], pieces)
-    rv = Reduce(place, vpart, (vfromc, vfromy, vfromp, vfromz), vdone, vsum_o, sems[10:], 1, 1)
+    r_ = Reduce(place, part, (fromc, fromy, fromp, fromz, fromx, frome), done, sum_o, sems[:14], pieces)
+    rv = Reduce(place, vpart, (vfromc, vfromy, vfromp, vfromz), vdone, vsum_o, sems[14:], vpart.shape[0], 1)
     ff_pieces = 4 * chunks
     first_ff = pairs + 2
     du, dz, y1 = pool.at[2], pool.at[3], pool.at[4]
@@ -929,7 +955,7 @@
     x_in.wait()
     first_seq = lax.broadcasted_iota(jnp.int32, (seq, LANES), 1) < HD
 
-    def pair(p):
+    def pair(p, last=False):
         head = pl.ds(pl.multiple_of(p * LANES, LANES), LANES)
         col = pl.multiple_of(lax.rem(p, 2) * PIECE, LANES)
         to = p // 2
@@ -954,24 +980,37 @@
                 grads.append((dot_tn(ds, k2) * 0.125, dot(ds, q2) * 0.125, dv))
             for k, (a, b) in enumerate(zip(*grads)):
                 pool[to, tok, pl.ds(col + k * LANES, LANES)] = jnp.where(first_seq, a, b).astype(bf16)
-            when((r == 0) & (p < twice), lambda: r_.turn(t0 + 2 * p))
+            if last:
+                r_.turn(t0 + p + twice + r)
+            else:
+                when((r == 0) & (p < twice), lambda: r_.turn(t0 + 2 * p))
 
         loop(rows, row)
-        when(p + 2 < pairs, lambda: q_in(p + 2).start())
+        if not last:
+            when(p + 2 < pairs, lambda: q_in(p + 2).start())
         d = pool[to, :, pl.ds(col, PIECE)]
-        weight_grad(x, d, ff_pieces + 2 + p, 1)
         sums = colsum(d.astype(f32))
         vrow[4:5, head] = sums[:, :LANES]
         vrow[5:6, head] = sums[:, 2 * LANES :]
-        r_.turn(t0 + p + jnp.minimum(p + 1, twice))
-
-    loop(pairs, pair)
-    t0 += pairs + twice
-    vpart[0, 0] = vrow[...].T.astype(bf16).reshape(4, 2, 2, own_rows, LANES)
-    rv.start(0)
-    left = pieces - t0
-    loop(left, lambda i: r_.turn(t0 + i))
-    t0 += left
+        if last:
+            def product(a):
+                w = dot_tn(x[:, pl.ds(pl.multiple_of(a * half, LANES), half)], d)
+                for t in range(3):
+                    vpart[t, 0, pl.ds(2 * a, 2)] = w[:, t * LANES : (t + 1) * LANES].astype(bf16).reshape(2, 2, 2, own_rows, LANES)
+
+            loop(2, product)
+            for t in range(3):
+                rv.start(t)
+            vpart[3, 0] = vrow[...].T.astype(bf16).reshape(4, 2, 2, own_rows, LANES)
+            rv.start(3)
+        else:
+            weight_grad(x, d, ff_pieces + 2 + p, 1)
+            r_.turn(t0 + p + jnp.minimum(p + 1, twice))
+
+    loop(pairs - 1, pair)
+    pair(pairs - 1, True)
+    t0 += pairs - 1 + twice + rows
+    singles = vpart.shape[0]
     wq_in.wait()
     blocks = tokens // 256
 
@@ -979,18 +1018,25 @@
         at = pl.ds(pl.multiple_of(i * 256, 256), 256)
         d = jnp.concatenate([pool[k, at, :] for k in range(pairs // 2)], 1)
         dcb[at, :] = (acc[at, :] + dot_nt(d, columns(wpool, *range(2, 2 + pairs)))).astype(bf16)
-        r_.turn(t0 + i)
-        for k, step in ((0, rv.x_step), (2, rv.z_step)):
-            when(i == k, lambda step=step: step(0))
+        when(i == 0, lambda: loop(singles, rv.x_step))
+        when(i < 2, lambda: r_.turn(t0 + i))
+        when(i == 2, lambda: loop(singles, rv.z_step))
+        when(i == 3, lambda: r_.turn(t0 + 2))
 
     loop(blocks, gin_block)
     gin_out = pltpu.make_async_copy(dcb, gin_o, out_sem)
     gin_out.start()
-    rv.p_step(0)
-    loop(REDUCE_LAGS[-1] - blocks, lambda i: r_.turn(t0 + blocks + i))
-    rv.finish(0)
+    t0 += 3
+    rest = pieces + REDUCE_LAGS[-1] - t0
+
+    def rest_turn(i):
+        r_.turn(t0 + i)
+        when(i == 0, lambda: loop(singles, rv.p_step))
+
+    loop(rest, rest_turn)
+    loop(singles, rv.finish)
     loop(pieces, r_.sent)
-    rv.sent(0)
+    loop(singles, rv.sent)
     gin_out.wait()
 
 
@@ -1001,7 +1047,7 @@
     own_rows = w.shape[-2]
     heads = width // HD
     pairs = heads // 2
-    pieces = 4 * chunks + 2 + pairs
+    pieces = 4 * chunks + 2 + pairs - 1
     sh = jax.ShapeDtypeStruct
     dma = pltpu.SemaphoreType.DMA
     v = pltpu.VMEM
@@ -1011,15 +1057,15 @@
     tok = v((tokens, width), bf16)
     scratch = [
         v((pieces, 3, 4, 2, 2) + tail, bf16), v((pieces, 3, 4, 2) + tail, bf16), v((pieces, 2, 4) + tail, bf16), v((pieces, 2) + tail, bf16),
-        v((pieces, 4, 2) + tail, bf16), v((pieces, 4, 2) + tail, bf16), v((pieces, 2) + tail, bf16),
-        v((1, 1, 4, 2, 2) + tail, bf16), v((1, 1, 4, 2) + tail, bf16), v((1, 1, 4) + tail, bf16), v((1, 1) + tail, bf16),
-        v((1, 4, 1) + tail, bf16), v((1, 1) + tail, bf16), v((5, tokens, width), bf16), v((8,) + w.shape[1:], bf16), v((2, tokens, width), f32),
+        v((pieces, 4, 2) + tail, bf16), v((pieces, 4, 2) + tail, bf16), v((pieces, 3) + tail, bf16), v((pieces, 2) + tail, bf16),
+        v((4, 1, 4, 2, 2) + tail, bf16), v((4, 1, 4, 2) + tail, bf16), v((4, 1, 4) + tail, bf16), v((4, 1) + tail, bf16),
+        v((4, 4, 1) + tail, bf16), v((4, 1) + tail, bf16), v((5, tokens, width), bf16), v((8,) + w.shape[1:], bf16), v((2, tokens, width), f32),
         v((tokens, width), f32), tok, tok, tok, v((tokens, LANES), f32), v((16, tokens), f32),
         v((LANES, width), f32),
-        dma((3 * chunks + 9 + pairs,)), dma(())] + [dma((pieces, 4))] * 2 + [dma((pieces,))] * 8 + [dma((1, 4))] * 2 + [dma((1,))] * 6
+        dma((3 * chunks + 9 + pairs,)), dma(())] + [dma((pieces, 4))] * 2 + [dma((pieces,))] * 12 + [dma((4, 4))] * 2 + [dma((4,))] * 6
     return pl.pallas_call(
         functools.partial(back_kernel, heads),
-        out_shape=(sh((tokens, width), bf16), sh((pieces, own_rows, PIECE), f32), sh((1, own_rows, LANES), f32)),
+        out_shape=(sh((tokens, width), bf16), sh((pieces, own_rows, PIECE), f32), sh((4, own_rows, LANES), f32)),
         in_specs=[hbm] * 11 + [vmem] * 4,
         out_specs=(hbm, vmem, vmem),
         scratch_shapes=scratch,
@@ -1051,11 +1097,11 @@
 
     rows, own = vm.shape
     square[...] = jnp.zeros_like(square)
-    square[:own, :] = vsum_ref[0]
+    square[:own, :] = vsum_ref[3]
     vm_o[...], vw_o[...], va_o[...] = advance(square[...].T[:rows, :own], vector, vm[...], vw[...], va[...])
     every = slice(None)
     pairs = att.shape[3] // LANES
-    ff_pieces = sum_ref.shape[0] - 2 - pairs
+    ff_pieces = sum_ref.shape[0] - 1 - pairs
     for c in loads[:3]:
         c.wait()
     for i in range(ff_pieces):
@@ -1069,7 +1115,8 @@
         advance_in(sum_ref[ff_pieces + i], att, (3, every, slice(i * PIECE, (i + 1) * PIECE)))
     for p in range(pairs):
         for k in range(3):
-            advance_in(sum_ref[ff_pieces + 2 + p, :, k * LANES : (k + 1) * LANES], att, (k, every, slice(p * LANES, (p + 1) * LANES)))
+            grad = vsum_ref[k] if p == pairs - 1 else sum_ref[ff_pieces + 2 + p, :, k * LANES : (k + 1) * LANES]
+            advance_in(grad, att, (k, every, slice(p * LANES, (p + 1) * LANES)))
     for c in loads[6:]:
         c.wait()
     for c in stores[3:]:

time: 199 us -> 196 us (0.985)
  Pallas kernels: 198 us -> 195 us
where the time goes in v6:
time: 196 us
  Pallas kernels  195 us (99%)
    pallas_call x1, Pallas kernels, back(): pl.pallas_call(functools.partial(back_kernel, heads), out_shape=(sh((toke...  98.5 us
    pallas_call x1, Pallas kernels, stage(): pl.pallas_call(functools.partial(stage_kernel, heads), out_shape=(sh((pai...  88.1 us
    pallas_call x1, Pallas kernels, update(): pl.pallas_call(functools.partial(update_kernel, rates), out_shape=(sh(gin...  8.19 us

profile of v6, /device:TPU:0, one launch (start us, length us, event | category | flops | bytes accessed | tf_op | source)
XLA Modules:
  0.0 195.6 jit_solution(17652378895389800060)
XLA Ops:
  0.6 88.1 %stage.1 = (bf16[6,1024,384]{2,1,0:T(8,128)(2,1)}, bf16[1024,768]{1,0:T(8,128)(2,1)}, f32[2,16,512]{2,1,0:T(8,128)}, bf16[24,3,2,2,2,2,48,128]{7,6,5,4,3,2,1,0:T...) custom-call(bf16[1024,768]{1,0:T(8,128)(2,1)} %bitcast.4, ...), custom_call_target="tpu_custom_call" | custom-call | tf_op jit(solution)/shard_map/stage/pallas_call | solution.py:709
  88.8 98.5 %back.1 = (bf16[1024,768]{1,0:T(8,128)(2,1)}, f32[23,48,384]{2,1,0:T(8,128)}, f32[4,48,128]{2,1,0:T(8,128)}) custom-call(bf16[1024,768]{1,0:T(8,128)(2,1)} %bitcast.5, bf16[1024,768]{1,0:T(8,128)(2,1)} %get-tuple-element.39.c_hbm, bf16[1024,768]{1,0:T(8,128)(2,1)} %get-tuple-element.40.y1_hbm, bf16[1024,768]{1,0:T(8,128)(2,1)} %get-tuple-element.41.dz_hbm, ...), custom_call_target="tpu_custom_call" | custom-call | tf_op jit(solution)/shard_map/back/pallas_call | solution.py:1066
  187.3 8.2 %update.1 = (bf16[1024,768]{1,0:T(8,128)(2,1)}, bf16[1024,768]{1,0:T(8,128)(2,1)}, f32[4,48,768]{2,1,0:T(8,128)}, f32[4,48,768]{2,1,0:T(8,128)}, f32[4,48,768]{2...) custom-call(f32[23,48,384]{2,1,0:T(8,128)} %get-tuple-element.52.sum, ...), custom_call_target="tpu_custom_call" | custom-call | tf_op jit(solution)/shard_map/update/pallas_call | solution.py:1135
